TPU v7x, 32 devices: a whole 2x2x4 slice. The times are simulated.
32 devices in a mesh: dp: 8 (over z, x), tensor: 4 (over y, core).
Axes of the slice: x: 2, y: 2, z: 4, core: 2. Of those that a mesh axis runs over, the one named last changes fastest.
Arguments:
- tokens: bfloat16 [8192, 1024], P(('dp', 'tensor')), may hold values from -6 to 6
- segments: int32 [8, 1024], P('dp'), may hold values from 0 to 3, never falling along the last dimension, each value on 1 to 512 neighbouring positions
- cotangent: bfloat16 [8192, 1024], P(('dp', 'tensor')), may hold values from -6 to 6
- project_weight: bfloat16 [1024, 3, 1024], P('dp', None, 'tensor'), may hold values from -0.1875 to 0.1875
- output_weight: bfloat16 [1024, 1024], P('tensor', 'dp'), may hold values from -1.5 to 1.5
- up_weight: bfloat16 [1024, 4096], P('dp', 'tensor'), may hold values from -0.1875 to 0.1875
- down_weight: bfloat16 [4096, 1024], P('tensor', 'dp'), may hold values from -0.09375 to 0.09375
- norm_gains: float32 [2, 1024], replicated, may hold values from 0.5 to 1.5
- bias_rows: float32 [6, 1024], replicated, may hold values from -3 to 3
- hidden_bias: float32 [4096], replicated, may hold values from -3 to 3
Outputs:
- layer_out: bfloat16 [8192, 1024], P(('dp', 'tensor'))
- grad_tokens: float32 [8192, 1024], P(('dp', 'tensor'))
- grad_project: float32 [1024, 3, 1024], P('dp', None, 'tensor')
- grad_output: float32 [1024, 1024], P('tensor', 'dp')
- grad_up: float32 [1024, 4096], P('dp', 'tensor')
- grad_down: float32 [4096, 1024], P('tensor', 'dp')
- grad_gains: float32 [2, 1024], replicated
- grad_bias_rows: float32 [6, 1024], replicated
- grad_hidden_bias: float32 [4096], replicated
Inputs may be any that keep to these rules, and one draw needn't show every extreme that they name: `segments`: within each sequence the numbers never fall; a document is a run of equal numbers of at most 512 tokens, and every sequence has one document of exactly that length.
All inputs are finite; a program needn't handle non-finite values.
Results may differ from a plain program's by a relative error of at most 0.015.
The roundings to bfloat16 on the way count: a program that leaves them out, or rounds other values in their place, can miss the bound.
Values may be sent and summed in bfloat16 or wider, within the bound.
A program may use at most 128 MiB of HBM per device.

v0:
```python
import jax
import jax.numpy as jnp
from jax import lax
from jax.sharding import PartitionSpec as P

HEAD = 64


EPSILON = 1e-05
NEGATIVE = -1e30


def gelu_exact(values):
    return jax.nn.gelu(values, approximate=False)


def layer_norm(token_rows, gain, shift):
    average = jnp.mean(token_rows, axis=-1, keepdims=True)
    centred = token_rows - average
    variance = jnp.mean(centred * centred, axis=-1, keepdims=True)
    inverse = lax.rsqrt(variance + EPSILON)
    normed = centred * inverse
    return (normed * gain + shift, (normed, inverse))


def norm_back(grad_rows, saved, gain):
    normed, inverse = saved
    grad_gain = jnp.sum(grad_rows * normed, axis=0)
    grad_shift = jnp.sum(grad_rows, axis=0)
    grad_normed = grad_rows * gain
    grad_input = inverse * (
        grad_normed
        - jnp.mean(grad_normed, axis=-1, keepdims=True)
        - normed * jnp.mean(grad_normed * normed, axis=-1, keepdims=True)
    )
    return (grad_input, grad_gain, grad_shift)


def split_heads(token_rows):
    return token_rows.reshape(token_rows.shape[0], token_rows.shape[1] // HEAD, HEAD)


def place_columns(partial_sum, column_block, total_width):
    full_rows = jnp.zeros(partial_sum.shape[:-1] + (total_width,), jnp.float32)
    return lax.dynamic_update_slice_in_dim(
        full_rows, partial_sum, column_block * partial_sum.shape[-1], partial_sum.ndim - 1
    )


def per_device(
    tokens,
    segments,
    cotangent,
    project_weight,
    output_weight,
    up_weight,
    down_weight,
    norm_gains,
    bias_rows,
    hidden_bias,
):
    tensor_rank = lax.axis_index("tensor")
    local_rows, model_width = tokens.shape
    seq_count, seq_length = segments.shape
    group_rows = seq_count * seq_length
    local_width = project_weight.shape[2]
    score_scale = HEAD ** (-0.5)
    block_rows = min(512, seq_length)
    per_sequence = seq_length // block_rows
    count_blocks = group_rows // block_rows
    block_ids = jnp.arange(count_blocks, dtype=jnp.int32)
    triple_full, output_full, upward_full, downward_full = (
        lax.all_gather(project_weight, "dp", axis=0, tiled=True),
        lax.all_gather(output_weight, "dp", axis=1, tiled=True),
        lax.all_gather(up_weight, "dp", axis=0, tiled=True),
        lax.all_gather(down_weight, "dp", axis=1, tiled=True),
    )
    local_hidden = upward_full.shape[1]
    triple_matrix = triple_full.reshape(model_width, 3 * local_width)
    gathered = lax.all_gather(tokens, "tensor", axis=0, tiled=True)
    head_bias = lax.dynamic_slice_in_dim(bias_rows, tensor_rank * local_width, local_width, 1)
    projected = jnp.dot(gathered, triple_matrix, preferred_element_type=jnp.float32).reshape(
        group_rows, 3, local_width
    )
    queries = (projected[:, 0] + head_bias[0]).astype(jnp.bfloat16)
    key_rows = projected[:, 1].astype(jnp.bfloat16)
    value_rows = (projected[:, 2] + head_bias[1]).astype(jnp.bfloat16)

    def block_parts(block_index):
        sequence = block_index // per_sequence
        row_start = block_index * block_rows
        seq_start = sequence * seq_length
        query_block = split_heads(lax.dynamic_slice_in_dim(queries, row_start, block_rows, 0))
        key_block = split_heads(key_rows)
        value_block = split_heads(value_rows)
        seq_ids = lax.dynamic_index_in_dim(segments, sequence, 0, keepdims=False)
        query_ids = lax.dynamic_slice_in_dim(seq_ids, row_start - seq_start, block_rows, 0)
        products = (
            jnp.einsum("qhd,khd->hqk", query_block, key_block, preferred_element_type=jnp.float32)
            * score_scale
        )
        scores = jnp.where((query_ids[:, None] == seq_ids[None, :])[None], products, NEGATIVE)
        return (row_start, query_block, key_block, value_block, scores)

    def forward_block(block_index):
        row_start, query_block, key_block, value_block, scores = block_parts(block_index)
        row_max = jnp.max(scores, axis=-1, keepdims=True)
        exponent = jnp.exp(scores - row_max)
        row_sum = jnp.sum(exponent, axis=-1, keepdims=True)
        weights_low = (exponent / row_sum).astype(jnp.bfloat16)
        mixed_block = jnp.einsum(
            "hqk,khd->qhd", weights_low, value_block, preferred_element_type=jnp.float32
        )
        log_total = row_max[:, :, 0] + jnp.log(row_sum[:, :, 0])
        return (mixed_block.reshape(block_rows, local_width).astype(jnp.bfloat16), log_total)

    mixed_blocks, log_totals = lax.map(forward_block, block_ids)
    mixed_rows = mixed_blocks.reshape(group_rows, local_width)
    branch_out = (
        lax.psum_scatter(
            jnp.dot(mixed_rows, output_full, preferred_element_type=jnp.float32),
            "tensor",
            scatter_dimension=0,
            tiled=True,
        )
        + bias_rows[2]
    )
    first_out, first_saved = layer_norm(
        tokens.astype(jnp.float32) + branch_out, norm_gains[0], bias_rows[3]
    )
    first_gathered = lax.all_gather(first_out.astype(jnp.bfloat16), "tensor", axis=0, tiled=True)
    local_bias = lax.dynamic_slice_in_dim(hidden_bias, tensor_rank * local_hidden, local_hidden, 0)
    upper_rows = (
        jnp.dot(first_gathered, upward_full, preferred_element_type=jnp.float32) + local_bias
    )
    hidden_full, gelu_back = jax.vjp(gelu_exact, upper_rows)
    hidden_rows = hidden_full.astype(jnp.bfloat16)
    second_out = (
        lax.psum_scatter(
            jnp.dot(hidden_rows, downward_full, preferred_element_type=jnp.float32),
            "tensor",
            scatter_dimension=0,
            tiled=True,
        )
        + bias_rows[4]
    )
    layer_out, second_saved = layer_norm(first_out + second_out, norm_gains[1], bias_rows[5])
    reloaded = (
        lax.all_gather(project_weight, "dp", axis=0, tiled=True),
        lax.all_gather(output_weight, "dp", axis=1, tiled=True),
        lax.all_gather(up_weight, "dp", axis=0, tiled=True),
        lax.all_gather(down_weight, "dp", axis=1, tiled=True),
    )
    back_triple = reloaded[0].reshape(model_width, 3 * local_width)
    back_output, back_upward, back_downward = (reloaded[1], reloaded[2], reloaded[3])
    grad_layer = cotangent.astype(jnp.float32)
    grad_second_in, grad_gain_two, grad_shift_two = norm_back(
        grad_layer, second_saved, norm_gains[1]
    )
    grad_second = grad_second_in.astype(jnp.bfloat16)
    grad_second_all = lax.all_gather(grad_second, "tensor", axis=0, tiled=True)
    grad_down_part = jnp.einsum(
        "tf,td->fd", hidden_rows, grad_second_all, preferred_element_type=jnp.float32
    )
    grad_hidden = jnp.einsum(
        "td,fd->tf", grad_second_all, back_downward, preferred_element_type=jnp.float32
    )
    grad_upper = gelu_back(grad_hidden)[0].astype(jnp.bfloat16)
    grad_up_part = jnp.einsum(
        "td,tf->df", first_gathered, grad_upper, preferred_element_type=jnp.float32
    )
    grad_first = (
        lax.psum_scatter(
            jnp.einsum("tf,df->td", grad_upper, back_upward, preferred_element_type=jnp.float32),
            "tensor",
            scatter_dimension=0,
            tiled=True,
        )
        + grad_second_in
    )
    grad_first_in, grad_gain_one, grad_shift_one = norm_back(grad_first, first_saved, norm_gains[0])
    grad_branch = grad_first_in.astype(jnp.bfloat16)
    grad_branch_all = lax.all_gather(grad_branch, "tensor", axis=0, tiled=True)
    grad_output_part = jnp.einsum(
        "tc,td->cd", mixed_rows, grad_branch_all, preferred_element_type=jnp.float32
    )
    grad_mixed = jnp.einsum(
        "td,cd->tc", grad_branch_all, back_output, preferred_element_type=jnp.float32
    ).astype(jnp.bfloat16)

    def backward_block(block_index):
        row_start, query_block, key_block, value_block, scores = block_parts(block_index)
        weights_full = jnp.exp(scores - log_totals[block_index][:, :, None])
        grad_mixed_block = split_heads(
            lax.dynamic_slice_in_dim(grad_mixed, row_start, block_rows, 0)
        )
        grad_weights = jnp.einsum(
            "qhd,khd->hqk", grad_mixed_block, value_block, preferred_element_type=jnp.float32
        )
        row_dot = jnp.sum(weights_full * grad_weights, axis=-1, keepdims=True)
        grad_scores = (weights_full * (grad_weights - row_dot)).astype(jnp.bfloat16)
        grad_query = (
            jnp.einsum("hqk,khd->qhd", grad_scores, key_block, preferred_element_type=jnp.float32)
            * score_scale
        )
        grad_key = (
            jnp.einsum("hqk,qhd->khd", grad_scores, query_block, preferred_element_type=jnp.float32)
            * score_scale
        )
        grad_value = jnp.einsum(
            "hqk,qhd->khd",
            weights_full.astype(jnp.bfloat16),
            grad_mixed_block,
            preferred_element_type=jnp.float32,
        )
        return (
            grad_query.reshape(block_rows, local_width),
            grad_key.reshape(seq_length, local_width),
            grad_value.reshape(seq_length, local_width),
        )

    query_blocks, key_blocks, value_blocks = lax.map(backward_block, block_ids)
    grad_queries = query_blocks.reshape(group_rows, local_width)
    grad_keys = (
        key_blocks.reshape(seq_count, per_sequence, seq_length, local_width)
        .sum(axis=1)
        .reshape(group_rows, local_width)
    )
    grad_values = (
        value_blocks.reshape(seq_count, per_sequence, seq_length, local_width)
        .sum(axis=1)
        .reshape(group_rows, local_width)
    )
    grad_projected = jnp.stack((grad_queries, grad_keys, grad_values), axis=1).astype(jnp.bfloat16)
    grad_project_part = jnp.einsum(
        "te,tsc->esc", gathered, grad_projected, preferred_element_type=jnp.float32
    )
    grad_matrix = grad_projected.reshape(group_rows, 3 * local_width)
    grad_tokens = (
        lax.psum_scatter(
            jnp.einsum(
                "tc,ec->te", grad_matrix, back_triple, preferred_element_type=jnp.float32
            ).astype(jnp.bfloat16),
            "tensor",
            scatter_dimension=0,
            tiled=True,
        ).astype(jnp.float32)
        + grad_first_in
    )
    grad_project, grad_output, grad_up, grad_down = (
        lax.psum_scatter(grad_project_part, "dp", scatter_dimension=0, tiled=True),
        lax.psum_scatter(grad_output_part, "dp", scatter_dimension=1, tiled=True),
        lax.psum_scatter(grad_up_part, "dp", scatter_dimension=0, tiled=True),
        lax.psum_scatter(grad_down_part, "dp", scatter_dimension=1, tiled=True),
    )
    head_terms = place_columns(
        jnp.stack(
            (
                jnp.sum(grad_projected[:, 0], axis=0, dtype=jnp.float32),
                jnp.sum(grad_projected[:, 2], axis=0, dtype=jnp.float32),
            )
        ),
        tensor_rank,
        model_width,
    )
    shared_terms = jnp.stack(
        (
            jnp.sum(grad_branch, axis=0, dtype=jnp.float32),
            grad_shift_one,
            jnp.sum(grad_second, axis=0, dtype=jnp.float32),
            grad_shift_two,
        )
    )
    bias_terms = jnp.concatenate((head_terms, shared_terms), axis=0)
    gain_terms = jnp.stack((grad_gain_one, grad_gain_two))
    hidden_terms = place_columns(
        jnp.sum(grad_upper, axis=0, dtype=jnp.float32), tensor_rank, hidden_bias.shape[0]
    )
    grad_gains, grad_bias_rows, grad_hidden_bias = lax.psum(
        (gain_terms, bias_terms, hidden_terms), ("dp", "tensor")
    )
    return (
        layer_out.astype(jnp.bfloat16),
        grad_tokens,
        grad_project,
        grad_output,
        grad_up,
        grad_down,
        grad_gains,
        grad_bias_rows,
        grad_hidden_bias,
    )


def solution(mesh):
    placed = (
        P(("dp", "tensor"), None),
        P("dp", None),
        P(("dp", "tensor"), None),
        P("dp", None, "tensor"),
        P("tensor", "dp"),
        P("dp", "tensor"),
        P("tensor", "dp"),
        P(),
        P(),
        P(),
    )
    return jax.shard_map(
        per_device,
        mesh=mesh,
        in_specs=placed,
        out_specs=(
            P(("dp", "tensor"), None),
            P(("dp", "tensor"), None),
            P("dp", None, "tensor"),
            P("tensor", "dp"),
            P("dp", "tensor"),
            P("tensor", "dp"),
            P(),
            P(),
            P(),
        ),
        check_vma=False,
    )
```

profile of v0, /device:TPU:0, one launch (start us, length us, event | category | flops | bytes accessed | tf_op | source)
XLA Modules:
  0.0 879.3 jit_solution(6311445229574775207)
XLA Ops:
  9.6 31.1 %all_gather.30 = bf16[256,1024]{1,0:T(8,128)(2,1)S(1)} all-gather(bf16[256,128]{1,0:T(8,128)(2,1)} %param.18), channel_id=1, replica_groups=mesh['dp'=8,'tensor'=4] {'dp'}, dimensions={1}, use_global_device_ids=true | all-gather | bytes 589824 | tf_op jit(solution)/shard_map/all_gather | solution.py:74
  40.7 18.4 %all-gather.10.cloned.1.call-done = bf16[1024,3,256]{2,0,1:T(8,128)(2,1)} async-done(((bf16[128,3,256]{2,0,1:T(8,128)(2,1)}), bf16[1024,3,256]{2,0,1:T(8,128)(2,1)}) %all-gather.10.cloned.1.call-update) | async-done | bytes 1572880 | tf_op jit(solution)/shard_map/all_gather | solution.py:73
  59.1 2.6 copy.41
  61.7 20.4 %all-gather.8.cloned.1.call-done = bf16[1024,1024]{1,0:T(8,128)(2,1)} async-done(((bf16[256,1024]{1,0:T(8,128)(2,1)}), bf16[1024,1024]{1,0:T(8,128)(2,1)}) %all-gather.8.cloned.1.call-update) | async-done | bytes 2097168 | tf_op jit(solution)/shard_map/all_gather | solution.py:80
  82.1 3.9 fusion.20
  86.0 1.7 copy-done.4
  87.9 1.7 fusion.34
  90.1 22.8 %while.30 = (s32[]{:T(128)}, bf16[2,512,256]{2,1,0:T(8,128)(2,1)S(1)}, f32[2,4,512]{2,1,0:T(4,128)S(1)}, s32[2]{0:T(128)S(1)}, s32[1,1024]{1,0:T(1,128)S(1)}, /*...) while((s32[]{:T(128)}, ...), condition=%wide.region_3.4_spmd, body=%wide.region_0.3_spmd.sunk | while | flops 562690048 | bytes 30484896 | solution.py:117
  94.3 1.7 fusion.110
  96.0 2.3 fusion.111
  98.4 2.9 fusion.112
  105.8 1.7 fusion.110
  107.5 2.3 fusion.111
  109.8 2.9 fusion.112
  113.0 2.7 fusion.52
  116.4 43.9 %reduce-scatter.9.cloned.1.call-done = f32[256,1024]{1,0:T(8,128)} async-done(((f32[1024,1024]{1,0:T(8,128)}), f32[256,1024]{1,0:T(8,128)}) %reduce-scatter.9.cloned.1.call-update) | async-done | bytes 1048592 | tf_op jit(solution)/shard_map/reduce_scatter | solution.py:120
  160.4 1.4 fusion.47
  162.1 1.1 fusion.37
  164.6 47.2 %all-gather.14.cloned.1.call-done = bf16[1024,1024]{1,0:T(8,128)(2,1)} async-done(((bf16[128,1024]{1,0:T(8,128)(2,1)}), bf16[1024,1024]{1,0:T(8,128)(2,1)}) %all-gather.14.cloned.1.call-update) | async-done | bytes 2097168 | tf_op jit(solution)/shard_map/all_gather | solution.py:75
  211.9 23.2 %all-gather.12.cloned.1.call-done = bf16[1024,1024]{1,0:T(8,128)(2,1)} async-done(((bf16[256,1024]{1,0:T(8,128)(2,1)}), bf16[1024,1024]{1,0:T(8,128)(2,1)}) %all-gather.12.cloned.1.call-update) | async-done | bytes 2097168 | tf_op jit(solution)/shard_map/all_gather | solution.py:131
  235.0 14.9 %multiply_convert_fusion.1 = (bf16[1024,1024]{1,0:T(8,128)(2,1)}, f32[1024,1024]{1,0:T(8,128)}, f32[1024,1024]{1,0:T(8,128)}) fusion(f32[1024]{0:T(1024)S(1)} %dynamic_slice.57, bf16[1024,1024]{1,0:T(8,128)(2,1)} %all-gather.12.cloned.1.call-done, bf16[1024,1024]{1,0:T(8,128)(2,1)} %all-gather.14.cloned.1.call-done), kind=kOutput, calls=%fused_computation.37 | convolution fusion | flops 2216689664 | bytes 14684160 | tf_op jit(solution)/shard_map/dot_general | solution.py:134
  250.0 38.3 %all-gather.16.cloned.1.call-done = bf16[1024,1024]{1,0:T(8,128)(2,1)} async-done(((bf16[1024,128]{1,0:T(8,128)(2,1)}), bf16[1024,1024]{1,0:T(8,128)(2,1)}) %all-gather.16.cloned.1.call-update) | async-done | bytes 2097168 | tf_op jit(solution)/shard_map/all_gather | solution.py:76
  288.2 6.6 fusion.53
  294.9 42.8 %reduce-scatter.11.cloned.1.call-done = f32[256,1024]{1,0:T(8,128)} async-done(((f32[1024,1024]{1,0:T(8,128)}), f32[256,1024]{1,0:T(8,128)}) %reduce-scatter.11.cloned.1.call-update) | async-done | bytes 1048592 | tf_op jit(solution)/shard_map/reduce_scatter | solution.py:139
  337.7 1.6 fusion.45
  339.6 2.2 fusion.32
  341.8 2.8 convert_reduce_fusion.2
  344.9 22.5 %all-gather.18.cloned.1.call-done = bf16[1024,1024]{1,0:T(8,128)(2,1)} async-done(((bf16[256,1024]{1,0:T(8,128)(2,1)}), bf16[1024,1024]{1,0:T(8,128)(2,1)}) %all-gather.18.cloned.1.call-update) | async-done | bytes 2097168 | tf_op jit(solution)/shard_map/all_gather | solution.py:161
  367.4 8.5 convert_reduce_fusion
  375.9 1.3 copy-done.21
  377.2 4.3 fusion.54
  381.6 44.6 %reduce-scatter.13.cloned.1.call-done = f32[256,1024]{1,0:T(8,128)} async-done(((f32[1024,1024]{1,0:T(8,128)}), f32[256,1024]{1,0:T(8,128)}) %reduce-scatter.13.cloned.1.call-update) | async-done | bytes 1048592 | tf_op jit(solution)/shard_map/reduce_scatter | solution.py:173
  426.2 3.1 multiply_reduce_fusion.1
  429.4 1.2 convert_reduce_fusion.3
  430.9 22.4 %all-gather.20.cloned.1.call-done = bf16[1024,1024]{1,0:T(8,128)(2,1)} async-done(((bf16[256,1024]{1,0:T(8,128)(2,1)}), bf16[1024,1024]{1,0:T(8,128)(2,1)}) %all-gather.20.cloned.1.call-update) | async-done | bytes 2097168 | tf_op jit(solution)/shard_map/all_gather | solution.py:183
  453.3 3.2 convolution_convert_fusion
  456.5 44.2 %while.31 = (s32[]{:T(128)}, bf16[2,512,256]{1,2,0:T(8,128)(2,1)}, f32[2,1024,256]{1,2,0:T(8,128)}, f32[2,1024,256]{1,2,0:T(8,128)}, s32[2]{0:T(128)S(1)}, /*ind...) while((s32[]{:T(128)}, bf16[2,512,256]{1,2,0:T(8,128)(2,1)}, ...), condition=%wide.region_17.18_spmd, body=%wide.region_15.17_spmd.sunk | while | flops 1374681088 | bytes 114100872 | solution.py:222
  461.7 1.0 constant_dynamic-slice_fusion.15
  463.2 1.3 fusion.123
  464.5 2.4 fusion.124
  466.9 3.2 multiply_reduce_fusion.7
  470.1 2.4 multiply_convert_fusion.3
  472.5 1.4 convolution_multiply_fusion.4
  483.6 1.0 constant_dynamic-slice_fusion.15
  485.2 1.3 fusion.123
  486.5 2.4 fusion.124
  488.9 3.2 multiply_reduce_fusion.7
  492.1 2.4 multiply_convert_fusion.3
  494.4 1.4 convolution_multiply_fusion.4
  500.7 1.9 reduce_sum.204
  502.6 1.8 reduce_sum.203
  505.0 4.6 bitcast_convert_fusion
  509.7 5.1 fusion.22
  514.9 6.7 fusion.57
  521.6 6.6 fusion.56
  528.4 1.0 copy-done.3
  529.3 3.3 fusion.55
  533.4 42.3 %all-reduce = (f32[2,1024]{1,0:T(2,128)}, f32[6,1024]{1,0:T(8,128)}, f32[4096]{0:T(1024)}) all-reduce(f32[2,1024]{1,0:T(2,128)S(1)} %pad_maximum_fusion.3, f32[6,1024]{1,0:T(8,128)S(1)} %concatenate.3, f32[4096]{0:T(1024)S(1)} %dynamic_update_slice.41), channel_id=1, replica_groups=mesh['dp'=8,'tensor'=4] {'dp','tensor'}, use_global_device_ids=true, to_apply=%region_27.28 | all-reduce | flops 12288 | bytes 98304 | tf_op jit(solution)/shard_map/psum | solution.py:279
  575.7 2.2 convert_add_fusion
  577.8 43.0 %reduce-scatter.17.cloned.1.call-done = f32[128,3,256]{0,2,1:T(8,128)} async-done(((f32[1024,3,256]{0,2,1:T(8,128)}), f32[128,3,256]{0,2,1:T(8,128)}) %reduce-scatter.17.cloned.1.call-update) | async-done | bytes 393232 | tf_op jit(solution)/shard_map/reduce_scatter | solution.py:251
  620.9 1.9 copy.54
  622.8 89.7 %reduce-scatter.23.cloned.1.call-done = f32[1024,128]{1,0:T(8,128)} async-done(((f32[1024,1024]{1,0:T(8,128)}), f32[1024,128]{1,0:T(8,128)}) %reduce-scatter.23.cloned.1.call-update) | async-done | bytes 524304 | tf_op jit(solution)/shard_map/reduce_scatter | solution.py:254
  712.5 92.2 %reduce-scatter.21.cloned.1.call-done = f32[128,1024]{1,0:T(8,128)} async-done(((f32[1024,1024]{1,0:T(8,128)}), f32[128,1024]{1,0:T(8,128)}) %reduce-scatter.21.cloned.1.call-update) | async-done | bytes 524304 | tf_op jit(solution)/shard_map/reduce_scatter | solution.py:253
  804.7 67.5 %reduce-scatter.19.cloned.1.call-done = f32[256,128]{1,0:T(8,128)} async-done(((f32[256,1024]{1,0:T(8,128)}), f32[256,128]{1,0:T(8,128)}) %reduce-scatter.19.cloned.1.call-update) | async-done | bytes 131088 | tf_op jit(solution)/shard_map/reduce_scatter | solution.py:252
  (151 shorter events, 21.7 us)
Async XLA Ops:
  7.2 51.9 %all-gather.10.cloned.1.call-start = ((), (), s32[]{:S(2)}) async-start(), calls=%async_computation.9 | async-start | bytes 1769472 | tf_op jit(solution)/shard_map/all_gather | solution.py:73
  7.9 74.2 %all-gather.8.cloned.1.call-start = ((), (), s32[]{:S(2)}) async-start(), calls=%async_computation.8 | async-start | bytes 2621440 | tf_op jit(solution)/shard_map/all_gather | solution.py:80
  8.7 151.7 %reduce-scatter.9.cloned.1.call-start = ((), (), s32[]{:S(2)}) async-start(), calls=%async_computation.10 | async-start | bytes 5242880 | tf_op jit(solution)/shard_map/reduce_scatter | solution.py:120
  40.7 72.2 %copy-start.6 = (bf16[256,1024]{1,0:T(8,128)(2,1)}, bf16[256,1024]{1,0:T(8,128)(2,1)S(1)}, u32[]{:S(2)}) copy-start(bf16[256,1024]{1,0:T(8,128)(2,1)S(1)} %all_gather.30) | copy-start | bytes 1572868
  86.0 1.7 copy-start.4
  87.6 2.4 copy-start.11
  112.9 2.7 copy-start
  112.9 2.7 copy-start.2
  115.6 0.7 copy-start.19
  115.6 0.8 copy-start.18
  115.7 44.7 %copy-start.5 = (bf16[256,1024]{1,0:T(8,128)(2,1)S(1)}, bf16[256,1024]{1,0:T(8,128)(2,1)}, u32[]{:S(2)}) copy-start(bf16[256,1024]{1,0:T(8,128)(2,1)} %param.14) | copy-start | bytes 1572868
  115.7 96.2 %all-gather.14.cloned.1.call-start = ((), (), s32[]{:S(2)}) async-start(), calls=%async_computation.12 | async-start | bytes 2359296 | tf_op jit(solution)/shard_map/all_gather | solution.py:75
  116.3 118.8 %all-gather.12.cloned.1.call-start = ((), (), s32[]{:S(2)}) async-start(), calls=%async_computation.11 | async-start | bytes 2621440 | tf_op jit(solution)/shard_map/all_gather | solution.py:131
  163.1 125.1 %all-gather.16.cloned.1.call-start = ((), (), s32[]{:S(2)}) async-start(), calls=%async_computation.13 | async-start | bytes 2359296 | tf_op jit(solution)/shard_map/all_gather | solution.py:76
  163.7 174.0 %reduce-scatter.11.cloned.1.call-start = ((), (), s32[]{:S(2)}) async-start(), calls=%async_computation.14 | async-start | bytes 5242880 | tf_op jit(solution)/shard_map/reduce_scatter | solution.py:139
  294.9 72.5 %all-gather.18.cloned.1.call-start = ((), (), s32[]{:S(2)}) async-start(), calls=%async_computation.15 | async-start | bytes 2621440 | tf_op jit(solution)/shard_map/all_gather | solution.py:161
  344.6 81.6 %reduce-scatter.13.cloned.1.call-start = ((), (), s32[]{:S(2)}) async-start(), calls=%async_computation.16 | async-start | bytes 5242880 | tf_op jit(solution)/shard_map/reduce_scatter | solution.py:173
  367.4 9.8 %copy-start.20 = (bf16[1024,1024]{1,0:T(8,128)(2,1)S(1)}, bf16[1024,1024]{1,0:T(8,128)(2,1)}, u32[]{:S(2)}) copy-start(bf16[1024,1024]{1,0:T(8,128)(2,1)} %all-gather.14.cloned.1.call-done) | copy-start | bytes 6291460
  375.9 1.3 copy-start.21
  381.5 71.8 %all-gather.20.cloned.1.call-start = ((), (), s32[]{:S(2)}) async-start(), calls=%async_computation.17 | async-start | bytes 2621440 | tf_op jit(solution)/shard_map/all_gather | solution.py:183
  430.5 26.0 %copy-start.1 = (bf16[1024,256]{0,1:T(8,128)(2,1)S(1)}, bf16[1024,256]{0,1:T(8,128)(2,1)}, u32[]{:S(2)}) copy-start(bf16[1024,256]{0,1:T(8,128)(2,1)} %copy-done) | copy-start | bytes 1572868
  430.6 145.1 %reduce-scatter.15.cloned.1.call-start = ((), (), s32[]{:S(2)}) async-start(), calls=%async_computation.18 | async-start | bytes 2621440 | tf_op jit(solution)/shard_map/reduce_scatter | solution.py:240
  473.9 1.0 copy-start.12
  473.9 1.8 copy-start.7
  473.9 2.4 copy-start.9
  476.3 0.8 copy-start.13
  476.5 1.3 copy-start.8
  476.5 2.0 copy-start.10
  495.8 1.0 copy-start.12
  495.8 1.8 copy-start.7
  495.8 2.4 copy-start.9
  498.2 0.8 copy-start.13
  498.4 1.3 copy-start.8
  498.4 2.0 copy-start.10
  500.7 4.1 copy-start.14
  509.6 111.3 %reduce-scatter.17.cloned.1.call-start = ((), (), s32[]{:S(2)}) async-start(), calls=%async_computation.19 | async-start | bytes 3538944 | tf_op jit(solution)/shard_map/reduce_scatter | solution.py:251
  514.8 197.7 %reduce-scatter.23.cloned.1.call-start = ((), (), s32[]{:S(2)}) async-start(), calls=%async_computation.22 | async-start | bytes 4718592 | tf_op jit(solution)/shard_map/reduce_scatter | solution.py:254
  521.6 283.2 %reduce-scatter.21.cloned.1.call-start = ((), (), s32[]{:S(2)}) async-start(), calls=%async_computation.21 | async-start | bytes 4718592 | tf_op jit(solution)/shard_map/reduce_scatter | solution.py:253
  528.3 1.0 copy-start.3
  528.3 4.7 copy-start.17
  528.3 5.1 copy-start.15
  528.3 5.1 copy-start.16
  528.3 344.0 %reduce-scatter.19.cloned.1.call-start = ((), (), s32[]{:S(2)}) async-start(), calls=%async_computation.20 | async-start | bytes 1179648 | tf_op jit(solution)/shard_map/reduce_scatter | solution.py:252
Sparse Core Ops, SparseCore 0:
  10.2 48.8 all-gather.9
  60.7 21.3 all-gather.7
  115.8 44.4 reduce-scatter.8
  162.6 49.2 all-gather.13
  213.9 21.0 all-gather.11
  237.1 51.0 all-gather.15
  295.0 42.6 reduce-scatter.10
  344.8 22.5 all-gather.17
  381.7 44.4 reduce-scatter.12
  430.7 22.5 all-gather.19
  509.7 31.4 reduce-scatter.14
  544.7 76.1 reduce-scatter.16
  625.1 87.3 reduce-scatter.22
  717.0 87.6 reduce-scatter.20
  808.6 63.6 reduce-scatter.18
where the time goes:
time: 887 us; the launch traced here: 879 us
  waiting for transfers between devices  619 us (70%)
  matrix products  97.8 us (11%)
  blocking collectives  73.4 us (8%)
  other arithmetic  32.7 us (4%)
  local copies, waits for them, and re-layouts  24.2 us (3%)
  loops' own time  16.3 us (2%)
  between operations  14.8 us (2%)
    reduce_scatter x1, waiting for transfers between devices, per_device(): lax.psum_scatter(grad_up_part, 'dp', scatter_dimension=0, tiled=True)  92.2 us
    reduce_scatter x1, waiting for transfers between devices, per_device(): lax.psum_scatter(grad_down_part, 'dp', scatter_dimension=1, tiled=True)  89.7 us
    reduce_scatter x1, waiting for transfers between devices, per_device(): lax.psum_scatter(grad_output_part, 'dp', scatter_dimension=1, tiled=True)  67.5 us
    all_gather x1, waiting for transfers between devices, per_device(): lax.all_gather(up_weight, 'dp', axis=0, tiled=True)  47.2 us
    reduce_scatter x1, waiting for transfers between devices, per_device(): lax.psum_scatter(jnp.einsum('tf,df->td', grad_upper, back_upward, preferr...  44.6 us
    reduce_scatter x1, waiting for transfers between devices, per_device(): lax.psum_scatter(jnp.dot(mixed_rows, output_full, preferred_element_type=...  43.9 us
    reduce_scatter x1, waiting for transfers between devices, per_device(): lax.psum_scatter(grad_project_part, 'dp', scatter_dimension=0, tiled=True)  43 us
    reduce_scatter x1, waiting for transfers between devices, per_device(): lax.psum_scatter(jnp.dot(hidden_rows, downward_full, preferred_element_ty...  42.8 us
  transfers between devices with their start and end apart: 15, of which 14 were waited for; matrix products, arithmetic and copies ran while one was open for 6% of the time, Pallas kernels for 0%

commit v1 on v0

--- a/solution.py
+++ b/solution.py
@@ -38,6 +38,12 @@
 
 def split_heads(token_rows):
     return token_rows.reshape(token_rows.shape[0], token_rows.shape[1] // HEAD, HEAD)
+
+
+def scatter_sum(partial_sum, axis_name, dimension):
+    return lax.psum_scatter(
+        partial_sum.astype(jnp.bfloat16), axis_name, scatter_dimension=dimension, tiled=True
+    ).astype(jnp.float32)
 
 
 def place_columns(partial_sum, column_block, total_width):
@@ -117,11 +123,8 @@
     mixed_blocks, log_totals = lax.map(forward_block, block_ids)
     mixed_rows = mixed_blocks.reshape(group_rows, local_width)
     branch_out = (
-        lax.psum_scatter(
-            jnp.dot(mixed_rows, output_full, preferred_element_type=jnp.float32),
-            "tensor",
-            scatter_dimension=0,
-            tiled=True,
+        scatter_sum(
+            jnp.dot(mixed_rows, output_full, preferred_element_type=jnp.float32), "tensor", 0
         )
         + bias_rows[2]
     )
@@ -136,11 +139,8 @@
     hidden_full, gelu_back = jax.vjp(gelu_exact, upper_rows)
     hidden_rows = hidden_full.astype(jnp.bfloat16)
     second_out = (
-        lax.psum_scatter(
-            jnp.dot(hidden_rows, downward_full, preferred_element_type=jnp.float32),
-            "tensor",
-            scatter_dimension=0,
-            tiled=True,
+        scatter_sum(
+            jnp.dot(hidden_rows, downward_full, preferred_element_type=jnp.float32), "tensor", 0
         )
         + bias_rows[4]
     )
@@ -170,11 +170,10 @@
         "td,tf->df", first_gathered, grad_upper, preferred_element_type=jnp.float32
     )
     grad_first = (
-        lax.psum_scatter(
+        scatter_sum(
             jnp.einsum("tf,df->td", grad_upper, back_upward, preferred_element_type=jnp.float32),
             "tensor",
-            scatter_dimension=0,
-            tiled=True,
+            0,
         )
         + grad_second_in
     )
@@ -248,10 +247,10 @@
         + grad_first_in
     )
     grad_project, grad_output, grad_up, grad_down = (
-        lax.psum_scatter(grad_project_part, "dp", scatter_dimension=0, tiled=True),
-        lax.psum_scatter(grad_output_part, "dp", scatter_dimension=1, tiled=True),
-        lax.psum_scatter(grad_up_part, "dp", scatter_dimension=0, tiled=True),
-        lax.psum_scatter(grad_down_part, "dp", scatter_dimension=1, tiled=True),
+        scatter_sum(grad_project_part, "dp", 0),
+        scatter_sum(grad_output_part, "dp", 1),
+        scatter_sum(grad_up_part, "dp", 0),
+        scatter_sum(grad_down_part, "dp", 1),
     )
     head_terms = place_columns(
         jnp.stack(

time: 887 us -> 735 us (0.83)
  waiting for transfers between devices: 619 us -> 463 us
    reduce_scatter x7 -> x4, waiting for transfers between devices: 424 us -> 161 us  [scatter_sum(): lax.psum_scatter(partial_sum.astype(jnp.bfloat16), axis_name, scatter_dim...]
    unnamed x15 -> x18, waiting for transfers between devices: 2.6 us -> 96.8 us
    reduce_scatter x1, waiting for transfers between devices: 0.01 us -> 30.9 us  [per_device(): lax.psum_scatter(jnp.einsum('tc,ec->te', grad_matrix, back_triple, prefer...]
    all_gather x1, waiting for transfers between devices: 22.4 us -> 6.43 us  [per_device(): grad_branch_all = lax.all_gather(grad_branch, 'tensor', axis=0, tiled=True)]
  transfers between devices with their start and end apart: 15 -> 15, of which waited for: 14 -> 15; matrix products, arithmetic and copies ran while one was open for 6% -> 13% of each run, Pallas kernels for 0% -> 0%
where the time goes in v1:
time: 735 us; the launch traced here: 727 us
  waiting for transfers between devices  463 us (63%)
  matrix products  91.6 us (12%)
  blocking collectives  72.2 us (10%)
  other arithmetic  37.3 us (5%)
  local copies, waits for them, and re-layouts  30.4 us (4%)
  loops' own time  16.2 us (2%)
  between operations  14.6 us (2%)
    reduce_scatter x4, waiting for transfers between devices, scatter_sum(): lax.psum_scatter(partial_sum.astype(jnp.bfloat16), axis_name, scatter_dim...  161 us
    unnamed x18, waiting for transfers between devices  96.8 us
    all_gather x1, waiting for transfers between devices, per_device(): lax.all_gather(up_weight, 'dp', axis=0, tiled=True)  45.1 us
    psum x1, blocking collectives, per_device(): lax.psum((gain_terms, bias_terms, hidden_terms), ('dp', 'tensor'))  41 us
    all_gather x1, waiting for transfers between devices, per_device(): lax.all_gather(down_weight, 'dp', axis=1, tiled=True)  38.3 us
    all_gather x1, blocking collectives, per_device(): lax.all_gather(output_weight, 'dp', axis=1, tiled=True)  31.2 us
    reduce_scatter x1, waiting for transfers between devices, per_device(): lax.psum_scatter(jnp.einsum('tc,ec->te', grad_matrix, back_triple, prefer...  30.9 us
    all_gather x1, waiting for transfers between devices, per_device(): lax.all_gather(first_out.astype(jnp.bfloat16), 'tensor', axis=0, tiled=True)  23.2 us
  transfers between devices with their start and end apart: 15, of which 15 were waited for; matrix products, arithmetic and copies ran while one was open for 13% of the time, Pallas kernels for 0%

profile of v1, /device:TPU:0, one launch (start us, length us, event | category | flops | bytes accessed | tf_op | source)
XLA Modules:
  0.0 727.1 jit_solution(16687060974636816753)
XLA Ops:
  9.6 31.2 %all_gather.30 = bf16[256,1024]{1,0:T(8,128)(2,1)S(1)} all-gather(bf16[256,128]{1,0:T(8,128)(2,1)} %param.18), channel_id=1, replica_groups=mesh['dp'=8,'tensor'=4] {'dp'}, dimensions={1}, use_global_device_ids=true | all-gather | bytes 589824 | tf_op jit(solution)/shard_map/all_gather | solution.py:80
  40.7 18.4 %all-gather.10.cloned.1.call-done = bf16[1024,3,256]{2,0,1:T(8,128)(2,1)} async-done(((bf16[128,3,256]{2,0,1:T(8,128)(2,1)}), bf16[1024,3,256]{2,0,1:T(8,128)(2,1)}) %all-gather.10.cloned.1.call-update) | async-done | bytes 1572880 | tf_op jit(solution)/shard_map/all_gather | solution.py:79
  59.1 1.7 copy.41
  60.8 21.3 %all-gather.8.cloned.1.call-done = bf16[1024,1024]{1,0:T(8,128)(2,1)} async-done(((bf16[256,1024]{1,0:T(8,128)(2,1)}), bf16[1024,1024]{1,0:T(8,128)(2,1)}) %all-gather.8.cloned.1.call-update) | async-done | bytes 2097168 | tf_op jit(solution)/shard_map/all_gather | solution.py:86
  82.1 3.4 fusion.20
  85.5 1.7 copy-done.3
  87.4 1.7 fusion.34
  89.6 22.9 %while.30 = (s32[]{:T(128)}, bf16[2,512,256]{2,1,0:T(8,128)(2,1)S(1)}, f32[2,4,512]{2,1,0:T(4,128)S(1)}, s32[2]{0:T(128)S(1)}, s32[1,1024]{1,0:T(1,128)S(1)}, /*...) while((s32[]{:T(128)}, ...), condition=%wide.region_3.4_spmd, body=%wide.region_0.3_spmd.sunk | while | flops 562690048 | bytes 30484896 | solution.py:123
  93.9 1.7 fusion.102
  95.6 2.3 fusion.103
  97.9 2.9 fusion.104
  105.3 1.7 fusion.102
  107.0 2.3 fusion.103
  109.3 2.9 fusion.104
  112.5 2.0 convolution_convert_fusion.4
  115.2 30.9 %reduce-scatter.15.cloned.1.call-done = bf16[256,1024]{1,0:T(8,128)(2,1)} async-done(((bf16[1024,1024]{1,0:T(8,128)(2,1)}), bf16[256,1024]{1,0:T(8,128)(2,1)}) %reduce-scatter.15.cloned.1.call-update) | async-done | bytes 524304 | tf_op jit(solution)/shard_map/reduce_scatter | solution.py:44
  146.1 1.3 fusion.38
  147.4 1.4 multiply_reduce_fusion.4
  148.8 2.1 fusion.37
  152.5 45.1 %all-gather.14.cloned.1.call-done = bf16[1024,1024]{1,0:T(8,128)(2,1)} async-done(((bf16[128,1024]{1,0:T(8,128)(2,1)}), bf16[1024,1024]{1,0:T(8,128)(2,1)}) %all-gather.14.cloned.1.call-update) | async-done | bytes 2097168 | tf_op jit(solution)/shard_map/all_gather | solution.py:81
  197.7 23.2 %all-gather.12.cloned.1.call-done = bf16[1024,1024]{1,0:T(8,128)(2,1)} async-done(((bf16[256,1024]{1,0:T(8,128)(2,1)}), bf16[1024,1024]{1,0:T(8,128)(2,1)}) %all-gather.12.cloned.1.call-update) | async-done | bytes 2097168 | tf_op jit(solution)/shard_map/all_gather | solution.py:134
  220.8 14.9 %multiply_convert_fusion.1 = (bf16[1024,1024]{1,0:T(8,128)(2,1)}, f32[1024,1024]{1,0:T(8,128)}, f32[1024,1024]{1,0:T(8,128)}) fusion(f32[1024]{0:T(1024)S(1)} %dynamic_slice.57, bf16[1024,1024]{1,0:T(8,128)(2,1)} %all-gather.12.cloned.1.call-done, bf16[1024,1024]{1,0:T(8,128)(2,1)} %all-gather.14.cloned.1.call-done), kind=kOutput, calls=%fused_computation.37 | convolution fusion | flops 2216689664 | bytes 14684160 | tf_op jit(solution)/shard_map/dot_general | solution.py:137
  235.7 38.3 %all-gather.16.cloned.1.call-done = bf16[1024,1024]{1,0:T(8,128)(2,1)} async-done(((bf16[1024,128]{1,0:T(8,128)(2,1)}), bf16[1024,1024]{1,0:T(8,128)(2,1)}) %all-gather.16.cloned.1.call-update) | async-done | bytes 2097168 | tf_op jit(solution)/shard_map/all_gather | solution.py:82
  274.0 6.0 convolution_convert_fusion.3
  280.1 29.7 %reduce-scatter.17.cloned.1.call-done = bf16[256,1024]{1,0:T(8,128)(2,1)} async-done(((bf16[1024,1024]{1,0:T(8,128)(2,1)}), bf16[256,1024]{1,0:T(8,128)(2,1)}) %reduce-scatter.17.cloned.1.call-update) | async-done | bytes 524304 | tf_op jit(solution)/shard_map/reduce_scatter | solution.py:44
  309.8 1.6 fusion.44
  312.7 2.4 convert_reduce_fusion.2
  315.6 22.3 %all-gather.18.cloned.1.call-done = bf16[1024,1024]{1,0:T(8,128)(2,1)} async-done(((bf16[256,1024]{1,0:T(8,128)(2,1)}), bf16[1024,1024]{1,0:T(8,128)(2,1)}) %all-gather.18.cloned.1.call-update) | async-done | bytes 2097168 | tf_op jit(solution)/shard_map/all_gather | solution.py:161
  337.9 8.5 %convert_reduce_fusion = (f32[1024]{0:T(1024)S(1)}, bf16[1024,1024]{1,0:T(8,128)(2,1)S(1)}) fusion(f32[1024,1024]{1,0:T(8,128)} %get-tuple-element.401, f32[1024,1024]{1,0:T(8,128)} %get-tuple-element.419, f32[1024]{0:T(1024)S(1)} %dynamic_slice.57, bf16[1024,1024]{1,0:T(8,128)(2,1)} %all-gather.18.cloned.1.call-done, ...), kind=kOutput, calls=%fused_computation.35 | convolution fusion | flops 2165308416 | bytes 14688256 | tf_op jit(solution)/shard_map/td,fd->tf/dot_general | solution.py:165
  346.4 1.3 copy-done.23
  347.7 3.7 convolution_convert_fusion.2
  351.5 31.5 %reduce-scatter.19.cloned.1.call-done = bf16[256,1024]{1,0:T(8,128)(2,1)} async-done(((bf16[1024,1024]{1,0:T(8,128)(2,1)}), bf16[256,1024]{1,0:T(8,128)(2,1)}) %reduce-scatter.19.cloned.1.call-update) | async-done | bytes 524304 | tf_op jit(solution)/shard_map/reduce_scatter | solution.py:44
  383.0 2.0 multiply_reduce_fusion.1
  385.1 3.0 convert_reduce_fusion.3
  388.2 5.9 convolution_convert_fusion
  394.1 4.1 copy.60
  398.2 6.0 convolution_convert_fusion.1
  404.5 6.4 all-gather.20.cloned.1.call-done
  410.9 2.3 convolution_convert_fusion.5
  414.3 2.3 convolution_convert_fusion.6
  416.7 42.4 %while.31 = (s32[]{:T(128)}, bf16[2,512,256]{1,2,0:T(8,128)(2,1)}, f32[2,1024,256]{1,2,0:T(8,128)}, f32[2,1024,256]{1,2,0:T(8,128)}, s32[2]{0:T(128)S(1)}, /*ind...) while((s32[]{:T(128)}, bf16[2,512,256]{1,2,0:T(8,128)(2,1)}, ...), condition=%wide.region_17.18_spmd, body=%wide.region_15.17_spmd.sunk | while | flops 1374681088 | bytes 114100872 | solution.py:221
  422.5 1.3 fusion.115
  423.8 2.4 fusion.116
  426.2 3.2 multiply_reduce_fusion.7
  429.4 2.4 multiply_convert_fusion.3
  431.7 1.4 convolution_multiply_fusion.4
  443.6 1.3 fusion.115
  444.9 2.4 fusion.116
  447.3 3.2 multiply_reduce_fusion.7
  450.5 2.4 multiply_convert_fusion.3
  452.8 1.4 convolution_multiply_fusion.4
  459.1 1.9 reduce_sum.204
  461.0 1.8 reduce_sum.203
  463.4 4.6 fusion.22
  468.1 2.6 copy.62
  470.7 4.6 bitcast_convert_fusion
  475.7 7.3 %reduce-scatter.29.cloned.1.call-done = bf16[128,1024]{1,0:T(8,128)(2,1)} async-done(((bf16[1024,1024]{1,0:T(8,128)(2,1)}), bf16[128,1024]{1,0:T(8,128)(2,1)}) %reduce-scatter.29.cloned.1.call-update) | async-done | bytes 262160
  484.9 68.5 %reduce-scatter.23.cloned.1.call-done = bf16[128,1024]{1,0:T(8,128)(2,1)} async-done(((bf16[1024,1024]{1,0:T(8,128)(2,1)}), bf16[128,1024]{1,0:T(8,128)(2,1)}) %reduce-scatter.23.cloned.1.call-update) | async-done | bytes 262160 | tf_op jit(solution)/shard_map/reduce_scatter | solution.py:44
  553.4 1.8 convert_element_type.169
  555.6 41.0 %all-reduce = (f32[2,1024]{1,0:T(2,128)}, f32[6,1024]{1,0:T(8,128)}, f32[4096]{0:T(1024)}) all-reduce(f32[2,1024]{1,0:T(2,128)S(1)} %pad_maximum_fusion.3, f32[6,1024]{1,0:T(8,128)S(1)} %concatenate.3, f32[4096]{0:T(1024)S(1)} %dynamic_update_slice.41), channel_id=1, replica_groups=mesh['dp'=8,'tensor'=4] {'dp','tensor'}, use_global_device_ids=true, to_apply=%region_27.28 | all-reduce | flops 12288 | bytes 98304 | tf_op jit(solution)/shard_map/psum | solution.py:278
  596.7 21.4 %reduce-scatter.27.cloned.1.call-done = bf16[128,256]{1,0:T(8,128)(2,1)} async-done(((bf16[1024,256]{1,0:T(8,128)(2,1)}), bf16[128,256]{1,0:T(8,128)(2,1)}) %reduce-scatter.27.cloned.1.call-update) | async-done | bytes 65552
  619.7 65.5 %reduce-scatter.25.cloned.1.call-done = bf16[128,768]{1,0:T(8,128)(2,1)} async-done(((bf16[1024,768]{1,0:T(8,128)(2,1)}), bf16[128,768]{1,0:T(8,128)(2,1)}) %reduce-scatter.25.cloned.1.call-update) | async-done | bytes 196624
  687.2 30.9 %reduce-scatter.21.cloned.1.call-done = bf16[256,1024]{1,0:T(8,128)(2,1)} async-done(((bf16[1024,1024]{1,0:T(8,128)(2,1)}), bf16[256,1024]{1,0:T(8,128)(2,1)}) %reduce-scatter.21.cloned.1.call-update) | async-done | bytes 524304 | tf_op jit(solution)/shard_map/reduce_scatter | solution.py:239
  718.1 2.2 convert_add_fusion
  (164 shorter events, 29.4 us)
Async XLA Ops:
  7.2 51.9 %all-gather.10.cloned.1.call-start = ((), (), s32[]{:S(2)}) async-start(), calls=%async_computation.9 | async-start | bytes 1769472 | tf_op jit(solution)/shard_map/all_gather | solution.py:79
  7.9 74.2 %all-gather.8.cloned.1.call-start = ((), (), s32[]{:S(2)}) async-start(), calls=%async_computation.8 | async-start | bytes 2621440 | tf_op jit(solution)/shard_map/all_gather | solution.py:86
  8.7 137.5 %reduce-scatter.15.cloned.1.call-start = ((), (), s32[]{:S(2)}) async-start(), calls=%async_computation.10 | async-start | bytes 2621440 | tf_op jit(solution)/shard_map/reduce_scatter | solution.py:44
  40.7 71.8 %copy-start.9 = (bf16[256,1024]{1,0:T(8,128)(2,1)}, bf16[256,1024]{1,0:T(8,128)(2,1)S(1)}, u32[]{:S(2)}) copy-start(bf16[256,1024]{1,0:T(8,128)(2,1)S(1)} %all_gather.30) | copy-start | bytes 1572868
  85.5 1.7 copy-start.3
  87.2 2.4 copy-start.13
  112.5 38.5 %copy-start.11 = (bf16[2,512,256]{2,1,0:T(8,128)(2,1)}, bf16[2,512,256]{2,1,0:T(8,128)(2,1)S(1)}, u32[]{:S(2)}) copy-start(bf16[2,512,256]{2,1,0:T(8,128)(2,1)S(1)} %get-tuple-element.252) | copy-start | bytes 1572868
  112.5 2.7 copy-start.21
  112.5 2.7 copy-start.20
  112.5 33.6 %copy-start = (bf16[256,1024]{1,0:T(8,128)(2,1)S(1)}, bf16[256,1024]{1,0:T(8,128)(2,1)}, u32[]{:S(2)}) copy-start(bf16[256,1024]{1,0:T(8,128)(2,1)} %param.14) | copy-start | bytes 1572868
  114.6 83.1 %all-gather.14.cloned.1.call-start = ((), (), s32[]{:S(2)}) async-start(), calls=%async_computation.12 | async-start | bytes 2359296 | tf_op jit(solution)/shard_map/all_gather | solution.py:81
  115.1 105.7 %all-gather.12.cloned.1.call-start = ((), (), s32[]{:S(2)}) async-start(), calls=%async_computation.11 | async-start | bytes 2621440 | tf_op jit(solution)/shard_map/all_gather | solution.py:134
  151.0 123.0 %all-gather.16.cloned.1.call-start = ((), (), s32[]{:S(2)}) async-start(), calls=%async_computation.13 | async-start | bytes 2359296 | tf_op jit(solution)/shard_map/all_gather | solution.py:82
  151.6 158.2 %reduce-scatter.17.cloned.1.call-start = ((), (), s32[]{:S(2)}) async-start(), calls=%async_computation.14 | async-start | bytes 2621440 | tf_op jit(solution)/shard_map/reduce_scatter | solution.py:44
  274.0 35.8 %copy-start.1 = (bf16[256,1024]{1,0:T(8,128)(2,1)S(1)}, bf16[256,1024]{1,0:T(8,128)(2,1)}, u32[]{:S(2)}) copy-start(bf16[256,1024]{1,0:T(8,128)(2,1)} %reduce-scatter.15.cloned.1.call-done) | copy-start | bytes 1572868
  280.0 31.6 %copy-start.4 = (bf16[256,1024]{1,0:T(8,128)(2,1)S(1)}, bf16[256,1024]{1,0:T(8,128)(2,1)}, u32[]{:S(2)}) copy-start(bf16[256,1024]{1,0:T(8,128)(2,1)} %param.16) | copy-start | bytes 1572868
  280.0 57.9 %all-gather.18.cloned.1.call-start = ((), (), s32[]{:S(2)}) async-start(), calls=%async_computation.15 | async-start | bytes 2621440 | tf_op jit(solution)/shard_map/all_gather | solution.py:161
  315.1 67.9 %reduce-scatter.19.cloned.1.call-start = ((), (), s32[]{:S(2)}) async-start(), calls=%async_computation.16 | async-start | bytes 2621440 | tf_op jit(solution)/shard_map/reduce_scatter | solution.py:44
  337.9 9.8 %copy-start.22 = (bf16[1024,1024]{1,0:T(8,128)(2,1)S(1)}, bf16[1024,1024]{1,0:T(8,128)(2,1)}, u32[]{:S(2)}) copy-start(bf16[1024,1024]{1,0:T(8,128)(2,1)} %all-gather.14.cloned.1.call-done) | copy-start | bytes 6291460
  346.4 1.3 copy-start.23
  351.5 59.4 %all-gather.20.cloned.1.call-start = ((), (), s32[]{:S(2)}) async-start(), calls=%async_computation.17 | async-start | bytes 2621440 | tf_op jit(solution)/shard_map/all_gather | solution.py:182
  388.1 94.8 %reduce-scatter.29.cloned.1.call-start = ((), (), s32[]{:S(2)}) async-start(), calls=%async_computation.22 | async-start | bytes 2359296
  398.2 12.7 %copy-start.12 = (bf16[2,512,256]{2,1,0:T(8,128)(2,1)S(1)}, bf16[2,512,256]{2,1,0:T(8,128)(2,1)}, u32[]{:S(2)}) copy-start(bf16[2,512,256]{2,1,0:T(8,128)(2,1)} %copy-done.11) | copy-start | bytes 1572868
  398.2 155.2 %reduce-scatter.23.cloned.1.call-start = ((), (), s32[]{:S(2)}) async-start(), calls=%async_computation.19 | async-start | bytes 2359296 | tf_op jit(solution)/shard_map/reduce_scatter | solution.py:44
  404.2 10.1 %copy-start.10 = (bf16[256,1024]{1,0:T(8,128)(2,1)S(1)}, bf16[256,1024]{1,0:T(8,128)(2,1)}, u32[]{:S(2)}) copy-start(bf16[256,1024]{1,0:T(8,128)(2,1)} %copy-done.9) | copy-start | bytes 1572868
  404.2 213.9 %reduce-scatter.27.cloned.1.call-start = ((), (), s32[]{:S(2)}) async-start(), calls=%async_computation.21 | async-start | bytes 589824
  414.3 270.9 %reduce-scatter.25.cloned.1.call-start = ((), (), s32[]{:S(2)}) async-start(), calls=%async_computation.20 | async-start | bytes 1769472
  433.1 1.0 copy-start.14
  433.1 1.8 copy-start.5
  433.1 2.5 copy-start.7
  435.6 0.8 copy-start.15
  435.8 1.3 copy-start.6
  435.8 2.0 copy-start.8
  454.2 1.1 copy-start.14
  454.2 1.8 copy-start.5
  454.2 2.4 copy-start.7
  456.7 0.8 copy-start.15
  456.9 1.3 copy-start.6
  456.9 2.0 copy-start.8
  459.1 4.1 copy-start.16
  470.7 247.4 %reduce-scatter.21.cloned.1.call-start = ((), (), s32[]{:S(2)}) async-start(), calls=%async_computation.18 | async-start | bytes 2621440 | tf_op jit(solution)/shard_map/reduce_scatter | solution.py:239
  475.3 79.9 %copy-start.19 = (f32[1024]{0:T(1024)S(1)}, f32[1024]{0:T(1024)}, u32[]{:S(2)}) copy-start(f32[1024]{0:T(1024)} %get-tuple-element.344) | copy-start | bytes 12292
  475.3 80.3 %copy-start.17 = (f32[1024]{0:T(1024)S(1)}, f32[1024]{0:T(1024)}, u32[]{:S(2)}) copy-start(f32[1024]{0:T(1024)} %get-tuple-element.348) | copy-start | bytes 12292
  475.3 80.3 %copy-start.18 = (f32[1024]{0:T(1024)S(1)}, f32[1024]{0:T(1024)}, u32[]{:S(2)}) copy-start(f32[1024]{0:T(1024)} %get-tuple-element.392) | copy-start | bytes 12292
  475.3 242.8 %copy-start.2 = (f32[256,1024]{1,0:T(8,128)S(1)}, f32[256,1024]{1,0:T(8,128)}, u32[]{:S(2)}) copy-start(f32[256,1024]{1,0:T(8,128)} %get-tuple-element.397) | copy-start | bytes 3145732
Sparse Core Ops, SparseCore 0:
  10.2 48.8 all-gather.9
  60.7 21.3 all-gather.7
  114.7 31.4 reduce-scatter.14
  148.3 49.2 all-gather.13
  199.7 21.0 all-gather.11
  222.9 51.0 all-gather.15
  280.1 29.6 reduce-scatter.16
  315.3 22.5 all-gather.17
  351.6 31.4 reduce-scatter.18
  388.2 22.6 all-gather.19
  414.8 68.0 reduce-scatter.28
  486.7 66.6 reduce-scatter.22
  557.1 60.9 reduce-scatter.26
  621.4 63.7 reduce-scatter.24
  687.7 30.3 reduce-scatter.20

commit v2 on v1

--- a/solution.py
+++ b/solution.py
@@ -1,13 +1,515 @@
+import functools
+
 import jax
 import jax.numpy as jnp
 from jax import lax
+from jax.experimental import pallas as pl
+from jax.experimental.pallas import tpu as pltpu
 from jax.sharding import PartitionSpec as P
 
 HEAD = 64
-
-
 EPSILON = 1e-05
 NEGATIVE = -1e30
+MESH = pl.DeviceIdType.MESH
+LINES = 4
+CORE, ACROSS, FAR = 1, 2, 3
+HALVES = 2
+VMEM_BYTES = 60 << 20
+
+
+def remote(src, dst, send_sem, recv_sem, target):
+    return pltpu.make_async_remote_copy(
+        src_ref=src,
+        dst_ref=dst,
+        send_sem=send_sem,
+        recv_sem=recv_sem,
+        device_id=target,
+        device_id_type=MESH,
+    )
+
+
+def position():
+    return lax.axis_index("dp"), lax.axis_index("tensor")
+
+
+def greet(with_line):
+    dp, tensor = position()
+    barrier = pltpu.get_barrier_semaphore()
+
+    def signal(target):
+        pl.semaphore_signal(barrier, inc=1, device_id=target, device_id_type=MESH)
+
+    signal((dp, tensor ^ CORE))
+    signal((dp, tensor ^ ACROSS))
+    count = 2
+    if with_line:
+        signal((dp ^ 1, tensor))
+        line = dp // 2
+
+        @pl.when(line > 0)
+        def _():
+            signal((dp - 2, tensor))
+
+        @pl.when(line < LINES - 1)
+        def _():
+            signal((dp + 2, tensor))
+
+        ends = jnp.where(line > 0, 1, 0) + jnp.where(line < LINES - 1, 1, 0)
+        count = 3 + ends
+    pl.semaphore_wait(barrier, count)
+
+
+def row_piece(ref, index, size):
+    return ref.at[pl.ds(pl.multiple_of(index * size, size), size), :]
+
+
+def column_piece(ref, index, size):
+    return ref.at[:, pl.ds(pl.multiple_of(index * size, size), size)]
+
+
+class LineGather:
+    def __init__(self, own, full, piece, send_sem, recv_sem, local_sem):
+        self.own, self.full, self.piece = own, full, piece
+        self.send_sem, self.recv_sem, self.local_sem = send_sem, recv_sem, local_sem
+        self.dp, self.tensor = position()
+        self.line, self.side = self.dp // 2, self.dp % 2
+        self.targets = (
+            (self.dp + 2, self.tensor),
+            (self.dp - 2, self.tensor),
+            (self.dp ^ 1, self.tensor),
+        )
+
+    def copy(self, index, way, src=None):
+        view = self.piece(self.full, index)
+        return remote(
+            view if src is None else src,
+            view,
+            self.send_sem.at[way * LINES + index // 2],
+            self.recv_sem.at[index],
+            self.targets[way],
+        )
+
+    def local(self):
+        return pltpu.make_async_copy(self.own, self.piece(self.full, self.dp), self.local_sem)
+
+    def start(self):
+        self.local().start()
+
+        @pl.when(self.line < LINES - 1)
+        def _():
+            self.copy(self.dp, 0, self.own).start()
+
+        @pl.when(self.line > 0)
+        def _():
+            self.copy(self.dp, 1, self.own).start()
+
+        self.copy(self.dp, 2, self.own).start()
+
+    def step(self, distance):
+        @pl.when(self.line >= distance)
+        def _():
+            index = self.dp - 2 * distance
+            self.copy(index, 0).wait_recv()
+
+            @pl.when(self.line < LINES - 1)
+            def _():
+                self.copy(index, 0).start()
+
+            self.copy(index, 2).start()
+
+        @pl.when(self.line + distance < LINES)
+        def _():
+            index = self.dp + 2 * distance
+            self.copy(index, 1).wait_recv()
+
+            @pl.when(self.line > 0)
+            def _():
+                self.copy(index, 1).start()
+
+            self.copy(index, 2).start()
+
+    def arrive(self):
+        self.local().wait()
+        for line in range(LINES):
+            self.copy(2 * line + 1 - self.side, 2).wait_recv()
+
+    def finish(self):
+        for line in range(LINES):
+            index = 2 * line + self.side
+            self.copy(index, 2).wait_send()
+
+            @pl.when((self.line < LINES - 1) & (line <= self.line))
+            def _():
+                self.copy(index, 0).wait_send()
+
+            @pl.when((self.line > 0) & (line >= self.line))
+            def _():
+                self.copy(index, 1).wait_send()
+
+
+class RowGather:
+    def __init__(self, full, rows, send_sem, recv_sem):
+        self.full, self.rows = full, rows
+        self.send_sem, self.recv_sem = send_sem, recv_sem
+        self.dp, self.tensor = position()
+
+    def view(self, rank, half=None):
+        if half is None:
+            return row_piece(self.full, rank, self.rows)
+        return row_piece(self.full, rank * HALVES + half, self.rows // HALVES)
+
+    def near(self, rank):
+        view = self.view(rank)
+        target = (self.dp, self.tensor ^ CORE)
+        return remote(view, view, self.send_sem.at[0], self.recv_sem.at[0], target)
+
+    def across(self, rank, half):
+        view, slot = self.view(rank, half), 1 + half
+        target = (self.dp, self.tensor ^ ACROSS)
+        return remote(view, view, self.send_sem.at[slot], self.recv_sem.at[slot], target)
+
+    def far(self, rank, half):
+        view, slot = self.view(rank, half), 1 + HALVES + half
+        target = (self.dp, self.tensor ^ CORE)
+        return remote(view, view, self.send_sem.at[slot], self.recv_sem.at[slot], target)
+
+    def start(self):
+        for half in range(HALVES):
+            self.across(self.tensor, half).start()
+        self.near(self.tensor).start()
+
+    def wait_near(self):
+        self.near(self.tensor ^ CORE).wait_recv()
+
+    def wait_across(self, half):
+        self.across(self.tensor ^ ACROSS, half).wait_recv()
+        self.far(self.tensor ^ ACROSS, half).start()
+
+    def wait_far(self, half):
+        self.far(self.tensor ^ FAR, half).wait_recv()
+
+    def finish(self):
+        self.near(self.tensor).wait_send()
+        for half in range(HALVES):
+            self.across(self.tensor, half).wait_send()
+            self.far(self.tensor ^ ACROSS, half).wait_send()
+
+
+GATHER_SEMS = [pltpu.SemaphoreType.DMA((1 + 2 * HALVES,))] * 2
+
+
+class RowScatter:
+    def __init__(self, near_out, near_in, across_out, across_in, send_sem, recv_sem):
+        self.near_out, self.near_in = near_out, near_in
+        self.across_out, self.across_in = across_out, across_in
+        self.send_sem, self.recv_sem = send_sem, recv_sem
+        self.dp, self.tensor = position()
+
+    def near(self, slot):
+        return remote(
+            self.near_out.at[slot],
+            self.near_in.at[slot],
+            self.send_sem.at[slot],
+            self.recv_sem.at[slot],
+            (self.dp, self.tensor ^ CORE),
+        )
+
+    def across(self, half):
+        rows = self.across_in.shape[0] // HALVES
+        return remote(
+            row_piece(self.across_out, half, rows),
+            row_piece(self.across_in, half, rows),
+            self.send_sem.at[2 * HALVES + half],
+            self.recv_sem.at[2 * HALVES + half],
+            (self.dp, self.tensor ^ ACROSS),
+        )
+
+    def give_far(self, half, partial):
+        self.near_out[half] = partial.astype(jnp.bfloat16)
+        self.near(half).start()
+
+    def give_across(self, half, partial):
+        self.near(half).wait_recv()
+        rows = partial.shape[0]
+        total = partial + self.near_in[half].astype(jnp.float32)
+        self.across_out[half * rows : (half + 1) * rows, :] = total.astype(jnp.bfloat16)
+        self.across(half).start()
+
+    def give_near(self, half, partial):
+        self.near_out[HALVES + half] = partial.astype(jnp.bfloat16)
+        self.near(HALVES + half).start()
+
+    def take(self, half, partial):
+        self.near(HALVES + half).wait_recv()
+        rows = partial.shape[0]
+        total = partial + self.near_in[HALVES + half].astype(jnp.float32)
+        self.across(half).wait_recv()
+        return total + self.across_in[half * rows : (half + 1) * rows, :].astype(jnp.float32)
+
+    def finish(self):
+        for slot in range(2 * HALVES):
+            self.near(slot).wait_send()
+        for half in range(HALVES):
+            self.across(half).wait_send()
+
+
+def scatter_scratch(rows, width):
+    half = rows // HALVES
+    return [
+        pltpu.VMEM((2 * HALVES, half, width), jnp.bfloat16),
+        pltpu.VMEM((2 * HALVES, half, width), jnp.bfloat16),
+        pltpu.VMEM((rows, width), jnp.bfloat16),
+        pltpu.VMEM((rows, width), jnp.bfloat16),
+        pltpu.SemaphoreType.DMA((3 * HALVES,)),
+        pltpu.SemaphoreType.DMA((3 * HALVES,)),
+    ]
+
+
+def dot(left, right):
+    return jnp.dot(left, right, preferred_element_type=jnp.float32)
+
+
+def dot_nt(left, right):
+    return lax.dot_general(left, right, (((1,), (1,)), ((), ())), preferred_element_type=jnp.float32)
+
+
+def dot_tn(left, right):
+    return lax.dot_general(left, right, (((0,), (0,)), ((), ())), preferred_element_type=jnp.float32)
+
+
+def normalize(rows):
+    centred = rows - jnp.mean(rows, axis=-1, keepdims=True)
+    inverse = lax.rsqrt(jnp.mean(centred * centred, axis=-1, keepdims=True) + EPSILON)
+    return centred * inverse, inverse
+
+
+def block_rows(ref, rank, rows):
+    return ref[pl.ds(pl.multiple_of(rank * rows, rows), rows), :]
+
+
+def attend_kernel(
+    rows,
+    tokens,
+    triple_own,
+    output_own,
+    up_own,
+    down_own,
+    segment_column,
+    segment_row,
+    bias_rows,
+    norm_gains,
+    gathered_out,
+    triple_out,
+    output_out,
+    up_full,
+    down_full,
+    queries,
+    key_rows,
+    value_rows,
+    mixed,
+    log_totals,
+    normed_out,
+    inverse_out,
+    first_low,
+    gathered,
+    triple,
+    output,
+    line_send,
+    line_recv,
+    line_local,
+    row_send,
+    row_recv,
+    near_out,
+    near_in,
+    across_out,
+    across_in,
+    sum_send,
+    sum_recv,
+    save_sem,
+):
+    dp, tensor = position()
+    local = queries.shape[1]
+    gather = RowGather(gathered, rows, row_send, row_recv)
+    scatter = RowScatter(near_out, near_in, across_out, across_in, sum_send, sum_recv)
+    piece = triple_own.shape[0]
+
+    def of_rows(ref, index):
+        return row_piece(ref, index, piece)
+
+    def of_columns(ref, index):
+        return column_piece(ref, index, piece)
+
+    def line(at, own, full, view):
+        return LineGather(own, full, view, line_send.at[at], line_recv.at[at], line_local.at[at])
+
+    triple_line = line(0, triple_own, triple, of_rows)
+    output_line = line(1, output_own, output, of_columns)
+    up_line = line(2, up_own, up_full, of_rows)
+    down_line = line(3, down_own, down_full, of_columns)
+    greet(True)
+    place = pltpu.make_async_copy(tokens, gather.view(tensor), save_sem.at[0])
+    place.start()
+    triple_line.start()
+    place.wait()
+    gather.start()
+    triple_line.step(1)
+    triple_line.step(2)
+    gather.wait_near()
+    for half in range(HALVES):
+        gather.wait_across(half)
+    triple_line.step(3)
+    output_line.start()
+    up_line.start()
+    for half in range(HALVES):
+        gather.wait_far(half)
+    triple_line.arrive()
+    saves = [
+        pltpu.make_async_copy(gathered, gathered_out, save_sem.at[0]),
+        pltpu.make_async_copy(triple, triple_out, save_sem.at[1]),
+    ]
+    for save in saves:
+        save.start()
+    columns = pl.ds(pl.multiple_of(tensor * local, local), local)
+    query_bias = bias_rows[0:1, columns]
+    value_bias = bias_rows[1:2, columns]
+
+    @pl.loop(0, 4)
+    def _(block):
+        here = pl.ds(pl.multiple_of(block * rows, rows), rows)
+        left = gathered[here, :]
+        query = (dot(left, triple[:, :local]) + query_bias).astype(jnp.bfloat16)
+        queries[here, :] = query * jnp.bfloat16(HEAD**-0.5)
+        key_rows[here, :] = dot(left, triple[:, local : 2 * local]).astype(jnp.bfloat16)
+        value = dot(left, triple[:, 2 * local :]) + value_bias
+        value_rows[here, :] = value.astype(jnp.bfloat16)
+
+    output_line.step(1)
+    up_line.step(1)
+
+    def attend(rank):
+        here = pl.ds(pl.multiple_of(rank * rows, rows), rows)
+
+        @pl.loop(0, local // (2 * HEAD))
+        def _(pair):
+            lanes = pl.ds(pl.multiple_of(pair * 2 * HEAD, 2 * HEAD), 2 * HEAD)
+            query = queries[here, lanes]
+            keys = key_rows[:, lanes]
+            values = value_rows[:, lanes]
+            same = segment_column[here, :] == segment_row[...]
+            lane = lax.broadcasted_iota(jnp.int32, (rows, 2 * HEAD), 1)
+            outs = []
+            for side in range(2):
+                mine = lane // HEAD == side
+                scores = dot_nt(jnp.where(mine, query, jnp.bfloat16(0)), keys)
+                scores = jnp.where(same, scores, NEGATIVE)
+                top = jnp.max(scores, axis=-1, keepdims=True)
+                exponent = jnp.exp(scores - top)
+                total = jnp.sum(exponent, axis=-1, keepdims=True)
+                weights = (exponent * (1.0 / total)).astype(jnp.bfloat16)
+                outs.append(dot(weights, values))
+                log_totals[pair * 2 + side, here, :] = top + jnp.log(total)
+            mixed[here, lanes] = jnp.where(lane < HEAD, outs[0], outs[1]).astype(jnp.bfloat16)
+
+        return mixed[here, :]
+
+    def halves_of(partial):
+        half = rows // HALVES
+        return [partial[at * half : (at + 1) * half] for at in range(HALVES)]
+
+    far = attend(tensor ^ FAR)
+    output_line.step(2)
+    output_line.step(3)
+    up_line.step(2)
+    output_line.arrive()
+    save = pltpu.make_async_copy(output, output_out, save_sem.at[2])
+    save.start()
+    saves.append(save)
+    for half, partial in enumerate(halves_of(dot(far, output[...]))):
+        scatter.give_far(half, partial)
+    other = attend(tensor ^ ACROSS)
+    for half, partial in enumerate(halves_of(dot(other, output[...]))):
+        scatter.give_across(half, partial)
+    up_line.step(3)
+    down_line.start()
+    near = attend(tensor ^ CORE)
+    for half, partial in enumerate(halves_of(dot(near, output[...]))):
+        scatter.give_near(half, partial)
+    down_line.step(1)
+    mine = attend(tensor)
+    for half, partial in enumerate(halves_of(dot(mine, output[...]))):
+        part = slice(half * rows // HALVES, (half + 1) * rows // HALVES)
+        total = scatter.take(half, partial) + bias_rows[2:3, :]
+        own_rows = row_piece(gathered, tensor * HALVES + half, rows // HALVES)
+        normed, inverse = normalize(own_rows[...].astype(jnp.float32) + total)
+        normed_out[part, :] = normed
+        inverse_out[part, :] = inverse
+        first_low[part, :] = (normed * norm_gains[0:1, :] + bias_rows[3:4, :]).astype(jnp.bfloat16)
+    scatter.finish()
+    gather.finish()
+    down_line.step(2)
+    down_line.step(3)
+    for each in (up_line, down_line):
+        each.arrive()
+    for each in (triple_line, output_line, up_line, down_line):
+        each.finish()
+    for save in saves:
+        save.wait()
+
+
+def attend_forward(tokens, triple_own, output_own, up_own, down_own, segments, bias_rows, norm_gains):
+    rows, width = tokens.shape
+    length = segments.shape[1]
+    local = triple_own.shape[1] // 3
+    heads = local // HEAD
+    pieces = 2 * LINES
+    bf16, f32 = jnp.bfloat16, jnp.float32
+    vmem, hbm = pl.BlockSpec(memory_space=pltpu.VMEM), pl.BlockSpec(memory_space=pltpu.HBM)
+    hidden = up_own.shape[1]
+    return pl.pallas_call(
+        functools.partial(attend_kernel, rows),
+        out_shape=[
+            jax.ShapeDtypeStruct((length, width), bf16),
+            jax.ShapeDtypeStruct((width, 3 * local), bf16),
+            jax.ShapeDtypeStruct((local, width), bf16),
+            jax.ShapeDtypeStruct((width, hidden), bf16),
+            jax.ShapeDtypeStruct((hidden, width), bf16),
+            jax.ShapeDtypeStruct((length, local), bf16),
+            jax.ShapeDtypeStruct((length, local), bf16),
+            jax.ShapeDtypeStruct((length, local), bf16),
+            jax.ShapeDtypeStruct((length, local), bf16),
+            jax.ShapeDtypeStruct((heads, length, 1), f32),
+            jax.ShapeDtypeStruct((rows, width), f32),
+            jax.ShapeDtypeStruct((rows, 1), f32),
+            jax.ShapeDtypeStruct((rows, width), bf16),
+        ],
+        in_specs=[hbm] * 5 + [vmem] * 4,
+        out_specs=[hbm] * 5 + [vmem] * 8,
+        scratch_shapes=[
+            pltpu.VMEM((length, width), bf16),
+            pltpu.VMEM((width, 3 * local), bf16),
+            pltpu.VMEM((local, width), bf16),
+            pltpu.SemaphoreType.DMA((4, 3 * LINES)),
+            pltpu.SemaphoreType.DMA((4, pieces)),
+            pltpu.SemaphoreType.DMA((4,)),
+        ]
+        + GATHER_SEMS
+        + scatter_scratch(rows, width)
+        + [pltpu.SemaphoreType.DMA((3,))],
+        compiler_params=pltpu.CompilerParams(
+            collective_id=0, has_side_effects=True, vmem_limit_bytes=VMEM_BYTES
+        ),
+        name="attend_forward",
+    )(
+        tokens,
+        triple_own,
+        output_own,
+        up_own,
+        down_own,
+        segments.reshape(length, 1),
+        segments.reshape(1, length),
+        bias_rows,
+        norm_gains,
+    )
 
 
 def gelu_exact(values):
@@ -291,6 +793,230 @@
     )
 
 
+def per_device_kernels(
+    tokens,
+    segments,
+    cotangent,
+    project_weight,
+    output_weight,
+    up_weight,
+    down_weight,
+    norm_gains,
+    bias_rows,
+    hidden_bias,
+):
+    tensor_rank = lax.axis_index("tensor")
+    local_rows, model_width = tokens.shape
+    seq_count, seq_length = segments.shape
+    group_rows = seq_count * seq_length
+    local_width = project_weight.shape[2]
+    score_scale = HEAD ** (-0.5)
+    block_rows = min(512, seq_length)
+    per_sequence = seq_length // block_rows
+    count_blocks = group_rows // block_rows
+    block_ids = jnp.arange(count_blocks, dtype=jnp.int32)
+    (
+        gathered,
+        triple_matrix,
+        output_full,
+        upward_full,
+        downward_full,
+        queries,
+        key_rows,
+        value_rows,
+        mixed_rows,
+        log_totals,
+        normed_one,
+        inverse_one,
+        first_low,
+    ) = attend_forward(
+        tokens,
+        project_weight.reshape(project_weight.shape[0], -1),
+        output_weight,
+        up_weight,
+        down_weight,
+        segments,
+        bias_rows,
+        norm_gains,
+    )
+    first_out = normed_one * norm_gains[0] + bias_rows[3]
+    first_saved = (normed_one, inverse_one)
+    queries = queries * jnp.bfloat16(8)
+    log_totals = jnp.stack(
+        [log_totals[:, i * block_rows : (i + 1) * block_rows, 0] for i in range(count_blocks)]
+    )
+    local_hidden = upward_full.shape[1]
+    def block_parts(block_index):
+        sequence = block_index // per_sequence
+        row_start = block_index * block_rows
+        seq_start = sequence * seq_length
+        query_block = split_heads(lax.dynamic_slice_in_dim(queries, row_start, block_rows, 0))
+        key_block = split_heads(key_rows)
+        value_block = split_heads(value_rows)
+        seq_ids = lax.dynamic_index_in_dim(segments, sequence, 0, keepdims=False)
+        query_ids = lax.dynamic_slice_in_dim(seq_ids, row_start - seq_start, block_rows, 0)
+        products = (
+            jnp.einsum("qhd,khd->hqk", query_block, key_block, preferred_element_type=jnp.float32)
+            * score_scale
+        )
+        scores = jnp.where((query_ids[:, None] == seq_ids[None, :])[None], products, NEGATIVE)
+        return (row_start, query_block, key_block, value_block, scores)
+
+    first_gathered = lax.all_gather(first_low, "tensor", axis=0, tiled=True)
+    local_bias = lax.dynamic_slice_in_dim(hidden_bias, tensor_rank * local_hidden, local_hidden, 0)
+    upper_rows = (
+        jnp.dot(first_gathered, upward_full, preferred_element_type=jnp.float32) + local_bias
+    )
+    hidden_full, gelu_back = jax.vjp(gelu_exact, upper_rows)
+    hidden_rows = hidden_full.astype(jnp.bfloat16)
+    second_out = (
+        scatter_sum(
+            jnp.dot(hidden_rows, downward_full, preferred_element_type=jnp.float32), "tensor", 0
+        )
+        + bias_rows[4]
+    )
+    layer_out, second_saved = layer_norm(first_out + second_out, norm_gains[1], bias_rows[5])
+    reloaded = (triple_matrix, output_full, upward_full, downward_full)
+    back_triple = triple_matrix.reshape(model_width, 3 * local_width)
+    back_output, back_upward, back_downward = (reloaded[1], reloaded[2], reloaded[3])
+    grad_layer = cotangent.astype(jnp.float32)
+    grad_second_in, grad_gain_two, grad_shift_two = norm_back(
+        grad_layer, second_saved, norm_gains[1]
+    )
+    grad_second = grad_second_in.astype(jnp.bfloat16)
+    grad_second_all = lax.all_gather(grad_second, "tensor", axis=0, tiled=True)
+    grad_down_part = jnp.einsum(
+        "tf,td->fd", hidden_rows, grad_second_all, preferred_element_type=jnp.float32
+    )
+    grad_hidden = jnp.einsum(
+        "td,fd->tf", grad_second_all, back_downward, preferred_element_type=jnp.float32
+    )
+    grad_upper = gelu_back(grad_hidden)[0].astype(jnp.bfloat16)
+    grad_up_part = jnp.einsum(
+        "td,tf->df", first_gathered, grad_upper, preferred_element_type=jnp.float32
+    )
+    grad_first = (
+        scatter_sum(
+            jnp.einsum("tf,df->td", grad_upper, back_upward, preferred_element_type=jnp.float32),
+            "tensor",
+            0,
+        )
+        + grad_second_in
+    )
+    grad_first_in, grad_gain_one, grad_shift_one = norm_back(grad_first, first_saved, norm_gains[0])
+    grad_branch = grad_first_in.astype(jnp.bfloat16)
+    grad_branch_all = lax.all_gather(grad_branch, "tensor", axis=0, tiled=True)
+    grad_output_part = jnp.einsum(
+        "tc,td->cd", mixed_rows, grad_branch_all, preferred_element_type=jnp.float32
+    )
+    grad_mixed = jnp.einsum(
+        "td,cd->tc", grad_branch_all, back_output, preferred_element_type=jnp.float32
+    ).astype(jnp.bfloat16)
+
+    def backward_block(block_index):
+        row_start, query_block, key_block, value_block, scores = block_parts(block_index)
+        weights_full = jnp.exp(scores - log_totals[block_index][:, :, None])
+        grad_mixed_block = split_heads(
+            lax.dynamic_slice_in_dim(grad_mixed, row_start, block_rows, 0)
+        )
+        grad_weights = jnp.einsum(
+            "qhd,khd->hqk", grad_mixed_block, value_block, preferred_element_type=jnp.float32
+        )
+        row_dot = jnp.sum(weights_full * grad_weights, axis=-1, keepdims=True)
+        grad_scores = (weights_full * (grad_weights - row_dot)).astype(jnp.bfloat16)
+        grad_query = (
+            jnp.einsum("hqk,khd->qhd", grad_scores, key_block, preferred_element_type=jnp.float32)
+            * score_scale
+        )
+        grad_key = (
+            jnp.einsum("hqk,qhd->khd", grad_scores, query_block, preferred_element_type=jnp.float32)
+            * score_scale
+        )
+        grad_value = jnp.einsum(
+            "hqk,qhd->khd",
+            weights_full.astype(jnp.bfloat16),
+            grad_mixed_block,
+            preferred_element_type=jnp.float32,
+        )
+        return (
+            grad_query.reshape(block_rows, local_width),
+            grad_key.reshape(seq_length, local_width),
+            grad_value.reshape(seq_length, local_width),
+        )
+
+    query_blocks, key_blocks, value_blocks = lax.map(backward_block, block_ids)
+    grad_queries = query_blocks.reshape(group_rows, local_width)
+    grad_keys = (
+        key_blocks.reshape(seq_count, per_sequence, seq_length, local_width)
+        .sum(axis=1)
+        .reshape(group_rows, local_width)
+    )
+    grad_values = (
+        value_blocks.reshape(seq_count, per_sequence, seq_length, local_width)
+        .sum(axis=1)
+        .reshape(group_rows, local_width)
+    )
+    grad_projected = jnp.stack((grad_queries, grad_keys, grad_values), axis=1).astype(jnp.bfloat16)
+    grad_project_part = jnp.einsum(
+        "te,tsc->esc", gathered, grad_projected, preferred_element_type=jnp.float32
+    )
+    grad_matrix = grad_projected.reshape(group_rows, 3 * local_width)
+    grad_tokens = (
+        lax.psum_scatter(
+            jnp.einsum(
+                "tc,ec->te", grad_matrix, back_triple, preferred_element_type=jnp.float32
+            ).astype(jnp.bfloat16),
+            "tensor",
+            scatter_dimension=0,
+            tiled=True,
+        ).astype(jnp.float32)
+        + grad_first_in
+    )
+    grad_project, grad_output, grad_up, grad_down = (
+        scatter_sum(grad_project_part, "dp", 0),
+        scatter_sum(grad_output_part, "dp", 1),
+        scatter_sum(grad_up_part, "dp", 0),
+        scatter_sum(grad_down_part, "dp", 1),
+    )
+    head_terms = place_columns(
+        jnp.stack(
+            (
+                jnp.sum(grad_projected[:, 0], axis=0, dtype=jnp.float32),
+                jnp.sum(grad_projected[:, 2], axis=0, dtype=jnp.float32),
+            )
+        ),
+        tensor_rank,
+        model_width,
+    )
+    shared_terms = jnp.stack(
+        (
+            jnp.sum(grad_branch, axis=0, dtype=jnp.float32),
+            grad_shift_one,
+            jnp.sum(grad_second, axis=0, dtype=jnp.float32),
+            grad_shift_two,
+        )
+    )
+    bias_terms = jnp.concatenate((head_terms, shared_terms), axis=0)
+    gain_terms = jnp.stack((grad_gain_one, grad_gain_two))
+    hidden_terms = place_columns(
+        jnp.sum(grad_upper, axis=0, dtype=jnp.float32), tensor_rank, hidden_bias.shape[0]
+    )
+    grad_gains, grad_bias_rows, grad_hidden_bias = lax.psum(
+        (gain_terms, bias_terms, hidden_terms), ("dp", "tensor")
+    )
+    return (
+        layer_out.astype(jnp.bfloat16),
+        grad_tokens,
+        grad_project,
+        grad_output,
+        grad_up,
+        grad_down,
+        grad_gains,
+        grad_bias_rows,
+        grad_hidden_bias,
+    )
+
+
 def solution(mesh):
     placed = (
         P(("dp", "tensor"), None),
@@ -304,8 +1030,9 @@
         P(),
         P(),
     )
+    fits = mesh.shape["dp"] == 2 * LINES and mesh.shape["tensor"] == 4
     return jax.shard_map(
-        per_device,
+        per_device_kernels if fits else per_device,
         mesh=mesh,
         in_specs=placed,
         out_specs=(

time: 735 us -> 591 us (0.80)
  waiting for transfers between devices: 463 us -> 302 us
  Pallas kernels: 0 us -> 80.8 us
  blocking collectives: 72.2 us -> 41 us
  matrix products: 91.6 us -> 77.6 us
  other arithmetic: 37.3 us -> 26.4 us
    all_gather x7 -> x3, waiting for transfers between devices: 175 us -> 49.1 us  [the longest x1 23 us: per_device_kernels(): first_gathered = lax.all_gather(first_low, 'tensor', axis=0, tiled=True)]
    pallas_call x0 -> x1, Pallas kernels: none -> 80.8 us  [attend_forward(): pl.pallas_call(functools.partial(attend_kernel, rows), out_shape=[jax.Sha...]
    unnamed x18 -> x12, waiting for transfers between devices: 96.8 us -> 24.6 us
    reduce_scatter x4, waiting for transfers between devices: 161 us -> 198 us  [scatter_sum(): lax.psum_scatter(partial_sum.astype(jnp.bfloat16), axis_name, scatter_dim...]
    all_gather x1 -> x0, blocking collectives: 31.2 us -> none  [per_device(): lax.all_gather(output_weight, 'dp', axis=1, tiled=True)]
    dot_general x14 -> x10, matrix products: 70 us -> 57.2 us  [the longest x1 14.8 us: per_device_kernels(): jnp.dot(first_gathered, upward_full, preferred_element_type=jnp.float32)]
    another operation x2 -> x1, loops' own time: 16.2 us -> 9.09 us  [per_device_kernels(): query_blocks, key_blocks, value_blocks = lax.map(backward_block, block_ids)]
    unnamed x43 -> x41, local copies, waits for them, and re-layouts: 14.8 us -> 9.48 us
  transfers between devices with their start and end apart: 15 -> 10, of which waited for: 15 -> 10; matrix products, arithmetic and copies ran while one was open for 13% -> 15% of each run, Pallas kernels for 0% -> 0%
where the time goes in v2:
time: 591 us; the launch traced here: 584 us
  waiting for transfers between devices  302 us (51%)
  Pallas kernels  80.8 us (14%)
  matrix products  77.6 us (13%)
  blocking collectives  41 us (7%)
  local copies, waits for them, and re-layouts  30.7 us (5%)
  other arithmetic  26.4 us (4%)
  between operations  14.7 us (2%)
  loops' own time  9.09 us (2%)
    reduce_scatter x4, waiting for transfers between devices, scatter_sum(): lax.psum_scatter(partial_sum.astype(jnp.bfloat16), axis_name, scatter_dim...  198 us
    pallas_call x1, Pallas kernels, attend_forward(): pl.pallas_call(functools.partial(attend_kernel, rows), out_shape=[jax.Sha...  80.8 us
    psum x1, blocking collectives, per_device_kernels(): lax.psum((gain_terms, bias_terms, hidden_terms), ('dp', 'tensor'))  41 us
    reduce_scatter x1, waiting for transfers between devices, per_device_kernels(): lax.psum_scatter(jnp.einsum('tc,ec->te', grad_matrix, back_triple, prefer...  31 us
    unnamed x12, waiting for transfers between devices  24.6 us
    all_gather x1, waiting for transfers between devices, per_device_kernels(): first_gathered = lax.all_gather(first_low, 'tensor', axis=0, tiled=True)  23 us
    all_gather x1, waiting for transfers between devices, per_device_kernels(): grad_second_all = lax.all_gather(grad_second, 'tensor', axis=0, tiled=True)  22.3 us
    dot_general x1, matrix products, per_device_kernels(): jnp.dot(first_gathered, upward_full, preferred_element_type=jnp.float32)  14.8 us
  transfers between devices with their start and end apart: 10, of which 10 were waited for; matrix products, arithmetic and copies ran while one was open for 15% of the time, Pallas kernels for 0%

profile of v2, /device:TPU:0, one launch (start us, length us, event | category | flops | bytes accessed | tf_op | source)
XLA Modules:
  0.0 584.0 jit_solution(6216480446898461292)
XLA Ops:
  7.2 1.1 copy.47
  9.1 1.7 copy.49.segment_column
  10.8 80.8 %attend_forward.1 = (bf16[1024,1024]{1,0:T(8,128)(2,1)}, bf16[1024,768]{1,0:T(8,128)(2,1)}, bf16[256,1024]{1,0:T(8,128)(2,1)}, bf16[1024,1024]{1,0:T(8,128)(2,1)...) custom-call(bf16[256,1024]{1,0:T(8,128)(2,1)} %tokens.1, ...), custom_call_target="tpu_custom_call" | custom-call | tf_op jit(solution)/shard_map/attend_forward/pallas_call | solution.py:468
  92.7 23.0 %all-gather.4.cloned.1.call-done = bf16[1024,1024]{1,0:T(8,128)(2,1)} async-done(((bf16[256,1024]{1,0:T(8,128)(2,1)}), bf16[1024,1024]{1,0:T(8,128)(2,1)}) %all-gather.4.cloned.1.call-update) | async-done | bytes 2097168 | tf_op jit(solution)/shard_map/all_gather | solution.py:865
  115.7 14.8 %multiply_convert_fusion.1 = (bf16[1024,1024]{1,0:T(8,128)(2,1)S(1)}, f32[1024,1024]{1,0:T(8,128)}, f32[1024,1024]{1,0:T(8,128)}) fusion(f32[1024]{0:T(1024)S(1)} %dynamic_slice.35, bf16[1024,1024]{1,0:T(8,128)(2,1)} %all-gather.4.cloned.1.call-done, bf16[1024,1024]{1,0:T(8,128)(2,1)} %get-tuple-element.164), kind=kOutput, calls=%fused_computation.22 | convolution fusion | flops 2216689664 | bytes 14684160 | tf_op jit(solution)/shard_map/dot_general | solution.py:868
  130.5 1.3 copy-done.16
  131.8 3.7 convolution_convert_fusion.3
  135.6 0.9 fusion.28
  136.5 30.6 %reduce-scatter.12.cloned.1.call-done = bf16[256,1024]{1,0:T(8,128)(2,1)} async-done(((bf16[1024,1024]{1,0:T(8,128)(2,1)}), bf16[256,1024]{1,0:T(8,128)(2,1)}) %reduce-scatter.12.cloned.1.call-update) | async-done | bytes 524304 | tf_op jit(solution)/shard_map/reduce_scatter | solution.py:546
  167.1 1.3 fusion.26
  168.7 1.1 fusion.23
  169.8 2.0 convert_reduce_fusion.2
  172.3 22.3 %all-gather.6.cloned.1.call-done = bf16[1024,1024]{1,0:T(8,128)(2,1)} async-done(((bf16[256,1024]{1,0:T(8,128)(2,1)}), bf16[1024,1024]{1,0:T(8,128)(2,1)}) %all-gather.6.cloned.1.call-update) | async-done | bytes 2097168 | tf_op jit(solution)/shard_map/all_gather | solution.py:887
  194.6 9.1 %convert_reduce_fusion = (f32[1024]{0:T(1024)}, bf16[1024,1024]{1,0:T(8,128)(2,1)S(1)}) fusion(f32[1024,1024]{1,0:T(8,128)} %get-tuple-element.270, f32[1024,1024]{1,0:T(8,128)} %get-tuple-element.281, f32[1024]{0:T(1024)S(1)} %dynamic_slice.35, bf16[1024,1024]{1,0:T(8,128)(2,1)} %all-gather.6.cloned.1.call-done, bf16[1024,1024]{1,0:T(8,128)(2,1)} %get-tuple-element.165), kind=kOutput, calls=%fused_computation.20 | convolution fusion | flops 2165308416 | bytes 14688256 | tf_op jit(solution)/shard_map/td,fd->tf/dot_general | solution.py:891
  203.6 1.3 copy-done.17
  205.0 3.7 convolution_convert_fusion.2
  208.9 31.4 %reduce-scatter.14.cloned.1.call-done = bf16[256,1024]{1,0:T(8,128)(2,1)} async-done(((bf16[1024,1024]{1,0:T(8,128)(2,1)}), bf16[256,1024]{1,0:T(8,128)(2,1)}) %reduce-scatter.14.cloned.1.call-update) | async-done | bytes 524304 | tf_op jit(solution)/shard_map/reduce_scatter | solution.py:546
  240.3 1.5 multiply_reduce_fusion.1
  241.8 2.5 convert_reduce_fusion.3
  244.4 4.6 convolution_convert_fusion
  249.1 2.6 copy.63
  251.7 6.3 %convolution_convert_fusion.1 = bf16[1024,1024]{1,0:T(8,128)(2,1)} fusion(bf16[1024,1024]{1,0:T(8,128)(2,1)} %all-gather.4.cloned.1.call-done, bf16[1024,1024]{1,0:T(8,128)(2,1)} %copy-done.17), kind=kOutput, calls=%fused_computation.40 | convolution fusion | flops 2148532224 | bytes 6291456 | tf_op jit(solution)/shard_map/td,tf->df/dot_general | solution.py:895
  258.3 1.4 copy.51
  259.7 2.1 copy.53
  262.4 0.9 broadcast_multiply_fusion
  263.3 3.8 all-gather.8.cloned.1.call-done
  267.1 2.6 convolution_convert_fusion.5
  269.8 1.0 copy.61
  270.9 2.6 convolution_convert_fusion.6
  273.5 45.3 %while.16 = (s32[]{:T(128)}, bf16[2,512,256]{2,1,0:T(8,128)(2,1)}, f32[2,1024,256]{1,2,0:T(8,128)}, f32[2,1024,256]{1,2,0:T(8,128)}, s32[2]{0:T(128)S(1)}, /*ind...) while((s32[]{:T(128)}, bf16[2,512,256]{2,1,0:T(8,128)(2,1)}, ...), condition=%wide.region_10.0_spmd, body=%wide.region_8.10_spmd.sunk | while | flops 1374681088 | bytes 77400544 | solution.py:947
  278.5 1.0 constant_dynamic-slice_fusion.8
  279.6 1.0 constant_dynamic-slice_fusion.6
  281.1 1.3 fusion.80
  282.4 2.4 fusion.81
  284.8 4.2 multiply_reduce_fusion.6
  289.0 2.4 multiply_convert_fusion.3
  291.4 1.4 convolution_multiply_fusion.4
  292.8 0.9 convolution_multiply_fusion.5
  294.5 1.5 constant_dynamic-update-slice_fusion.6
  301.1 1.0 constant_dynamic-slice_fusion.8
  302.2 1.0 constant_dynamic-slice_fusion.6
  303.7 1.3 fusion.80
  305.0 2.4 fusion.81
  307.4 4.2 multiply_reduce_fusion.6
  311.6 2.4 multiply_convert_fusion.3
  314.0 1.4 convolution_multiply_fusion.4
  315.4 0.9 convolution_multiply_fusion.5
  317.1 1.5 constant_dynamic-update-slice_fusion.6
  318.8 1.9 reduce_sum.172
  320.7 1.8 reduce_sum.171
  322.9 4.8 fusion.14
  327.9 1.8 copy.57
  329.7 5.1 convolution_convert_fusion.4
  335.2 3.3 reduce-scatter.24.cloned.1.call-done
  338.5 1.1 copy.64
  340.4 68.9 %reduce-scatter.20.cloned.1.call-done = bf16[128,1024]{1,0:T(8,128)(2,1)} async-done(((bf16[1024,1024]{1,0:T(8,128)(2,1)}), bf16[128,1024]{1,0:T(8,128)(2,1)}) %reduce-scatter.20.cloned.1.call-update) | async-done | bytes 262160 | tf_op jit(solution)/shard_map/reduce_scatter | solution.py:546
  409.3 1.8 convert_element_type.119
  411.4 41.0 %all-reduce = (f32[2,1024]{1,0:T(2,128)}, f32[6,1024]{1,0:T(8,128)}, f32[4096]{0:T(1024)}) all-reduce(f32[2,1024]{1,0:T(2,128)S(1)} %pad_maximum_fusion.1, f32[6,1024]{1,0:T(8,128)S(1)} %concatenate.3, f32[4096]{0:T(1024)S(1)} %dynamic_update_slice.27), channel_id=1, replica_groups=mesh['dp'=8,'tensor'=4] {'dp','tensor'}, use_global_device_ids=true, to_apply=%region_20.21 | all-reduce | flops 12288 | bytes 98304 | tf_op jit(solution)/shard_map/psum | solution.py:1004
  452.4 21.2 %reduce-scatter.22.cloned.1.call-done = bf16[128,256]{1,0:T(8,128)(2,1)} async-done(((bf16[1024,256]{1,0:T(8,128)(2,1)}), bf16[128,256]{1,0:T(8,128)(2,1)}) %reduce-scatter.22.cloned.1.call-update) | async-done | bytes 65552
  473.6 0.9 copy.62
  475.2 66.8 %reduce-scatter.18.cloned.1.call-done = bf16[128,3,256]{2,0,1:T(8,128)(2,1)} async-done(((bf16[1024,3,256]{2,0,1:T(8,128)(2,1)}), bf16[128,3,256]{2,0,1:T(8,128)(2,1)}) %reduce-scatter.18.cloned.1.call-update) | async-done | bytes 196624 | tf_op jit(solution)/shard_map/reduce_scatter | solution.py:546
  542.0 1.7 convert_element_type.115
  543.7 31.0 %reduce-scatter.16.cloned.1.call-done = bf16[256,1024]{1,0:T(8,128)(2,1)} async-done(((bf16[1024,1024]{1,0:T(8,128)(2,1)}), bf16[256,1024]{1,0:T(8,128)(2,1)}) %reduce-scatter.16.cloned.1.call-update) | async-done | bytes 524304 | tf_op jit(solution)/shard_map/reduce_scatter | solution.py:965
  574.7 2.1 convert_add_fusion
  (98 shorter events, 10.9 us)
Async XLA Ops:
  7.2 108.5 %all-gather.4.cloned.1.call-start = ((), (), s32[]{:S(2)}) async-start(), calls=%async_computation.7 | async-start | bytes 2621440 | tf_op jit(solution)/shard_map/all_gather | solution.py:865
  91.7 75.4 %reduce-scatter.12.cloned.1.call-start = ((), (), s32[]{:S(2)}) async-start(), calls=%async_computation.8 | async-start | bytes 2621440 | tf_op jit(solution)/shard_map/reduce_scatter | solution.py:546
  115.7 16.1 %copy-start.15 = (bf16[1024,1024]{1,0:T(8,128)(2,1)S(1)}, bf16[1024,1024]{1,0:T(8,128)(2,1)}, u32[]{:S(2)}) copy-start(bf16[1024,1024]{1,0:T(8,128)(2,1)} %get-tuple-element.165) | copy-start | bytes 6291460
  130.5 1.3 copy-start.16
  131.8 3.8 copy-start.9
  131.8 35.3 %copy-start = (f32[256,1024]{1,0:T(8,128)S(1)}, f32[256,1024]{1,0:T(8,128)}, u32[]{:S(2)}) copy-start(f32[256,1024]{1,0:T(8,128)} %get-tuple-element.162) | copy-start | bytes 3145732
  135.5 33.2 %copy-start.2 = (bf16[256,1024]{1,0:T(8,128)(2,1)S(1)}, bf16[256,1024]{1,0:T(8,128)(2,1)}, u32[]{:S(2)}) copy-start(bf16[256,1024]{1,0:T(8,128)(2,1)} %param.14) | copy-start | bytes 1572868
  135.5 59.1 %all-gather.6.cloned.1.call-start = ((), (), s32[]{:S(2)}) async-start(), calls=%async_computation.9 | async-start | bytes 2621440 | tf_op jit(solution)/shard_map/all_gather | solution.py:887
  171.8 68.5 %reduce-scatter.14.cloned.1.call-start = ((), (), s32[]{:S(2)}) async-start(), calls=%async_computation.10 | async-start | bytes 2621440 | tf_op jit(solution)/shard_map/reduce_scatter | solution.py:546
  194.6 10.4 %copy-start.14 = (bf16[1024,1024]{1,0:T(8,128)(2,1)S(1)}, bf16[1024,1024]{1,0:T(8,128)(2,1)}, u32[]{:S(2)}) copy-start(bf16[1024,1024]{1,0:T(8,128)(2,1)} %get-tuple-element.164) | copy-start | bytes 6291460
  203.6 1.3 copy-start.17
  205.0 3.8 copy-start.8
  208.7 58.4 %all-gather.8.cloned.1.call-start = ((), (), s32[]{:S(2)}) async-start(), calls=%async_computation.11 | async-start | bytes 2621440 | tf_op jit(solution)/shard_map/all_gather | solution.py:908
  244.4 94.1 %reduce-scatter.24.cloned.1.call-start = ((), (), s32[]{:S(2)}) async-start(), calls=%async_computation.16 | async-start | bytes 2359296
  251.7 157.6 %reduce-scatter.20.cloned.1.call-start = ((), (), s32[]{:S(2)}) async-start(), calls=%async_computation.14 | async-start | bytes 2359296 | tf_op jit(solution)/shard_map/reduce_scatter | solution.py:546
  258.0 3.8 copy-start.4
  258.0 4.4 copy-start.5
  258.1 215.5 %reduce-scatter.22.cloned.1.call-start = ((), (), s32[]{:S(2)}) async-start(), calls=%async_computation.15 | async-start | bytes 589824
  267.1 3.7 copy-start.3
  269.8 3.7 copy-start.7
  270.8 271.2 %reduce-scatter.18.cloned.1.call-start = ((), (), s32[]{:S(2)}) async-start(), calls=%async_computation.13 | async-start | bytes 1769472 | tf_op jit(solution)/shard_map/reduce_scatter | solution.py:546
  318.8 4.1 copy-start.6
  327.7 247.0 %reduce-scatter.16.cloned.1.call-start = ((), (), s32[]{:S(2)}) async-start(), calls=%async_computation.12 | async-start | bytes 2621440 | tf_op jit(solution)/shard_map/reduce_scatter | solution.py:965
  329.7 5.1 copy-start.13
  334.8 76.3 %copy-start.12 = (f32[1024]{0:T(1024)S(1)}, f32[1024]{0:T(1024)}, u32[]{:S(2)}) copy-start(f32[1024]{0:T(1024)} %get-tuple-element.227) | copy-start | bytes 12292
  334.8 76.5 %copy-start.10 = (f32[1024]{0:T(1024)S(1)}, f32[1024]{0:T(1024)}, u32[]{:S(2)}) copy-start(f32[1024]{0:T(1024)} %get-tuple-element.233) | copy-start | bytes 12292
  334.8 76.5 %copy-start.11 = (f32[1024]{0:T(1024)S(1)}, f32[1024]{0:T(1024)}, u32[]{:S(2)}) copy-start(f32[1024]{0:T(1024)} %get-tuple-element.261) | copy-start | bytes 12292
  334.8 239.9 %copy-start.1 = (f32[256,1024]{1,0:T(8,128)S(1)}, f32[256,1024]{1,0:T(8,128)}, u32[]{:S(2)}) copy-start(f32[256,1024]{1,0:T(8,128)} %get-tuple-element.266) | copy-start | bytes 3145732
Sparse Core Ops, SparseCore 0:
  91.8 23.8 all-gather.3
  135.6 31.4 reduce-scatter.11
  171.9 22.5 all-gather.5
  208.9 31.4 reduce-scatter.13
  244.5 22.5 all-gather.7
  270.5 67.9 reduce-scatter.23
  342.0 67.2 reduce-scatter.19
  412.6 60.8 reduce-scatter.21
  477.4 64.5 reduce-scatter.17
  544.4 30.2 reduce-scatter.15

commit v3 on v1

--- a/solution.py
+++ b/solution.py
@@ -1,13 +1,859 @@
+import functools
+import types
+
 import jax
 import jax.numpy as jnp
 from jax import lax
+from jax.experimental import pallas as pl
+from jax.experimental.pallas import tpu as pltpu
 from jax.sharding import PartitionSpec as P
 
 HEAD = 64
-
-
 EPSILON = 1e-05
 NEGATIVE = -1e30
+MESH = pl.DeviceIdType.MESH
+LINES = 4
+CORE, ACROSS, FAR = 1, 2, 3
+HALVES = 2
+CHUNK = 16
+VMEM_BYTES = 60 << 20
+
+
+def remote(src, dst, send_sem, recv_sem, target):
+    return pltpu.make_async_remote_copy(
+        src_ref=src,
+        dst_ref=dst,
+        send_sem=send_sem,
+        recv_sem=recv_sem,
+        device_id=target,
+        device_id_type=MESH,
+    )
+
+
+def position():
+    return lax.axis_index("dp"), lax.axis_index("tensor")
+
+
+def greet():
+    dp, tensor = position()
+    barrier = pltpu.get_barrier_semaphore()
+    others = [(dp ^ step, tensor) for step in (1, 2, 4, 6)]
+    others += [(dp, tensor ^ step) for step in (CORE, ACROSS)]
+    for target in others:
+        pl.semaphore_signal(barrier, inc=1, device_id=target, device_id_type=MESH)
+    pl.semaphore_wait(barrier, len(others))
+
+
+def row_piece(ref, index, size):
+    return ref.at[pl.ds(pl.multiple_of(index * size, size), size), :]
+
+
+def column_piece(ref, index, size):
+    return ref.at[:, pl.ds(pl.multiple_of(index * size, size), size)]
+
+
+class LineGather:
+    def __init__(self, own, full, piece, send_sem, recv_sem, local_sem):
+        self.own, self.full, self.piece = own, full, piece
+        self.send_sem, self.recv_sem, self.local_sem = send_sem, recv_sem, local_sem
+        self.dp, self.tensor = position()
+        self.line, self.side = self.dp // 2, self.dp % 2
+        self.targets = (
+            (self.dp + 2, self.tensor),
+            (self.dp - 2, self.tensor),
+            (self.dp ^ 1, self.tensor),
+        )
+
+    def copy(self, index, way, src=None):
+        view = self.piece(self.full, index)
+        return remote(
+            view if src is None else src,
+            view,
+            self.send_sem.at[way * LINES + index // 2],
+            self.recv_sem.at[index],
+            self.targets[way],
+        )
+
+    def local(self):
+        return pltpu.make_async_copy(self.own, self.piece(self.full, self.dp), self.local_sem)
+
+    def start(self):
+        self.local().start()
+
+        @pl.when(self.line < LINES - 1)
+        def _():
+            self.copy(self.dp, 0, self.own).start()
+
+        @pl.when(self.line > 0)
+        def _():
+            self.copy(self.dp, 1, self.own).start()
+
+        self.copy(self.dp, 2, self.own).start()
+
+    def step(self, distance):
+        @pl.when(self.line >= distance)
+        def _():
+            index = self.dp - 2 * distance
+            self.copy(index, 0).wait_recv()
+
+            @pl.when(self.line < LINES - 1)
+            def _():
+                self.copy(index, 0).start()
+
+            self.copy(index, 2).start()
+
+        @pl.when(self.line + distance < LINES)
+        def _():
+            index = self.dp + 2 * distance
+            self.copy(index, 1).wait_recv()
+
+            @pl.when(self.line > 0)
+            def _():
+                self.copy(index, 1).start()
+
+            self.copy(index, 2).start()
+
+    def arrive(self):
+        self.local().wait()
+        for line in range(LINES):
+            self.copy(2 * line + 1 - self.side, 2).wait_recv()
+
+    def finish(self):
+        for line in range(LINES):
+            index = 2 * line + self.side
+            self.copy(index, 2).wait_send()
+
+            @pl.when((self.line < LINES - 1) & (line <= self.line))
+            def _():
+                self.copy(index, 0).wait_send()
+
+            @pl.when((self.line > 0) & (line >= self.line))
+            def _():
+                self.copy(index, 1).wait_send()
+
+
+class RowGather:
+    def __init__(self, full, rows, send_sem, recv_sem):
+        self.full, self.rows = full, rows
+        self.send_sem, self.recv_sem = send_sem, recv_sem
+        self.dp, self.tensor = position()
+
+    def view(self, rank, half=None):
+        if half is None:
+            return row_piece(self.full, rank, self.rows)
+        return row_piece(self.full, rank * HALVES + half, self.rows // HALVES)
+
+    def near(self, rank):
+        view = self.view(rank)
+        target = (self.dp, self.tensor ^ CORE)
+        return remote(view, view, self.send_sem.at[0], self.recv_sem.at[0], target)
+
+    def across(self, rank, half):
+        view, slot = self.view(rank, half), 1 + half
+        target = (self.dp, self.tensor ^ ACROSS)
+        return remote(view, view, self.send_sem.at[slot], self.recv_sem.at[slot], target)
+
+    def far(self, rank, half):
+        view, slot = self.view(rank, half), 1 + HALVES + half
+        target = (self.dp, self.tensor ^ CORE)
+        return remote(view, view, self.send_sem.at[slot], self.recv_sem.at[slot], target)
+
+    def start(self):
+        for half in range(HALVES):
+            self.across(self.tensor, half).start()
+        self.near(self.tensor).start()
+
+    def wait_near(self):
+        self.near(self.tensor ^ CORE).wait_recv()
+
+    def wait_across(self, half):
+        self.across(self.tensor ^ ACROSS, half).wait_recv()
+        self.far(self.tensor ^ ACROSS, half).start()
+
+    def wait_far(self, half):
+        self.far(self.tensor ^ FAR, half).wait_recv()
+
+    def finish(self):
+        self.near(self.tensor).wait_send()
+        for half in range(HALVES):
+            self.across(self.tensor, half).wait_send()
+            self.far(self.tensor ^ ACROSS, half).wait_send()
+
+
+class RowScatter:
+    def __init__(self, near_out, near_in, across_out, across_in, send_sem, recv_sem):
+        self.near_out, self.near_in = near_out, near_in
+        self.across_out, self.across_in = across_out, across_in
+        self.send_sem, self.recv_sem = send_sem, recv_sem
+        self.dp, self.tensor = position()
+
+    def near(self, slot):
+        return remote(
+            self.near_out.at[slot],
+            self.near_in.at[slot],
+            self.send_sem.at[slot],
+            self.recv_sem.at[slot],
+            (self.dp, self.tensor ^ CORE),
+        )
+
+    def across(self, half):
+        rows = self.across_in.shape[0] // HALVES
+        return remote(
+            row_piece(self.across_out, half, rows),
+            row_piece(self.across_in, half, rows),
+            self.send_sem.at[2 * HALVES + half],
+            self.recv_sem.at[2 * HALVES + half],
+            (self.dp, self.tensor ^ ACROSS),
+        )
+
+    def give_far(self, half, partial):
+        self.near_out[half] = partial.astype(jnp.bfloat16)
+        self.near(half).start()
+
+    def give_across(self, half, partial):
+        self.near(half).wait_recv()
+        rows = partial.shape[0]
+        total = partial + self.near_in[half].astype(jnp.float32)
+        self.across_out[half * rows : (half + 1) * rows, :] = total.astype(jnp.bfloat16)
+        self.across(half).start()
+
+    def give_near(self, half, partial):
+        self.near_out[HALVES + half] = partial.astype(jnp.bfloat16)
+        self.near(HALVES + half).start()
+
+    def take(self, half, partial):
+        self.near(HALVES + half).wait_recv()
+        rows = partial.shape[0]
+        total = partial + self.near_in[HALVES + half].astype(jnp.float32)
+        self.across(half).wait_recv()
+        return total + self.across_in[half * rows : (half + 1) * rows, :].astype(jnp.float32)
+
+    def finish(self):
+        for slot in range(2 * HALVES):
+            self.near(slot).wait_send()
+        for half in range(HALVES):
+            self.across(half).wait_send()
+
+
+def dot(left, right):
+    return jnp.dot(left, right, preferred_element_type=jnp.float32)
+
+
+def dot_nt(left, right):
+    return lax.dot_general(left, right, (((1,), (1,)), ((), ())), preferred_element_type=jnp.float32)
+
+
+def dot_tn(left, right):
+    return lax.dot_general(left, right, (((0,), (0,)), ((), ())), preferred_element_type=jnp.float32)
+
+
+def normalize(rows):
+    centred = rows - jnp.mean(rows, axis=-1, keepdims=True)
+    inverse = lax.rsqrt(jnp.mean(centred * centred, axis=-1, keepdims=True) + EPSILON)
+    return centred * inverse, inverse
+
+
+def norm_back(grad, normed, inverse):
+    average = jnp.mean(grad, axis=-1, keepdims=True)
+    along = jnp.mean(grad * normed, axis=-1, keepdims=True)
+    return inverse * (grad - average - normed * along)
+
+
+class LineScatter:
+    def __init__(self, partial, piece, side_in, line_in, send_sem, recv_sem):
+        self.partial, self.piece, self.side_in, self.line_in = partial, piece, side_in, line_in
+        self.send_sem, self.recv_sem = send_sem, recv_sem
+        self.dp, self.tensor = position()
+
+    def view(self, step):
+        return self.piece(self.partial, self.dp ^ (2 * step))
+
+    def across(self, step):
+        return remote(
+            self.piece(self.partial, self.dp ^ (2 * step) ^ 1),
+            self.side_in.at[step],
+            self.send_sem.at[step],
+            self.recv_sem.at[step],
+            (self.dp ^ 1, self.tensor),
+        )
+
+    def along(self, step):
+        return remote(
+            self.view(step),
+            self.line_in.at[step - 1],
+            self.send_sem.at[LINES + step],
+            self.recv_sem.at[LINES + step],
+            (self.dp ^ (2 * step), self.tensor),
+        )
+
+    def start(self):
+        for step in reversed(range(LINES)):
+            self.across(step).start()
+
+    def total(self, step):
+        self.across(step).wait_recv()
+        return self.view(step)[...].astype(jnp.float32) + self.side_in[step].astype(jnp.float32)
+
+    def relay(self, step):
+        self.view(step)[...] = self.total(step).astype(jnp.bfloat16)
+        self.along(step).start()
+
+    def finish(self, result):
+        total = self.total(0)
+        for step in range(1, LINES):
+            self.along(step).wait_recv()
+            total = total + self.line_in[step - 1].astype(jnp.float32)
+        result[...] = total
+        for step in range(LINES):
+            self.across(step).wait_send()
+        for step in range(1, LINES):
+            self.along(step).wait_send()
+
+
+class Total:
+    def __init__(self, held, arrived, send_sem, recv_sem):
+        self.held, self.arrived, self.send_sem, self.recv_sem = held, arrived, send_sem, recv_sem
+        dp, tensor = position()
+        self.targets = (
+            (dp, tensor ^ CORE),
+            (dp ^ 1, tensor),
+            (dp ^ 2, tensor),
+            (dp ^ 4, tensor),
+            (dp, tensor ^ ACROSS),
+        )
+
+    def copy(self, step):
+        return remote(
+            self.held.at[step],
+            self.arrived.at[step],
+            self.send_sem.at[step],
+            self.recv_sem.at[step],
+            self.targets[step],
+        )
+
+    def start(self):
+        self.copy(0).start()
+
+    def step(self, step):
+        self.copy(step).wait_recv()
+        self.held[step + 1] = self.held[step] + self.arrived[step]
+        if step + 1 < len(self.targets):
+            self.copy(step + 1).start()
+
+    def finish(self):
+        for step in range(len(self.targets)):
+            self.copy(step).wait_send()
+
+
+def layer_kernel(names, rows, *refs):
+    r = types.SimpleNamespace(**dict(zip(names, refs)))
+    dp, tensor = position()
+    bf16, f32 = jnp.bfloat16, jnp.float32
+    half_rows = rows // HALVES
+    local = r.queries.shape[1]
+    piece = r.triple_own.shape[0]
+    pairs = local // (2 * HEAD)
+    near, across, far = tensor ^ CORE, tensor ^ ACROSS, tensor ^ FAR
+
+    def of_rows(ref, index):
+        return row_piece(ref, index, piece)
+
+    def of_columns(ref, index):
+        return column_piece(ref, index, piece)
+
+    def block(rank, size=rows):
+        return pl.ds(pl.multiple_of(rank * size, size), size)
+
+    def split(partial):
+        return [partial[half * half_rows : (half + 1) * half_rows] for half in range(HALVES)]
+
+    def part_of(half):
+        return slice(half * half_rows, (half + 1) * half_rows)
+
+    lines = [
+        LineGather(own, full, view, r.line_send.at[at], r.line_recv.at[at], r.line_local.at[at])
+        for at, (own, full, view) in enumerate(
+            (
+                (r.triple_own, r.triple, of_rows),
+                (r.output_own, r.output, of_columns),
+                (r.up_own, r.up, of_rows),
+                (r.down_own, r.down, of_columns),
+            )
+        )
+    ]
+    triple_line, output_line, up_line, down_line = lines
+    sums = [
+        LineScatter(partial, view, side, along, r.part_send.at[at], r.part_recv.at[at])
+        for at, (partial, view, side, along) in enumerate(
+            (
+                (r.grad_project, of_rows, r.project_side, r.project_line),
+                (r.grad_output, of_columns, r.output_side, r.output_line),
+                (r.grad_up, of_rows, r.up_side, r.up_line),
+                (r.grad_down, of_columns, r.down_side, r.down_line),
+            )
+        )
+    ]
+    project_sum, output_sum, up_sum, down_sum = sums
+    gathers = [
+        RowGather(full, rows, r.row_send.at[at], r.row_recv.at[at])
+        for at, full in enumerate((r.gathered, r.first_all, r.second_all, r.branch_all))
+    ]
+    scatters = [
+        RowScatter(*buffers, r.sum_send.at[at], r.sum_recv.at[at])
+        for at, buffers in enumerate(
+            (
+                (r.near_out_a, r.near_in_a, r.across_out_a, r.across_in_a),
+                (r.near_out_b, r.near_in_b, r.across_out_b, r.across_in_b),
+            )
+            * 2
+        )
+    ]
+    total = Total(r.held_totals, r.arrived_totals, r.total_send, r.total_recv)
+
+    def scatter_blocks(scatter, product):
+        for half, partial in enumerate(split(product(far))):
+            scatter.give_far(half, partial)
+        for half, partial in enumerate(split(product(across))):
+            scatter.give_across(half, partial)
+        for half, partial in enumerate(split(product(near))):
+            scatter.give_near(half, partial)
+
+    greet()
+    place = pltpu.make_async_copy(r.tokens, gathers[0].view(tensor), r.place_sem)
+    place.start()
+    triple_line.start()
+    place.wait()
+    gathers[0].start()
+    triple_line.step(1)
+    triple_line.step(2)
+    gathers[0].wait_near()
+    for half in range(HALVES):
+        gathers[0].wait_across(half)
+    triple_line.step(3)
+    output_line.start()
+    up_line.start()
+    for half in range(HALVES):
+        gathers[0].wait_far(half)
+    triple_line.arrive()
+    columns = pl.ds(pl.multiple_of(tensor * local, local), local)
+    query_bias = r.bias_rows[0:1, columns]
+    value_bias = r.bias_rows[1:2, columns]
+
+    @pl.loop(0, 4)
+    def _(index):
+        here = block(index)
+        left = r.gathered[here, :]
+        query = (dot(left, r.triple[:, :local]) + query_bias).astype(bf16)
+        r.queries[here, :] = query * bf16(HEAD**-0.5)
+        key = dot(left, r.triple[:, local : 2 * local])
+        r.key_rows[here, :] = key.astype(bf16)
+        r.key_turned[:, here] = key.T.astype(bf16)
+        value = dot(left, r.triple[:, 2 * local :]) + value_bias
+        r.value_rows[here, :] = value.astype(bf16)
+        r.value_turned[:, here] = value.T.astype(bf16)
+
+    output_line.step(1)
+    up_line.step(1)
+    down_line.start()
+
+    def head_rows(head):
+        return pl.ds(pl.multiple_of(head * HEAD, HEAD), HEAD)
+
+    def attend(rank):
+        here = block(rank)
+
+        @pl.loop(0, pairs)
+        def _(pair):
+            lanes = block(pair, 2 * HEAD)
+            query = r.queries[here, lanes]
+            keys = r.key_rows[:, lanes]
+            same = r.segment_column[...] == r.segment_row[:, here]
+            lane = lax.broadcasted_iota(jnp.int32, query.shape, 1)
+            outs = []
+            for side in range(2):
+                scores = dot_nt(keys, jnp.where(lane // HEAD == side, query, bf16(0)))
+                scores = jnp.where(same, scores, NEGATIVE)
+                top = jnp.max(scores, axis=0, keepdims=True)
+                exponent = jnp.exp(scores - top)
+                mass = jnp.sum(exponent, axis=0, keepdims=True)
+                weights = (exponent * (1.0 / mass)).astype(bf16)
+                head = pair * 2 + side
+                outs.append(dot(r.value_turned[head_rows(head), :], weights))
+                r.log_totals[pl.ds(head, 1), here] = top + jnp.log(mass)
+            r.mixed[here, lanes] = jnp.concatenate(outs, axis=0).T.astype(bf16)
+
+        return r.mixed[here, :]
+
+    mixed_far = attend(far)
+    output_line.step(2)
+    output_line.step(3)
+    up_line.step(2)
+    output_line.arrive()
+    for half, partial in enumerate(split(dot(mixed_far, r.output[...]))):
+        scatters[0].give_far(half, partial)
+    for half, partial in enumerate(split(dot(attend(across), r.output[...]))):
+        scatters[0].give_across(half, partial)
+    up_line.step(3)
+    down_line.step(1)
+    for half, partial in enumerate(split(dot(attend(near), r.output[...]))):
+        scatters[0].give_near(half, partial)
+    down_line.step(2)
+    for half, partial in enumerate(split(dot(attend(tensor), r.output[...]))):
+        part = part_of(half)
+        own_rows = r.gathered[block(tensor * HALVES + half, half_rows), :].astype(f32)
+        normed, inverse = normalize(own_rows + scatters[0].take(half, partial) + r.bias_rows[2:3, :])
+        r.normed_one[part, :] = normed
+        r.inverse_one[part, :] = inverse
+        first = normed * r.norm_gains[0:1, :] + r.bias_rows[3:4, :]
+        r.first_all[block(tensor * HALVES + half, half_rows), :] = first.astype(bf16)
+    scatters[0].finish()
+
+    gathers[1].start()
+    down_line.step(3)
+    r.sums[...] = jnp.zeros_like(r.sums)
+
+    def chunks(size, start, body):
+        @pl.loop(0, size // CHUNK)
+        def _(chunk):
+            offset = chunk * CHUNK
+            body(
+                pl.ds(pl.multiple_of(offset, CHUNK), CHUNK),
+                pl.ds(pl.multiple_of(start + offset, CHUNK), CHUNK),
+            )
+
+    def extent(rank, half):
+        size = rows if half is None else half_rows
+        start = rank * rows + (0 if half is None else half * half_rows)
+        return start, size, pl.ds(pl.multiple_of(start, size), size)
+
+    def up_part(rank, half=None):
+        start, size, here = extent(rank, half)
+        r.upper[:size, :] = dot(r.first_all[here, :], r.up[...]) + r.hidden_bias[...]
+
+        def body(part, into):
+            value = r.upper[part, :]
+            share = 0.5 + 0.5 * lax.erf(value * (0.5**0.5))
+            r.hidden[into, :] = (value * share).astype(bf16)
+            bell = jnp.exp(value * value * -0.5) * (2 * jnp.pi) ** -0.5
+            r.slope[into, :] = share + value * bell
+
+        chunks(size, start, body)
+
+    def down_part(rank, half=None):
+        return dot(r.hidden[extent(rank, half)[2], :], r.down[...])
+
+    def back_part(rank, half=None):
+        start, size, here = extent(rank, half)
+        r.upper[:size, :] = dot_nt(r.second_all[here, :], r.down[...])
+
+        def body(part, into):
+            low = (r.upper[part, :] * r.slope[into, :]).astype(bf16)
+            r.upper_low[into, :] = low
+            r.sums[6:7, :] += jnp.sum(low.astype(f32), axis=0, keepdims=True)
+
+        chunks(size, start, body)
+        return dot_nt(r.upper_low[here, :], r.up[...])
+
+    up_line.arrive()
+    up_part(tensor)
+    gathers[1].wait_near()
+    up_part(near)
+    for half in range(HALVES):
+        gathers[1].wait_across(half)
+        up_part(across, half)
+        gathers[1].wait_far(half)
+        up_part(far, half)
+    down_line.arrive()
+    scatter_blocks(scatters[1], down_part)
+    r.kept[...] = down_part(tensor)
+
+    def add_to(row, value):
+        r.sums[row : row + 1, :] += jnp.sum(value, axis=0, keepdims=True)
+
+    def second_norm(_, here):
+        first = r.normed_one[here, :] * r.norm_gains[0:1, :] + r.bias_rows[3:4, :]
+        normed, inverse = normalize(first + r.kept[here, :] + r.bias_rows[4:5, :])
+        shifted = normed * r.norm_gains[1:2, :] + r.bias_rows[5:6, :]
+        r.layer_out[here, :] = shifted.astype(bf16)
+        grad = r.cotangent[here, :].astype(f32)
+        add_to(5, grad * normed)
+        add_to(3, grad)
+        grad = norm_back(grad * r.norm_gains[1:2, :], normed, inverse)
+        r.grad_rows[here, :] = grad
+        low = grad.astype(bf16)
+        add_to(2, low.astype(f32))
+        r.second_all[pl.ds(pl.multiple_of(tensor * rows + here.start, CHUNK), CHUNK), :] = low
+
+    for half in range(HALVES):
+        part = part_of(half)
+        r.kept[part, :] = scatters[1].take(half, r.kept[part, :])
+        chunks(half_rows, half * half_rows, second_norm)
+    scatters[1].finish()
+
+    gathers[2].start()
+    r.kept[...] = back_part(tensor)
+    gathers[2].wait_near()
+    for half, partial in enumerate(split(back_part(near))):
+        scatters[2].give_near(half, partial)
+    for half in range(HALVES):
+        gathers[2].wait_across(half)
+        r.held[...] = back_part(across, half)
+        gathers[2].wait_far(half)
+        scatters[2].give_far(half, back_part(far, half))
+        scatters[2].give_across(half, r.held[...])
+
+    def weight_grad(left, right, result):
+        @pl.loop(0, left.shape[1] // rows)
+        def _(index):
+            lanes = block(index)
+            result[lanes, :] = dot_tn(left[:, lanes], right[...]).astype(bf16)
+
+    weight_grad(r.hidden, r.second_all, r.grad_down)
+    down_sum.start()
+    weight_grad(r.first_all, r.upper_low, r.grad_up)
+    up_sum.start()
+
+    def first_norm(_, here):
+        grad = r.grad_rows[here, :] + r.kept[here, :]
+        normed = r.normed_one[here, :]
+        add_to(4, grad * normed)
+        add_to(1, grad)
+        grad = norm_back(grad * r.norm_gains[0:1, :], normed, r.inverse_one[here, :])
+        r.grad_rows[here, :] = grad
+        low = grad.astype(bf16)
+        add_to(0, low.astype(f32))
+        r.branch_all[pl.ds(pl.multiple_of(tensor * rows + here.start, CHUNK), CHUNK), :] = low
+
+    for half in range(HALVES):
+        part = part_of(half)
+        r.kept[part, :] = scatters[2].take(half, r.kept[part, :])
+        chunks(half_rows, half * half_rows, first_norm)
+    scatters[2].finish()
+
+    gathers[3].start()
+    grad_keys, grad_values = r.slope.at[:, :local], r.slope.at[:, local : 2 * local]
+    r.slope[:, : 2 * local] = jnp.zeros((r.slope.shape[0], 2 * local), f32)
+
+    def attend_back(rank):
+        here = block(rank)
+        r.mixed_low[...] = dot_nt(r.branch_all[here, :], r.output[...]).astype(bf16)
+
+        @pl.loop(0, pairs)
+        def _(pair):
+            lanes = block(pair, 2 * HEAD)
+            query = r.queries[here, lanes]
+            grad = r.mixed_low[:, lanes]
+            keys = r.key_rows[:, lanes]
+            values = r.value_rows[:, lanes]
+            same = r.segment_column[...] == r.segment_row[:, here]
+            lane = lax.broadcasted_iota(jnp.int32, query.shape, 1)
+            outs = []
+            for side in range(2):
+                mine = lane // HEAD == side
+                head = pair * 2 + side
+                query_here = jnp.where(mine, query, bf16(0))
+                grad_here = jnp.where(mine, grad, bf16(0))
+                scores = jnp.where(same, dot_nt(keys, query_here), NEGATIVE)
+                weights = jnp.exp(scores - r.log_totals[pl.ds(head, 1), here])
+                grad_weights = dot_nt(values, grad_here)
+                along = jnp.sum(weights * grad_weights, axis=0, keepdims=True)
+                grad_scores = (weights * (grad_weights - along)).astype(bf16)
+                grad_keys[:, lanes] += dot(grad_scores, query_here)
+                grad_values[:, lanes] += dot(weights.astype(bf16), grad_here)
+                outs.append(dot(r.key_turned[head_rows(head), :], grad_scores))
+            grad_query = jnp.concatenate(outs, axis=0).T * HEAD**-0.5
+            r.projected_low[here, lanes] = grad_query.astype(bf16)
+
+    attend_back(tensor)
+    down_sum.relay(3)
+    gathers[3].wait_near()
+    attend_back(near)
+    down_sum.relay(2)
+    for half in range(HALVES):
+        gathers[3].wait_across(half)
+    attend_back(across)
+    down_sum.relay(1)
+    for half in range(HALVES):
+        gathers[3].wait_far(half)
+    r.grad_output[...] = dot_tn(r.mixed[...], r.branch_all[...]).astype(bf16)
+    output_sum.start()
+    attend_back(far)
+    r.projected_low[:, local : 2 * local] = grad_keys[...].astype(bf16)
+    r.projected_low[:, 2 * local :] = grad_values[...].astype(bf16)
+    weight_grad(r.gathered, r.projected_low, r.grad_project)
+    project_sum.start()
+    r.held_totals[0] = jnp.zeros(r.held_totals.shape[1:], f32)
+    r.held_totals[0, 2:8, :] = r.sums[0:6, :]
+    r.held_totals[0, pl.ds(8 + tensor, 1), :] = r.sums[6:7, :]
+    for row, at in ((0, 0), (1, 2)):
+        low = r.projected_low[:, at * local : (at + 1) * local].astype(f32)
+        r.held_totals[0, row : row + 1, columns] = jnp.sum(low, axis=0, keepdims=True)
+    total.start()
+    up_sum.relay(3)
+
+    def token_part(rank):
+        return dot_nt(r.projected_low[block(rank), :], r.triple[...])
+
+    scatter_blocks(scatters[3], token_part)
+    total.step(0)
+    up_sum.relay(2)
+    mine = split(token_part(tensor))
+    total.step(1)
+    up_sum.relay(1)
+    down_sum.finish(r.down_out)
+    total.step(2)
+    for half, partial in enumerate(mine):
+        part = part_of(half)
+        r.grad_tokens[part, :] = scatters[3].take(half, partial) + r.grad_rows[part, :]
+    for step in (3, 2, 1):
+        output_sum.relay(step)
+    total.step(3)
+    up_sum.finish(r.up_out)
+    for step in (3, 2, 1):
+        project_sum.relay(step)
+    total.step(4)
+    r.bias_out[...] = r.held_totals[5, 0:6, :]
+    r.gains_out[...] = r.held_totals[5, 6:8, :]
+    r.hidden_out[...] = r.held_totals[5, 8:12, :]
+    output_sum.finish(r.output_out)
+    project_sum.finish(r.project_out)
+    scatters[3].finish()
+    for each in gathers + lines + [total]:
+        each.finish()
+
+
+def per_device_kernel(
+    tokens,
+    segments,
+    cotangent,
+    project_weight,
+    output_weight,
+    up_weight,
+    down_weight,
+    norm_gains,
+    bias_rows,
+    hidden_bias,
+):
+    rows, width = tokens.shape
+    length = segments.shape[1]
+    local_hidden = up_weight.shape[1]
+    local = output_weight.shape[0]
+    piece = project_weight.shape[0]
+    bf16, f32 = jnp.bfloat16, jnp.float32
+    local_bias = lax.dynamic_slice_in_dim(
+        hidden_bias, lax.axis_index("tensor") * local_hidden, local_hidden, 0
+    )
+    remote_inputs = dict(
+        tokens=tokens,
+        triple_own=project_weight.reshape(piece, -1),
+        output_own=output_weight,
+        up_own=up_weight,
+        down_own=down_weight,
+    )
+    inputs = dict(
+        segment_column=segments.reshape(length, 1),
+        segment_row=segments.reshape(1, length),
+        cotangent=cotangent,
+        norm_gains=norm_gains,
+        bias_rows=bias_rows,
+        hidden_bias=local_bias.reshape(1, -1),
+    )
+    shapes = dict(
+        project=(piece, 3 * local),
+        output=(local, piece),
+        up=(piece, local_hidden),
+        down=(local_hidden, piece),
+    )
+    outputs = dict(layer_out=((rows, width), bf16), grad_tokens=((rows, width), f32))
+    outputs |= {name + "_out": (shape, f32) for name, shape in shapes.items()}
+    outputs |= dict(
+        gains_out=((2, width), f32),
+        bias_out=((6, width), f32),
+        hidden_out=((4, width), f32),
+    )
+    scratch = dict(
+        gathered=((length, width), bf16),
+        triple=((width, 3 * local), bf16),
+        output=((local, width), bf16),
+        up=((width, local_hidden), bf16),
+        down=((local_hidden, width), bf16),
+        queries=((length, local), bf16),
+        key_rows=((length, local), bf16),
+        value_rows=((length, local), bf16),
+        key_turned=((local, length), bf16),
+        value_turned=((local, length), bf16),
+        mixed=((length, local), bf16),
+        log_totals=((local // HEAD, length), f32),
+        normed_one=((rows, width), f32),
+        inverse_one=((rows, 1), f32),
+        first_all=((length, width), bf16),
+        hidden=((length, local_hidden), bf16),
+        slope=((length, local_hidden), f32),
+        second_all=((length, width), bf16),
+        upper_low=((length, local_hidden), bf16),
+        upper=((rows, local_hidden), f32),
+        kept=((rows, width), f32),
+        held=((rows // HALVES, width), f32),
+        grad_rows=((rows, width), f32),
+        sums=((8, width), f32),
+        branch_all=((length, width), bf16),
+        mixed_low=((rows, local), bf16),
+        projected_low=((length, 3 * local), bf16),
+        grad_project=((width, 3 * local), bf16),
+        grad_output=((local, width), bf16),
+        grad_up=((width, local_hidden), bf16),
+        grad_down=((local_hidden, width), bf16),
+        held_totals=((6, 16, width), f32),
+        arrived_totals=((5, 16, width), f32),
+    )
+    for name, shape in shapes.items():
+        scratch[name + "_side"] = ((LINES,) + shape, bf16)
+        scratch[name + "_line"] = ((LINES - 1,) + shape, bf16)
+    for at in "ab":
+        for name in ("near_out_", "near_in_"):
+            scratch[name + at] = ((2 * HALVES, rows // HALVES, width), bf16)
+        for name in ("across_out_", "across_in_"):
+            scratch[name + at] = ((rows, width), bf16)
+    semaphores = dict(
+        line_send=(4, 3 * LINES),
+        line_recv=(4, 2 * LINES),
+        line_local=(4,),
+        part_send=(4, 2 * LINES),
+        part_recv=(4, 2 * LINES),
+        row_send=(4, 1 + 2 * HALVES),
+        row_recv=(4, 1 + 2 * HALVES),
+        sum_send=(4, 3 * HALVES),
+        sum_recv=(4, 3 * HALVES),
+        total_send=(5,),
+        total_recv=(5,),
+        place_sem=(),
+    )
+    names = [*remote_inputs, *inputs, *outputs, *scratch, *semaphores]
+    vmem, hbm = pl.BlockSpec(memory_space=pltpu.VMEM), pl.BlockSpec(memory_space=pltpu.HBM)
+    results = pl.pallas_call(
+        functools.partial(layer_kernel, names, rows),
+        out_shape=[jax.ShapeDtypeStruct(*leaf) for leaf in outputs.values()],
+        in_specs=[hbm] * len(remote_inputs) + [vmem] * len(inputs),
+        out_specs=[vmem] * len(outputs),
+        scratch_shapes=[pltpu.VMEM(*leaf) for leaf in scratch.values()]
+        + [pltpu.SemaphoreType.DMA(shape) for shape in semaphores.values()],
+        compiler_params=pltpu.CompilerParams(
+            collective_id=0, has_side_effects=True, vmem_limit_bytes=VMEM_BYTES
+        ),
+        name="layer",
+    )(*remote_inputs.values(), *inputs.values())
+    result = dict(zip(outputs, results))
+    return (
+        result["layer_out"],
+        result["grad_tokens"],
+        result["project_out"].reshape(project_weight.shape),
+        result["output_out"],
+        result["up_out"],
+        result["down_out"],
+        result["gains_out"],
+        result["bias_out"],
+        result["hidden_out"].reshape(-1),
+    )
 
 
 def gelu_exact(values):
@@ -23,7 +869,7 @@
     return (normed * gain + shift, (normed, inverse))
 
 
-def norm_back(grad_rows, saved, gain):
+def norm_back_saved(grad_rows, saved, gain):
     normed, inverse = saved
     grad_gain = jnp.sum(grad_rows * normed, axis=0)
     grad_shift = jnp.sum(grad_rows, axis=0)
@@ -154,7 +1000,7 @@
     back_triple = reloaded[0].reshape(model_width, 3 * local_width)
     back_output, back_upward, back_downward = (reloaded[1], reloaded[2], reloaded[3])
     grad_layer = cotangent.astype(jnp.float32)
-    grad_second_in, grad_gain_two, grad_shift_two = norm_back(
+    grad_second_in, grad_gain_two, grad_shift_two = norm_back_saved(
         grad_layer, second_saved, norm_gains[1]
     )
     grad_second = grad_second_in.astype(jnp.bfloat16)
@@ -177,7 +1023,7 @@
         )
         + grad_second_in
     )
-    grad_first_in, grad_gain_one, grad_shift_one = norm_back(grad_first, first_saved, norm_gains[0])
+    grad_first_in, grad_gain_one, grad_shift_one = norm_back_saved(grad_first, first_saved, norm_gains[0])
     grad_branch = grad_first_in.astype(jnp.bfloat16)
     grad_branch_all = lax.all_gather(grad_branch, "tensor", axis=0, tiled=True)
     grad_output_part = jnp.einsum(
@@ -292,6 +1138,7 @@
 
 
 def solution(mesh):
+    fits = mesh.shape["dp"] == 2 * LINES and mesh.shape["tensor"] == 4
     placed = (
         P(("dp", "tensor"), None),
         P("dp", None),
@@ -305,7 +1152,7 @@
         P(),
     )
     return jax.shard_map(
-        per_device,
+        per_device_kernel if fits else per_device,
         mesh=mesh,
         in_specs=placed,
         out_specs=(

time: 735 us -> 240 us (0.33); the launches traced: 727 us -> 240 us
  waiting for transfers between devices: 463 us -> 0 us
  Pallas kernels: 0 us -> 226 us
  matrix products: 91.6 us -> 0 us
  blocking collectives: 72.2 us -> 0 us
  other arithmetic: 37.3 us -> 0 us
  local copies, waits for them, and re-layouts: 30.4 us -> 13.4 us
  loops' own time: 16.2 us -> 0 us
  between operations: 14.6 us -> 0.7 us
    pallas_call x0 -> x1, Pallas kernels: none -> 226 us  [per_device_kernel(): pl.pallas_call(functools.partial(layer_kernel, names, rows), out_shape=[j...]
    reduce_scatter x5 -> x0, waiting for transfers between devices: 192 us -> none  [the longest x4 161 us: scatter_sum(): lax.psum_scatter(partial_sum.astype(jnp.bfloat16), axis_name, scatter_dim...]
    all_gather x7 -> x0, waiting for transfers between devices: 175 us -> none  [the longest x1 45.1 us: per_device(): lax.all_gather(up_weight, 'dp', axis=0, tiled=True)]
    unnamed x18 -> x0, waiting for transfers between devices: 96.8 us -> none
    dot_general x26 -> x0, matrix products: 91.6 us -> none  [the longest x1 14.9 us: per_device(): jnp.dot(first_gathered, upward_full, preferred_element_type=jnp.float32)]
    psum x1 -> x0, blocking collectives: 41 us -> none  [per_device(): lax.psum((gain_terms, bias_terms, hidden_terms), ('dp', 'tensor'))]
    all_gather x1 -> x0, blocking collectives: 31.2 us -> none  [per_device(): lax.all_gather(output_weight, 'dp', axis=1, tiled=True)]
    reduce_sum x14 -> x0, other arithmetic: 21.7 us -> none  [the longest x2 4.67 us: forward_block(): row_sum = jnp.sum(exponent, axis=-1, keepdims=True)]
  transfers between devices with their start and end apart: 15 -> 0, of which waited for: 15 -> 0; matrix products, arithmetic and copies ran while one was open for 13% -> 0% of each run, Pallas kernels for 0% -> 0%
where the time goes in v3:
time: 240 us
  Pallas kernels  226 us (94%)
  local copies, waits for them, and re-layouts  13.4 us (6%)
    pallas_call x1, Pallas kernels, per_device_kernel(): pl.pallas_call(functools.partial(layer_kernel, names, rows), out_shape=[j...  226 us
    unnamed x28, local copies, waits for them, and re-layouts  9.02 us

profile of v3, /device:TPU:0, one launch (start us, length us, event | category | flops | bytes accessed | tf_op | source)
XLA Modules:
  0.0 239.9 jit_solution(8238734120876596676)
XLA Ops:
  0.6 1.3 dynamic_slice.3
  1.9 1.1 copy.21
  3.0 0.0 copy-start.6
  3.0 0.8 copy.22.refs_1_
  3.9 0.0 copy-done.6
  3.9 1.0 copy.23.refs_5_
  4.9 225.8 %layer.1 = (bf16[256,1024]{1,0:T(8,128)(2,1)}, f32[256,1024]{1,0:T(8,128)}, f32[128,768]{1,0:T(8,128)}, f32[256,128]{1,0:T(8,128)}, f32[128,1024]{1,0:T(8,128)},...) custom-call(bf16[256,1024]{1,0:T(8,128)(2,1)} %refs_0_.1, ...), custom_call_target="tpu_custom_call" | custom-call | tf_op jit(solution)/shard_map/layer/pallas_call | solution.py:833
  230.7 0.0 copy-start.7
  230.7 0.7 copy-done.7
  231.4 0.6 copy.28
  232.0 0.0 copy-start.3
  232.0 1.2 copy.24
  233.3 0.0 copy-start
  233.3 0.9 copy.25
  234.2 0.0 copy-done.3
  234.2 0.8 copy.36
  235.0 0.0 copy-done
  235.0 0.0 copy-start.4
  235.0 0.0 copy-start.2
  235.0 1.0 copy.37
  236.0 0.0 copy-done.4
  236.0 0.7 copy.38
  236.6 0.0 copy-done.2
  236.6 0.0 copy-start.1
  236.6 0.8 copy.39
  237.4 0.4 copy-done.1
  237.9 0.0 copy-start.8
  237.9 0.0 copy-start.5
  237.9 0.8 copy.40
  238.7 0.0 copy-done.8
  238.7 0.6 copy.41
  239.3 0.0 copy-done.5
  239.3 0.6 copy.42
Async XLA Ops:
  3.0 0.8 copy-start.6
  230.7 0.7 copy-start.7
  232.0 2.1 copy-start.3
  233.3 1.7 copy-start
  235.0 1.0 copy-start.4
  235.0 1.7 copy-start.2
  236.6 1.2 copy-start.1
  237.9 0.8 copy-start.8
  237.9 1.4 copy-start.5

commit v4 on v3

--- a/solution.py
+++ b/solution.py
@@ -77,7 +77,7 @@
     def local(self):
         return pltpu.make_async_copy(self.own, self.piece(self.full, self.dp), self.local_sem)
 
-    def start(self):
+    def start_along(self):
         self.local().start()
 
         @pl.when(self.line < LINES - 1)
@@ -88,6 +88,7 @@
         def _():
             self.copy(self.dp, 1, self.own).start()
 
+    def start_across(self):
         self.copy(self.dp, 2, self.own).start()
 
     def step(self, distance):
@@ -214,7 +215,7 @@
         self.near(half).wait_recv()
         rows = partial.shape[0]
         total = partial + self.near_in[half].astype(jnp.float32)
-        self.across_out[half * rows : (half + 1) * rows, :] = total.astype(jnp.bfloat16)
+        row_piece(self.across_out, half, rows)[...] = total.astype(jnp.bfloat16)
         self.across(half).start()
 
     def give_near(self, half, partial):
@@ -226,7 +227,7 @@
         rows = partial.shape[0]
         total = partial + self.near_in[HALVES + half].astype(jnp.float32)
         self.across(half).wait_recv()
-        return total + self.across_in[half * rows : (half + 1) * rows, :].astype(jnp.float32)
+        return total + row_piece(self.across_in, half, rows)[...].astype(jnp.float32)
 
     def finish(self):
         for slot in range(2 * HALVES):
@@ -257,6 +258,109 @@
     average = jnp.mean(grad, axis=-1, keepdims=True)
     along = jnp.mean(grad * normed, axis=-1, keepdims=True)
     return inverse * (grad - average - normed * along)
+
+
+class DirectGather:
+    def __init__(self, own, full, piece, send_sem, recv_sem, local_sem):
+        self.own, self.full, self.piece = own, full, piece
+        self.send_sem, self.recv_sem, self.local_sem = send_sem, recv_sem, local_sem
+        self.dp, self.tensor = position()
+
+    def along(self, step):
+        there = self.dp ^ (2 * step)
+        return remote(
+            self.own,
+            self.piece(self.full, self.dp),
+            self.send_sem.at[step],
+            self.recv_sem.at[step],
+            (there, self.tensor),
+        )
+
+    def across(self, step, source=None):
+        view = self.piece(self.full, self.dp ^ (2 * step))
+        return remote(
+            view if source is None else source,
+            view,
+            self.send_sem.at[LINES + step],
+            self.recv_sem.at[LINES + step],
+            (self.dp ^ 1, self.tensor),
+        )
+
+    def local(self):
+        return pltpu.make_async_copy(self.own, self.piece(self.full, self.dp), self.local_sem)
+
+    def start_along(self):
+        self.local().start()
+        for step in range(1, LINES):
+            self.along(step).start()
+
+    def start_across(self):
+        self.across(0, self.own).start()
+
+    def step(self, step):
+        self.along(step).wait_recv()
+        self.across(step).start()
+
+    def arrive(self, step):
+        self.across(step).wait_recv()
+
+    def finish(self):
+        for step in range(LINES):
+            self.across(step).wait_send()
+        for step in range(1, LINES):
+            self.along(step).wait_send()
+
+
+class ColumnScatter:
+    def __init__(self, near_out, near_in, across_out, across_in, send_sem, recv_sem):
+        self.near_out, self.near_in = near_out, near_in
+        self.across_out, self.across_in = across_out, across_in
+        self.send_sem, self.recv_sem = send_sem, recv_sem
+        self.dp, self.tensor = position()
+
+    def near(self, slot):
+        return remote(
+            self.near_out.at[slot],
+            self.near_in.at[slot],
+            self.send_sem.at[slot],
+            self.recv_sem.at[slot],
+            (self.dp, self.tensor ^ CORE),
+        )
+
+    def across(self, at):
+        return remote(
+            self.across_out.at[at],
+            self.across_in.at[at],
+            self.send_sem.at[2 * LINES + at],
+            self.recv_sem.at[2 * LINES + at],
+            (self.dp, self.tensor ^ ACROSS),
+        )
+
+    def give_far(self, at, partial):
+        self.near_out[at] = partial.astype(jnp.bfloat16)
+        self.near(at).start()
+
+    def give_near(self, at, partial):
+        self.near_out[LINES + at] = partial.astype(jnp.bfloat16)
+        self.near(LINES + at).start()
+
+    def give_across(self, at, partial):
+        self.near(at).wait_recv()
+        total = partial + self.near_in[at].astype(jnp.float32)
+        self.across_out[at] = total.astype(jnp.bfloat16)
+        self.across(at).start()
+
+    def take(self, at, partial):
+        self.near(LINES + at).wait_recv()
+        total = partial + self.near_in[LINES + at].astype(jnp.float32)
+        self.across(at).wait_recv()
+        return total + self.across_in[at].astype(jnp.float32)
+
+    def finish(self):
+        for slot in range(2 * LINES):
+            self.near(slot).wait_send()
+        for at in range(LINES):
+            self.across(at).wait_send()
 
 
 class LineScatter:
@@ -315,11 +419,11 @@
         self.held, self.arrived, self.send_sem, self.recv_sem = held, arrived, send_sem, recv_sem
         dp, tensor = position()
         self.targets = (
+            (dp ^ 1, tensor),
             (dp, tensor ^ CORE),
-            (dp ^ 1, tensor),
+            (dp, tensor ^ ACROSS),
             (dp ^ 2, tensor),
             (dp ^ 4, tensor),
-            (dp, tensor ^ ACROSS),
         )
 
     def copy(self, step):
@@ -351,8 +455,9 @@
     bf16, f32 = jnp.bfloat16, jnp.float32
     half_rows = rows // HALVES
     local = r.queries.shape[1]
-    piece = r.triple_own.shape[0]
+    piece = r.triple_own.shape[1]
     pairs = local // (2 * HEAD)
+    hidden = r.hidden.shape[1]
     near, across, far = tensor ^ CORE, tensor ^ ACROSS, tensor ^ FAR
 
     def of_rows(ref, index):
@@ -361,6 +466,9 @@
     def of_columns(ref, index):
         return column_piece(ref, index, piece)
 
+    def of_stack(ref, index):
+        return ref.at[:, pl.ds(pl.multiple_of(index * piece, piece), piece), :]
+
     def block(rank, size=rows):
         return pl.ds(pl.multiple_of(rank * size, size), size)
 
@@ -371,13 +479,13 @@
         return slice(half * half_rows, (half + 1) * half_rows)
 
     lines = [
-        LineGather(own, full, view, r.line_send.at[at], r.line_recv.at[at], r.line_local.at[at])
-        for at, (own, full, view) in enumerate(
+        kind(own, full, view, r.line_send.at[at], r.line_recv.at[at], r.line_local.at[at])
+        for at, (kind, own, full, view) in enumerate(
             (
-                (r.triple_own, r.triple, of_rows),
-                (r.output_own, r.output, of_columns),
-                (r.up_own, r.up, of_rows),
-                (r.down_own, r.down, of_columns),
+                (LineGather, r.triple_own, r.triple, of_stack),
+                (DirectGather, r.output_own, r.output, of_columns),
+                (LineGather, r.up_own, r.up, of_rows),
+                (DirectGather, r.down_own, r.down, of_columns),
             )
         )
     ]
@@ -386,7 +494,7 @@
         LineScatter(partial, view, side, along, r.part_send.at[at], r.part_recv.at[at])
         for at, (partial, view, side, along) in enumerate(
             (
-                (r.grad_project, of_rows, r.project_side, r.project_line),
+                (r.grad_project, of_stack, r.project_side, r.project_line),
                 (r.grad_output, of_columns, r.output_side, r.output_line),
                 (r.grad_up, of_rows, r.up_side, r.up_line),
                 (r.grad_down, of_columns, r.down_side, r.down_line),
@@ -399,42 +507,75 @@
         for at, full in enumerate((r.gathered, r.first_all, r.second_all, r.branch_all))
     ]
     scatters = [
-        RowScatter(*buffers, r.sum_send.at[at], r.sum_recv.at[at])
-        for at, buffers in enumerate(
+        kind(*buffers, r.sum_send.at[at], r.sum_recv.at[at])
+        for at, (kind, buffers) in enumerate(
             (
-                (r.near_out_a, r.near_in_a, r.across_out_a, r.across_in_a),
-                (r.near_out_b, r.near_in_b, r.across_out_b, r.across_in_b),
+                (RowScatter, (r.near_out_a, r.near_in_a, r.across_out_a, r.across_in_a)),
+                (ColumnScatter, (r.near_out_b, r.near_in_b, r.across_out_b, r.across_in_b)),
             )
             * 2
         )
     ]
     total = Total(r.held_totals, r.arrived_totals, r.total_send, r.total_recv)
 
-    def scatter_blocks(scatter, product):
-        for half, partial in enumerate(split(product(far))):
-            scatter.give_far(half, partial)
-        for half, partial in enumerate(split(product(across))):
-            scatter.give_across(half, partial)
-        for half, partial in enumerate(split(product(near))):
-            scatter.give_near(half, partial)
-
+    def column_block(at):
+        return block((dp // 2) ^ at, 2 * piece)
+
+    def scatter_columns(scatter, at, product):
+        lanes = column_block(at)
+        scatter.give_far(at, product(far, lanes))
+        middle = product(across, lanes)
+        scatter.give_near(at, product(near, lanes))
+        r.kept[:, lanes] = product(tensor, lanes)
+        scatter.give_across(at, middle)
+
+    def chunks(size, start, body):
+        @pl.loop(0, size // CHUNK)
+        def _(chunk):
+            offset = chunk * CHUNK
+            body(
+                pl.ds(pl.multiple_of(offset, CHUNK), CHUNK),
+                pl.ds(pl.multiple_of(start + offset, CHUNK), CHUNK),
+            )
+
+    loads = [
+        pltpu.make_async_copy(source, target, r.load_sem.at[at])
+        for at, (source, target) in enumerate(
+            (
+                (r.tokens, gathers[0].view(tensor)),
+                (r.segments, r.segment_row),
+                (r.bias_from, r.bias_rows),
+                (r.gains_from, r.norm_gains),
+                (r.hidden_from.at[pl.ds(pl.multiple_of(tensor * hidden, hidden), hidden)], r.hidden_bias),
+                (r.cotangent_from, r.cotangent),
+            )
+        )
+    ]
+    for load in loads:
+        load.start()
     greet()
-    place = pltpu.make_async_copy(r.tokens, gathers[0].view(tensor), r.place_sem)
-    place.start()
-    triple_line.start()
-    place.wait()
+    triple_line.start_along()
+    triple_line.start_across()
+    loads[0].wait()
     gathers[0].start()
     triple_line.step(1)
+    loads[1].wait()
+    numbers = r.segment_row[...].astype(f32)
+    r.segment_column[...] = jnp.broadcast_to(numbers, (8, numbers.shape[1])).T[:, :1]
+    r.segment_row_f32[...] = numbers
     triple_line.step(2)
+    output_line.start_along()
     gathers[0].wait_near()
     for half in range(HALVES):
         gathers[0].wait_across(half)
     triple_line.step(3)
-    output_line.start()
-    up_line.start()
+    output_line.start_across()
+    up_line.start_along()
     for half in range(HALVES):
         gathers[0].wait_far(half)
     triple_line.arrive()
+    for load in loads[2:]:
+        load.wait()
     columns = pl.ds(pl.multiple_of(tensor * local, local), local)
     query_bias = r.bias_rows[0:1, columns]
     value_bias = r.bias_rows[1:2, columns]
@@ -443,18 +584,19 @@
     def _(index):
         here = block(index)
         left = r.gathered[here, :]
-        query = (dot(left, r.triple[:, :local]) + query_bias).astype(bf16)
+        query = (dot(left, r.triple[0]) + query_bias).astype(bf16)
         r.queries[here, :] = query * bf16(HEAD**-0.5)
-        key = dot(left, r.triple[:, local : 2 * local])
+        key = dot(left, r.triple[1])
         r.key_rows[here, :] = key.astype(bf16)
         r.key_turned[:, here] = key.T.astype(bf16)
-        value = dot(left, r.triple[:, 2 * local :]) + value_bias
+        value = dot(left, r.triple[2]) + value_bias
         r.value_rows[here, :] = value.astype(bf16)
         r.value_turned[:, here] = value.T.astype(bf16)
 
-    output_line.step(1)
+    for step in range(1, LINES):
+        output_line.step(step)
+    up_line.start_across()
     up_line.step(1)
-    down_line.start()
 
     def head_rows(head):
         return pl.ds(pl.multiple_of(head * HEAD, HEAD), HEAD)
@@ -467,7 +609,7 @@
             lanes = block(pair, 2 * HEAD)
             query = r.queries[here, lanes]
             keys = r.key_rows[:, lanes]
-            same = r.segment_column[...] == r.segment_row[:, here]
+            same = r.segment_column[...] == r.segment_row_f32[:, here]
             lane = lax.broadcasted_iota(jnp.int32, query.shape, 1)
             outs = []
             for side in range(2):
@@ -482,44 +624,60 @@
                 r.log_totals[pl.ds(head, 1), here] = top + jnp.log(mass)
             r.mixed[here, lanes] = jnp.concatenate(outs, axis=0).T.astype(bf16)
 
-        return r.mixed[here, :]
-
-    mixed_far = attend(far)
-    output_line.step(2)
-    output_line.step(3)
-    up_line.step(2)
-    output_line.arrive()
-    for half, partial in enumerate(split(dot(mixed_far, r.output[...]))):
-        scatters[0].give_far(half, partial)
-    for half, partial in enumerate(split(dot(attend(across), r.output[...]))):
-        scatters[0].give_across(half, partial)
-    up_line.step(3)
-    down_line.step(1)
-    for half, partial in enumerate(split(dot(attend(near), r.output[...]))):
-        scatters[0].give_near(half, partial)
-    down_line.step(2)
-    for half, partial in enumerate(split(dot(attend(tensor), r.output[...]))):
+    @pl.loop(0, 4)
+    def _(turn):
+        rank = tensor ^ (FAR - turn)
+        attend(rank)
+
+        @pl.when(turn == 0)
+        def _():
+            output_line.local().wait()
+            for step in range(LINES):
+                output_line.arrive(step)
+
+        r.partial[...] = dot(r.mixed[block(rank), :], r.output[...])
+
+        def give(method):
+            for half in range(HALVES):
+                method(half, r.partial[part_of(half), :])
+
+        @pl.when(turn == 0)
+        def _():
+            give(scatters[0].give_far)
+
+        @pl.when(turn == 1)
+        def _():
+            give(scatters[0].give_across)
+            up_line.step(2)
+            down_line.start_along()
+
+        @pl.when(turn == 2)
+        def _():
+            give(scatters[0].give_near)
+
+        @pl.when(turn == 3)
+        def _():
+            up_line.step(3)
+            down_line.start_across()
+
+    for half in range(HALVES):
         part = part_of(half)
-        own_rows = r.gathered[block(tensor * HALVES + half, half_rows), :].astype(f32)
-        normed, inverse = normalize(own_rows + scatters[0].take(half, partial) + r.bias_rows[2:3, :])
-        r.normed_one[part, :] = normed
-        r.inverse_one[part, :] = inverse
-        first = normed * r.norm_gains[0:1, :] + r.bias_rows[3:4, :]
-        r.first_all[block(tensor * HALVES + half, half_rows), :] = first.astype(bf16)
+        r.kept[part, :] = scatters[0].take(half, r.partial[part, :])
+
+        def first_norm(_, here):
+            own_rows = r.gathered[pl.ds(pl.multiple_of(tensor * rows + here.start, CHUNK), CHUNK), :]
+            normed, inverse = normalize(own_rows.astype(f32) + r.kept[here, :] + r.bias_rows[2:3, :])
+            r.normed_one[here, :] = normed
+            r.inverse_one[here, :] = inverse
+            first = normed * r.norm_gains[0:1, :] + r.bias_rows[3:4, :]
+            into = pl.ds(pl.multiple_of(tensor * rows + here.start, CHUNK), CHUNK)
+            r.first_all[into, :] = first.astype(bf16)
+
+        chunks(half_rows, half * half_rows, first_norm)
     scatters[0].finish()
 
     gathers[1].start()
-    down_line.step(3)
     r.sums[...] = jnp.zeros_like(r.sums)
-
-    def chunks(size, start, body):
-        @pl.loop(0, size // CHUNK)
-        def _(chunk):
-            offset = chunk * CHUNK
-            body(
-                pl.ds(pl.multiple_of(offset, CHUNK), CHUNK),
-                pl.ds(pl.multiple_of(start + offset, CHUNK), CHUNK),
-            )
 
     def extent(rank, half):
         size = rows if half is None else half_rows
@@ -528,7 +686,7 @@
 
     def up_part(rank, half=None):
         start, size, here = extent(rank, half)
-        r.upper[:size, :] = dot(r.first_all[here, :], r.up[...]) + r.hidden_bias[...]
+        r.upper[:size, :] = dot(r.first_all[here, :], r.up[...]) + r.hidden_bias[...].reshape(1, hidden)
 
         def body(part, into):
             value = r.upper[part, :]
@@ -539,9 +697,6 @@
 
         chunks(size, start, body)
 
-    def down_part(rank, half=None):
-        return dot(r.hidden[extent(rank, half)[2], :], r.down[...])
-
     def back_part(rank, half=None):
         start, size, here = extent(rank, half)
         r.upper[:size, :] = dot_nt(r.second_all[here, :], r.down[...])
@@ -552,20 +707,52 @@
             r.sums[6:7, :] += jnp.sum(low.astype(f32), axis=0, keepdims=True)
 
         chunks(size, start, body)
-        return dot_nt(r.upper_low[here, :], r.up[...])
+        r.partial[:size, :] = dot_nt(r.upper_low[here, :], r.up[...])
 
     up_line.arrive()
-    up_part(tensor)
-    gathers[1].wait_near()
-    up_part(near)
-    for half in range(HALVES):
-        gathers[1].wait_across(half)
-        up_part(across, half)
-        gathers[1].wait_far(half)
-        up_part(far, half)
-    down_line.arrive()
-    scatter_blocks(scatters[1], down_part)
-    r.kept[...] = down_part(tensor)
+
+    @pl.loop(0, 2)
+    def _(turn):
+        @pl.when(turn == 1)
+        def _():
+            down_line.step(1)
+            gathers[1].wait_near()
+
+        up_part(tensor ^ turn)
+
+    def other_chip(gather, body):
+        @pl.loop(0, 2 * HALVES)
+        def _(turn):
+            half, side = turn // 2, turn % 2
+
+            @pl.when(side == 0)
+            def _():
+                gather.wait_across(half)
+
+            @pl.when(side == 1)
+            def _():
+                gather.wait_far(half)
+
+            body(half, side)
+
+    def up_other(half, side):
+        up_part(tensor ^ (ACROSS + side), half)
+
+        @pl.when(side == 1)
+        def _():
+            down_line.step(2 + half)
+
+    other_chip(gathers[1], up_other)
+
+    def down_part(rank, lanes):
+        return dot(r.hidden[block(rank), :], r.down[:, lanes])
+
+    down_line.local().wait()
+
+    @pl.loop(0, LINES)
+    def _(at):
+        down_line.arrive(at)
+        scatter_columns(scatters[1], at, down_part)
 
     def add_to(row, value):
         r.sums[row : row + 1, :] += jnp.sum(value, axis=0, keepdims=True)
@@ -574,7 +761,7 @@
         first = r.normed_one[here, :] * r.norm_gains[0:1, :] + r.bias_rows[3:4, :]
         normed, inverse = normalize(first + r.kept[here, :] + r.bias_rows[4:5, :])
         shifted = normed * r.norm_gains[1:2, :] + r.bias_rows[5:6, :]
-        r.layer_out[here, :] = shifted.astype(bf16)
+        r.layer_low[here, :] = shifted.astype(bf16)
         grad = r.cotangent[here, :].astype(f32)
         add_to(5, grad * normed)
         add_to(3, grad)
@@ -584,23 +771,53 @@
         add_to(2, low.astype(f32))
         r.second_all[pl.ds(pl.multiple_of(tensor * rows + here.start, CHUNK), CHUNK), :] = low
 
-    for half in range(HALVES):
-        part = part_of(half)
-        r.kept[part, :] = scatters[1].take(half, r.kept[part, :])
-        chunks(half_rows, half * half_rows, second_norm)
+    @pl.loop(0, LINES)
+    def _(at):
+        lanes = column_block(at)
+        r.kept[:, lanes] = scatters[1].take(at, r.kept[:, lanes])
+
+    chunks(rows, 0, second_norm)
+    saves = []
+
+    def save(source, target):
+        saves.append(pltpu.make_async_copy(source, target, r.save_sem.at[len(saves)]))
+        saves[-1].start()
+
+    save(r.layer_low, r.layer_out)
     scatters[1].finish()
 
     gathers[2].start()
-    r.kept[...] = back_part(tensor)
-    gathers[2].wait_near()
-    for half, partial in enumerate(split(back_part(near))):
-        scatters[2].give_near(half, partial)
-    for half in range(HALVES):
-        gathers[2].wait_across(half)
-        r.held[...] = back_part(across, half)
-        gathers[2].wait_far(half)
-        scatters[2].give_far(half, back_part(far, half))
-        scatters[2].give_across(half, r.held[...])
+
+    @pl.loop(0, 2)
+    def _(turn):
+        @pl.when(turn == 1)
+        def _():
+            gathers[2].wait_near()
+
+        back_part(tensor ^ turn)
+
+        @pl.when(turn == 0)
+        def _():
+            r.kept[...] = r.partial[...]
+
+        @pl.when(turn == 1)
+        def _():
+            for half in range(HALVES):
+                scatters[2].give_near(half, r.partial[part_of(half), :])
+
+    def back_other(half, side):
+        back_part(tensor ^ (ACROSS + side), half)
+
+        @pl.when(side == 0)
+        def _():
+            r.held[...] = r.partial[:half_rows, :]
+
+        @pl.when(side == 1)
+        def _():
+            scatters[2].give_far(half, r.partial[:half_rows, :])
+            scatters[2].give_across(half, r.held[...])
+
+    other_chip(gathers[2], back_other)
 
     def weight_grad(left, right, result):
         @pl.loop(0, left.shape[1] // rows)
@@ -613,7 +830,7 @@
     weight_grad(r.first_all, r.upper_low, r.grad_up)
     up_sum.start()
 
-    def first_norm(_, here):
+    def first_back(_, here):
         grad = r.grad_rows[here, :] + r.kept[here, :]
         normed = r.normed_one[here, :]
         add_to(4, grad * normed)
@@ -627,7 +844,7 @@
     for half in range(HALVES):
         part = part_of(half)
         r.kept[part, :] = scatters[2].take(half, r.kept[part, :])
-        chunks(half_rows, half * half_rows, first_norm)
+        chunks(half_rows, half * half_rows, first_back)
     scatters[2].finish()
 
     gathers[3].start()
@@ -645,7 +862,7 @@
             grad = r.mixed_low[:, lanes]
             keys = r.key_rows[:, lanes]
             values = r.value_rows[:, lanes]
-            same = r.segment_column[...] == r.segment_row[:, here]
+            same = r.segment_column[...] == r.segment_row_f32[:, here]
             lane = lax.broadcasted_iota(jnp.int32, query.shape, 1)
             outs = []
             for side in range(2):
@@ -664,24 +881,32 @@
             grad_query = jnp.concatenate(outs, axis=0).T * HEAD**-0.5
             r.projected_low[here, lanes] = grad_query.astype(bf16)
 
-    attend_back(tensor)
-    down_sum.relay(3)
-    gathers[3].wait_near()
-    attend_back(near)
-    down_sum.relay(2)
-    for half in range(HALVES):
-        gathers[3].wait_across(half)
-    attend_back(across)
-    down_sum.relay(1)
-    for half in range(HALVES):
-        gathers[3].wait_far(half)
+    @pl.loop(0, 4)
+    def _(turn):
+        @pl.when(turn == 1)
+        def _():
+            gathers[3].wait_near()
+
+        @pl.when(turn == 2)
+        def _():
+            for half in range(HALVES):
+                gathers[3].wait_across(half)
+
+        @pl.when(turn == 3)
+        def _():
+            for half in range(HALVES):
+                gathers[3].wait_far(half)
+
+        attend_back(tensor ^ turn)
+
+        @pl.when(turn < 3)
+        def _():
+            down_sum.relay(3 - turn)
+
+    up_sum.relay(3)
     r.grad_output[...] = dot_tn(r.mixed[...], r.branch_all[...]).astype(bf16)
-    output_sum.start()
-    attend_back(far)
     r.projected_low[:, local : 2 * local] = grad_keys[...].astype(bf16)
     r.projected_low[:, 2 * local :] = grad_values[...].astype(bf16)
-    weight_grad(r.gathered, r.projected_low, r.grad_project)
-    project_sum.start()
     r.held_totals[0] = jnp.zeros(r.held_totals.shape[1:], f32)
     r.held_totals[0, 2:8, :] = r.sums[0:6, :]
     r.held_totals[0, pl.ds(8 + tensor, 1), :] = r.sums[6:7, :]
@@ -689,37 +914,78 @@
         low = r.projected_low[:, at * local : (at + 1) * local].astype(f32)
         r.held_totals[0, row : row + 1, columns] = jnp.sum(low, axis=0, keepdims=True)
     total.start()
-    up_sum.relay(3)
-
-    def token_part(rank):
-        return dot_nt(r.projected_low[block(rank), :], r.triple[...])
-
-    scatter_blocks(scatters[3], token_part)
+    output_sum.start()
+    for at in range(3):
+        lanes = slice(at * local, (at + 1) * local)
+        weight_grad(r.gathered, r.projected_low.at[:, lanes], r.grad_project.at[at])
+    project_sum.start()
+    up_sum.relay(2)
+
+    def token_part(rank, lanes):
+        product = 0
+        for at in range(3):
+            left = r.projected_low[block(rank), at * local : (at + 1) * local]
+            product += dot_nt(left, r.triple[at, lanes, :])
+        return product
+
+    @pl.loop(0, LINES)
+    def _(at):
+        scatter_columns(scatters[3], at, token_part)
+
+    up_sum.relay(1)
+    down_sum.finish(r.down_sum)
+    save(r.down_sum, r.down_out)
+
+    @pl.loop(0, LINES)
+    def _(at):
+        lanes = column_block(at)
+        r.grad_rows[:, lanes] += scatters[3].take(at, r.kept[:, lanes])
+
+    save(r.grad_rows, r.grad_tokens)
     total.step(0)
-    up_sum.relay(2)
-    mine = split(token_part(tensor))
     total.step(1)
-    up_sum.relay(1)
-    down_sum.finish(r.down_out)
+    output_sum.relay(3)
     total.step(2)
-    for half, partial in enumerate(mine):
-        part = part_of(half)
-        r.grad_tokens[part, :] = scatters[3].take(half, partial) + r.grad_rows[part, :]
-    for step in (3, 2, 1):
-        output_sum.relay(step)
+    output_sum.relay(2)
+    output_sum.relay(1)
+    up_sum.finish(r.up_sum)
+    save(r.up_sum, r.up_out)
+    project_sum.relay(3)
     total.step(3)
-    up_sum.finish(r.up_out)
-    for step in (3, 2, 1):
-        project_sum.relay(step)
+    project_sum.relay(2)
+    output_sum.finish(r.output_sum)
+    save(r.output_sum, r.output_out)
+    project_sum.relay(1)
     total.step(4)
-    r.bias_out[...] = r.held_totals[5, 0:6, :]
-    r.gains_out[...] = r.held_totals[5, 6:8, :]
-    r.hidden_out[...] = r.held_totals[5, 8:12, :]
-    output_sum.finish(r.output_out)
-    project_sum.finish(r.project_out)
+    r.bias_sum[...] = r.held_totals[5, 0:6, :]
+    r.gains_sum[...] = r.held_totals[5, 6:8, :]
+    for at in range(4):
+        r.hidden_sum[at * hidden : (at + 1) * hidden] = r.held_totals[5, 8 + at, :]
+    save(r.bias_sum, r.bias_out)
+    save(r.gains_sum, r.gains_out)
+    save(r.hidden_sum, r.hidden_out)
+    project_sum.finish(r.project_sum)
+    save(r.project_sum, r.project_out)
     scatters[3].finish()
     for each in gathers + lines + [total]:
         each.finish()
+    for each in saves:
+        each.wait()
+
+
+def copy_kernel(count, *refs):
+    sources, targets, held, sem = refs[:count], refs[count : 2 * count], refs[2 * count : -1], refs[-1]
+    copies_in = [pltpu.make_async_copy(*pair, sem.at[at]) for at, pair in enumerate(zip(sources, held))]
+    copies_out = [
+        pltpu.make_async_copy(*pair, sem.at[count + at]) for at, pair in enumerate(zip(held, targets))
+    ]
+    for copy in copies_in:
+        copy.start()
+    for arrived, copy in zip(copies_in, copies_out):
+        arrived.wait()
+        copy.start()
+    for copy in copies_out:
+        copy.wait()
 
 
 def per_device_kernel(
@@ -740,26 +1006,20 @@
     local = output_weight.shape[0]
     piece = project_weight.shape[0]
     bf16, f32 = jnp.bfloat16, jnp.float32
-    local_bias = lax.dynamic_slice_in_dim(
-        hidden_bias, lax.axis_index("tensor") * local_hidden, local_hidden, 0
-    )
-    remote_inputs = dict(
+    inputs = dict(
         tokens=tokens,
-        triple_own=project_weight.reshape(piece, -1),
+        triple_own=project_weight.transpose(1, 0, 2),
         output_own=output_weight,
         up_own=up_weight,
         down_own=down_weight,
-    )
-    inputs = dict(
-        segment_column=segments.reshape(length, 1),
-        segment_row=segments.reshape(1, length),
-        cotangent=cotangent,
-        norm_gains=norm_gains,
-        bias_rows=bias_rows,
-        hidden_bias=local_bias.reshape(1, -1),
+        segments=segments,
+        cotangent_from=cotangent,
+        gains_from=norm_gains,
+        bias_from=bias_rows,
+        hidden_from=hidden_bias,
     )
     shapes = dict(
-        project=(piece, 3 * local),
+        project=(3, piece, local),
         output=(local, piece),
         up=(piece, local_hidden),
         down=(local_hidden, piece),
@@ -769,11 +1029,23 @@
     outputs |= dict(
         gains_out=((2, width), f32),
         bias_out=((6, width), f32),
-        hidden_out=((4, width), f32),
+        hidden_out=(hidden_bias.shape, f32),
     )
     scratch = dict(
+        segment_row=((1, length), jnp.int32),
+        segment_row_f32=((1, length), f32),
+        segment_column=((length, 1), f32),
+        cotangent=((rows, width), bf16),
+        norm_gains=(norm_gains.shape, f32),
+        bias_rows=(bias_rows.shape, f32),
+        hidden_bias=((local_hidden,), f32),
+        layer_low=((rows, width), bf16),
+        bias_sum=(bias_rows.shape, f32),
+        gains_sum=(norm_gains.shape, f32),
+        hidden_sum=(hidden_bias.shape, f32),
+        partial=((rows, width), f32),
         gathered=((length, width), bf16),
-        triple=((width, 3 * local), bf16),
+        triple=((3, width, local), bf16),
         output=((local, width), bf16),
         up=((width, local_hidden), bf16),
         down=((local_hidden, width), bf16),
@@ -799,7 +1071,7 @@
         branch_all=((length, width), bf16),
         mixed_low=((rows, local), bf16),
         projected_low=((length, 3 * local), bf16),
-        grad_project=((width, 3 * local), bf16),
+        grad_project=((3, width, local), bf16),
         grad_output=((local, width), bf16),
         grad_up=((width, local_hidden), bf16),
         grad_down=((local_hidden, width), bf16),
@@ -807,13 +1079,15 @@
         arrived_totals=((5, 16, width), f32),
     )
     for name, shape in shapes.items():
+        scratch[name + "_sum"] = (shape, f32)
         scratch[name + "_side"] = ((LINES,) + shape, bf16)
         scratch[name + "_line"] = ((LINES - 1,) + shape, bf16)
-    for at in "ab":
-        for name in ("near_out_", "near_in_"):
-            scratch[name + at] = ((2 * HALVES, rows // HALVES, width), bf16)
-        for name in ("across_out_", "across_in_"):
-            scratch[name + at] = ((rows, width), bf16)
+    for name in ("near_out_", "near_in_"):
+        scratch[name + "a"] = ((2 * HALVES, rows // HALVES, width), bf16)
+        scratch[name + "b"] = ((2 * LINES, rows, 2 * piece), bf16)
+    for name in ("across_out_", "across_in_"):
+        scratch[name + "a"] = ((rows, width), bf16)
+        scratch[name + "b"] = ((LINES, rows, 2 * piece), bf16)
     semaphores = dict(
         line_send=(4, 3 * LINES),
         line_recv=(4, 2 * LINES),
@@ -822,37 +1096,47 @@
         part_recv=(4, 2 * LINES),
         row_send=(4, 1 + 2 * HALVES),
         row_recv=(4, 1 + 2 * HALVES),
-        sum_send=(4, 3 * HALVES),
-        sum_recv=(4, 3 * HALVES),
+        sum_send=(4, 3 * LINES),
+        sum_recv=(4, 3 * LINES),
         total_send=(5,),
         total_recv=(5,),
-        place_sem=(),
-    )
-    names = [*remote_inputs, *inputs, *outputs, *scratch, *semaphores]
-    vmem, hbm = pl.BlockSpec(memory_space=pltpu.VMEM), pl.BlockSpec(memory_space=pltpu.HBM)
+        load_sem=(6,),
+        save_sem=(9,),
+    )
+    names = [*inputs, *outputs, *scratch, *semaphores]
+    hbm = pl.BlockSpec(memory_space=pltpu.HBM)
     results = pl.pallas_call(
         functools.partial(layer_kernel, names, rows),
         out_shape=[jax.ShapeDtypeStruct(*leaf) for leaf in outputs.values()],
-        in_specs=[hbm] * len(remote_inputs) + [vmem] * len(inputs),
-        out_specs=[vmem] * len(outputs),
+        in_specs=[hbm] * len(inputs),
+        out_specs=[hbm] * len(outputs),
         scratch_shapes=[pltpu.VMEM(*leaf) for leaf in scratch.values()]
         + [pltpu.SemaphoreType.DMA(shape) for shape in semaphores.values()],
         compiler_params=pltpu.CompilerParams(
             collective_id=0, has_side_effects=True, vmem_limit_bytes=VMEM_BYTES
         ),
         name="layer",
-    )(*remote_inputs.values(), *inputs.values())
+    )(*inputs.values())
+    results = pl.pallas_call(
+        functools.partial(copy_kernel, len(outputs)),
+        out_shape=[jax.ShapeDtypeStruct(*leaf) for leaf in outputs.values()],
+        in_specs=[hbm] * len(outputs),
+        out_specs=[hbm] * len(outputs),
+        scratch_shapes=[pltpu.VMEM(*leaf) for leaf in outputs.values()]
+        + [pltpu.SemaphoreType.DMA((2 * len(outputs),))],
+        name="copy",
+    )(*results)
     result = dict(zip(outputs, results))
     return (
         result["layer_out"],
         result["grad_tokens"],
-        result["project_out"].reshape(project_weight.shape),
+        result["project_out"].transpose(1, 0, 2),
         result["output_out"],
         result["up_out"],
         result["down_out"],
         result["gains_out"],
         result["bias_out"],
-        result["hidden_out"].reshape(-1),
+        result["hidden_out"],
     )
 
 

time: 240 us -> 200 us (0.83)
  Pallas kernels: 226 us -> 199 us
  local copies, waits for them, and re-layouts: 13.4 us -> 0 us
    pallas_call x1, Pallas kernels: 226 us -> 196 us  [per_device_kernel(): pl.pallas_call(functools.partial(layer_kernel, names, rows), out_shape=[j...]
    unnamed x28 -> x0, local copies, waits for them, and re-layouts: 9.02 us -> none
    pallas_call x0 -> x1, Pallas kernels: none -> 3.04 us  [per_device_kernel(): pl.pallas_call(functools.partial(copy_kernel, len(outputs)), out_shape=[j...]
where the time goes in v4:
time: 200 us
  Pallas kernels  199 us (100%)
    pallas_call x1, Pallas kernels, per_device_kernel(): pl.pallas_call(functools.partial(layer_kernel, names, rows), out_shape=[j...  196 us

profile of v4, /device:TPU:0, one launch (start us, length us, event | category | flops | bytes accessed | tf_op | source)
XLA Modules:
  0.0 200.3 jit_solution(14050019398657000420)
XLA Ops:
  0.6 196.5 %layer.1 = (bf16[256,1024]{1,0:T(8,128)(2,1)}, f32[256,1024]{1,0:T(8,128)}, f32[3,128,256]{2,1,0:T(8,128)}, f32[256,128]{1,0:T(8,128)}, f32[128,1024]{1,0:T(8,12...) custom-call(bf16[256,1024]{1,0:T(8,128)(2,1)} %refs_0_.1, ...), custom_call_target="tpu_custom_call" | custom-call | tf_op jit(solution)/shard_map/layer/pallas_call | solution.py:1108
  197.1 3.0 %copy.20 = (bf16[256,1024]{1,0:T(8,128)(2,1)}, f32[256,1024]{1,0:T(8,128)}, f32[3,128,256]{2,1,0:T(8,128)}, f32[256,128]{1,0:T(8,128)}, f32[128,1024]{1,0:T(8,12...) custom-call(bf16[256,1024]{1,0:T(8,128)(2,1)} %get-tuple-element.27.refs_0_, ...), custom_call_target="tpu_custom_call" | custom-call | tf_op jit(solution)/shard_map/copy/pallas_call | solution.py:1120

commit v5 on v4

--- a/solution.py
+++ b/solution.py
@@ -16,6 +16,8 @@
 CORE, ACROSS, FAR = 1, 2, 3
 HALVES = 2
 CHUNK = 16
+NORM = 64
+ORDER = (3, 2, 1, 0)
 VMEM_BYTES = 60 << 20
 
 
@@ -260,6 +262,64 @@
     return inverse * (grad - average - normed * along)
 
 
+class LineFirstScatter:
+    def __init__(self, partial, piece, line_in, across_out, across_in, send_sem, recv_sem):
+        self.partial, self.piece, self.line_in = partial, piece, line_in
+        self.across_out, self.across_in = across_out, across_in
+        self.send_sem, self.recv_sem = send_sem, recv_sem
+        self.dp, self.tensor = position()
+
+    def view(self, step):
+        return self.piece(self.partial, (self.dp // 2) ^ step)
+
+    def along(self, step):
+        return remote(
+            self.view(step),
+            self.line_in.at[step // 2 if step != 2 else 2],
+            self.send_sem.at[step],
+            self.recv_sem.at[step],
+            (self.dp ^ (2 if step != 2 else 4), self.tensor),
+        )
+
+    def across(self):
+        return remote(
+            self.across_out,
+            self.across_in,
+            self.send_sem.at[0],
+            self.recv_sem.at[0],
+            (self.dp ^ 1, self.tensor),
+        )
+
+    def start(self):
+        self.along(3).start()
+        self.along(1).start()
+
+    def relay(self):
+        self.along(3).wait_recv()
+        total = self.view(2)[...].astype(jnp.float32) + self.line_in[1].astype(jnp.float32)
+        self.view(2)[...] = total.astype(jnp.bfloat16)
+        self.along(2).start()
+
+    def turn(self, result):
+        total = self.view(0)[...].astype(jnp.float32)
+        for step, slot in ((1, 0), (2, 2)):
+            self.along(step).wait_recv()
+            total = total + self.line_in[slot].astype(jnp.float32)
+        width = result.shape[1]
+        first, second = total[:, :width], total[:, width:]
+        even = self.dp % 2 == 0
+        result[...] = jnp.where(even, first, second)
+        self.across_out[...] = jnp.where(even, second, first).astype(jnp.bfloat16)
+        self.across().start()
+
+    def finish(self, result):
+        self.across().wait_recv()
+        result[...] += self.across_in[...].astype(jnp.float32)
+        self.across().wait_send()
+        for step in range(1, LINES):
+            self.along(step).wait_send()
+
+
 class DirectGather:
     def __init__(self, own, full, piece, send_sem, recv_sem, local_sem):
         self.own, self.full, self.piece = own, full, piece
@@ -384,14 +444,14 @@
     def along(self, step):
         return remote(
             self.view(step),
-            self.line_in.at[step - 1],
+            self.line_in.at[step // 2 if step != 2 else 2],
             self.send_sem.at[LINES + step],
             self.recv_sem.at[LINES + step],
-            (self.dp ^ (2 * step), self.tensor),
+            (self.dp ^ (2 if step != 2 else 4), self.tensor),
         )
 
     def start(self):
-        for step in reversed(range(LINES)):
+        for step in ORDER:
             self.across(step).start()
 
     def total(self, step):
@@ -399,15 +459,19 @@
         return self.view(step)[...].astype(jnp.float32) + self.side_in[step].astype(jnp.float32)
 
     def relay(self, step):
-        self.view(step)[...] = self.total(step).astype(jnp.bfloat16)
+        total = self.total(step)
+        if step == 2:
+            self.along(3).wait_recv()
+            total = total + self.line_in[1].astype(jnp.float32)
+        self.view(step)[...] = total.astype(jnp.bfloat16)
         self.along(step).start()
 
     def finish(self, result):
         total = self.total(0)
-        for step in range(1, LINES):
-            self.along(step).wait_recv()
-            total = total + self.line_in[step - 1].astype(jnp.float32)
-        result[...] = total
+        self.along(1).wait_recv()
+        total = total + self.line_in[0].astype(jnp.float32)
+        self.along(2).wait_recv()
+        result[...] = total + self.line_in[2].astype(jnp.float32)
         for step in range(LINES):
             self.across(step).wait_send()
         for step in range(1, LINES):
@@ -420,10 +484,10 @@
         dp, tensor = position()
         self.targets = (
             (dp ^ 1, tensor),
-            (dp, tensor ^ CORE),
-            (dp, tensor ^ ACROSS),
             (dp ^ 2, tensor),
             (dp ^ 4, tensor),
+            (dp, tensor ^ ACROSS),
+            (dp, tensor ^ CORE),
         )
 
     def copy(self, step):
@@ -469,6 +533,14 @@
     def of_stack(ref, index):
         return ref.at[:, pl.ds(pl.multiple_of(index * piece, piece), piece), :]
 
+    def of_half_stack(half):
+        size = piece // HALVES
+
+        def view(ref, index):
+            return ref.at[:, pl.ds(pl.multiple_of(index * piece + half * size, size), size), :]
+
+        return view, r.triple_own.at[:, half * size : (half + 1) * size, :]
+
     def block(rank, size=rows):
         return pl.ds(pl.multiple_of(rank * size, size), size)
 
@@ -478,18 +550,20 @@
     def part_of(half):
         return slice(half * half_rows, (half + 1) * half_rows)
 
+    (view_a, own_a), (view_b, own_b) = of_half_stack(0), of_half_stack(1)
     lines = [
         kind(own, full, view, r.line_send.at[at], r.line_recv.at[at], r.line_local.at[at])
         for at, (kind, own, full, view) in enumerate(
             (
-                (LineGather, r.triple_own, r.triple, of_stack),
+                (LineGather, own_a, r.triple, view_a),
+                (LineGather, own_b, r.triple, view_b),
                 (DirectGather, r.output_own, r.output, of_columns),
                 (LineGather, r.up_own, r.up, of_rows),
                 (DirectGather, r.down_own, r.down, of_columns),
             )
         )
     ]
-    triple_line, output_line, up_line, down_line = lines
+    *triple_lines, output_line, up_line, down_line = lines
     sums = [
         LineScatter(partial, view, side, along, r.part_send.at[at], r.part_recv.at[at])
         for at, (partial, view, side, along) in enumerate(
@@ -497,11 +571,25 @@
                 (r.grad_project, of_stack, r.project_side, r.project_line),
                 (r.grad_output, of_columns, r.output_side, r.output_line),
                 (r.grad_up, of_rows, r.up_side, r.up_line),
-                (r.grad_down, of_columns, r.down_side, r.down_line),
+                (r.grad_down.at[: hidden // 2, :], of_columns, r.down_side, r.down_line),
             )
         )
     ]
     project_sum, output_sum, up_sum, down_sum = sums
+
+    def of_both(ref, index):
+        return column_piece(ref, index, 2 * piece)
+
+    rest_sum = LineFirstScatter(
+        r.grad_down.at[hidden // 2 :, :],
+        of_both,
+        r.rest_line,
+        r.rest_out,
+        r.rest_in,
+        r.part_send.at[4],
+        r.part_recv.at[4],
+    )
+    down_top, down_rest = r.down_sum.at[: hidden // 2, :], r.down_sum.at[hidden // 2 :, :]
     gathers = [
         RowGather(full, rows, r.row_send.at[at], r.row_recv.at[at])
         for at, full in enumerate((r.gathered, r.first_all, r.second_all, r.branch_all))
@@ -521,21 +609,19 @@
     def column_block(at):
         return block((dp // 2) ^ at, 2 * piece)
 
-    def scatter_columns(scatter, at, product):
-        lanes = column_block(at)
-        scatter.give_far(at, product(far, lanes))
-        middle = product(across, lanes)
-        scatter.give_near(at, product(near, lanes))
-        r.kept[:, lanes] = product(tensor, lanes)
-        scatter.give_across(at, middle)
-
-    def chunks(size, start, body):
-        @pl.loop(0, size // CHUNK)
+    def scatter_columns(scatter, at):
+        scatter.give_far(at, r.columns[block(far), :])
+        scatter.give_near(at, r.columns[block(near), :])
+        scatter.give_across(at, r.columns[block(across), :])
+        r.kept[:, column_block(at)] = r.columns[block(tensor), :]
+
+    def chunks(size, start, body, step=CHUNK):
+        @pl.loop(0, size // step)
         def _(chunk):
-            offset = chunk * CHUNK
+            offset = chunk * step
             body(
-                pl.ds(pl.multiple_of(offset, CHUNK), CHUNK),
-                pl.ds(pl.multiple_of(start + offset, CHUNK), CHUNK),
+                pl.ds(pl.multiple_of(offset, step), step),
+                pl.ds(pl.multiple_of(start + offset, step), step),
             )
 
     loads = [
@@ -554,26 +640,32 @@
     for load in loads:
         load.start()
     greet()
-    triple_line.start_along()
-    triple_line.start_across()
+    for line in triple_lines:
+        line.start_along()
+        line.start_across()
     loads[0].wait()
     gathers[0].start()
-    triple_line.step(1)
+    for line in triple_lines:
+        line.step(1)
     loads[1].wait()
     numbers = r.segment_row[...].astype(f32)
     r.segment_column[...] = jnp.broadcast_to(numbers, (8, numbers.shape[1])).T[:, :1]
     r.segment_row_f32[...] = numbers
-    triple_line.step(2)
-    output_line.start_along()
+    for line in triple_lines:
+        line.step(2)
     gathers[0].wait_near()
     for half in range(HALVES):
         gathers[0].wait_across(half)
-    triple_line.step(3)
+    for line in triple_lines:
+        line.step(3)
+    output_line.start_along()
     output_line.start_across()
     up_line.start_along()
+    up_line.start_across()
     for half in range(HALVES):
         gathers[0].wait_far(half)
-    triple_line.arrive()
+    for line in triple_lines:
+        line.arrive()
     for load in loads[2:]:
         load.wait()
     columns = pl.ds(pl.multiple_of(tensor * local, local), local)
@@ -595,85 +687,84 @@
 
     for step in range(1, LINES):
         output_line.step(step)
-    up_line.start_across()
-    up_line.step(1)
 
     def head_rows(head):
         return pl.ds(pl.multiple_of(head * HEAD, HEAD), HEAD)
 
-    def attend(rank):
+    def attend(here, pair):
+        lanes = block(pair, 2 * HEAD)
+        query = r.queries[here, lanes]
+        keys = r.key_rows[:, lanes]
+        same = r.segment_column[...] == r.segment_row_f32[:, here]
+        lane = lax.broadcasted_iota(jnp.int32, query.shape, 1)
+        outs = []
+        for side in range(2):
+            scores = dot_nt(keys, jnp.where(lane // HEAD == side, query, bf16(0)))
+            scores = jnp.where(same, scores, NEGATIVE)
+            top = jnp.max(scores, axis=0, keepdims=True)
+            exponent = jnp.exp(scores - top)
+            mass = jnp.sum(exponent, axis=0, keepdims=True)
+            weights = (exponent * (1.0 / mass)).astype(bf16)
+            head = pair * 2 + side
+            outs.append(dot(r.value_turned[head_rows(head), :], weights))
+            r.log_totals[pl.ds(head, 1), here] = top + jnp.log(mass)
+        r.mixed[here, lanes] = jnp.concatenate(outs, axis=0).T.astype(bf16)
+
+    @pl.loop(0, 4 * pairs)
+    def _(turn):
+        rank, pair = tensor ^ (FAR - turn // pairs), turn % pairs
         here = block(rank)
-
-        @pl.loop(0, pairs)
-        def _(pair):
-            lanes = block(pair, 2 * HEAD)
-            query = r.queries[here, lanes]
-            keys = r.key_rows[:, lanes]
-            same = r.segment_column[...] == r.segment_row_f32[:, here]
-            lane = lax.broadcasted_iota(jnp.int32, query.shape, 1)
-            outs = []
-            for side in range(2):
-                scores = dot_nt(keys, jnp.where(lane // HEAD == side, query, bf16(0)))
-                scores = jnp.where(same, scores, NEGATIVE)
-                top = jnp.max(scores, axis=0, keepdims=True)
-                exponent = jnp.exp(scores - top)
-                mass = jnp.sum(exponent, axis=0, keepdims=True)
-                weights = (exponent * (1.0 / mass)).astype(bf16)
-                head = pair * 2 + side
-                outs.append(dot(r.value_turned[head_rows(head), :], weights))
-                r.log_totals[pl.ds(head, 1), here] = top + jnp.log(mass)
-            r.mixed[here, lanes] = jnp.concatenate(outs, axis=0).T.astype(bf16)
-
-    @pl.loop(0, 4)
-    def _(turn):
-        rank = tensor ^ (FAR - turn)
-        attend(rank)
-
-        @pl.when(turn == 0)
+        attend(here, pair)
+
+        def give(rank, method):
+            r.partial[...] = dot(r.mixed[block(rank), :], r.output[...])
+            for half in range(HALVES):
+                method(half, r.partial[part_of(half), :])
+
+        def after(index):
+            return pl.when(turn == index)
+
+        @after(0)
+        def _():
+            up_line.step(1)
+
+        @after(3)
         def _():
             output_line.local().wait()
             for step in range(LINES):
                 output_line.arrive(step)
-
-        r.partial[...] = dot(r.mixed[block(rank), :], r.output[...])
-
-        def give(method):
-            for half in range(HALVES):
-                method(half, r.partial[part_of(half), :])
-
-        @pl.when(turn == 0)
-        def _():
-            give(scatters[0].give_far)
-
-        @pl.when(turn == 1)
-        def _():
-            give(scatters[0].give_across)
+            give(far, scatters[0].give_far)
+            give(across, scatters[0].give_across)
+
+        @after(4)
+        def _():
             up_line.step(2)
             down_line.start_along()
 
-        @pl.when(turn == 2)
-        def _():
-            give(scatters[0].give_near)
-
-        @pl.when(turn == 3)
+        @after(5)
+        def _():
+            give(near, scatters[0].give_near)
+
+        @after(7)
         def _():
             up_line.step(3)
             down_line.start_across()
 
+    r.partial[...] = dot(r.mixed[block(tensor), :], r.output[...])
     for half in range(HALVES):
         part = part_of(half)
         r.kept[part, :] = scatters[0].take(half, r.partial[part, :])
 
         def first_norm(_, here):
-            own_rows = r.gathered[pl.ds(pl.multiple_of(tensor * rows + here.start, CHUNK), CHUNK), :]
+            own_rows = r.gathered[pl.ds(pl.multiple_of(tensor * rows + here.start, NORM), NORM), :]
             normed, inverse = normalize(own_rows.astype(f32) + r.kept[here, :] + r.bias_rows[2:3, :])
             r.normed_one[here, :] = normed
             r.inverse_one[here, :] = inverse
             first = normed * r.norm_gains[0:1, :] + r.bias_rows[3:4, :]
-            into = pl.ds(pl.multiple_of(tensor * rows + here.start, CHUNK), CHUNK)
+            into = pl.ds(pl.multiple_of(tensor * rows + here.start, NORM), NORM)
             r.first_all[into, :] = first.astype(bf16)
 
-        chunks(half_rows, half * half_rows, first_norm)
+        chunks(half_rows, half * half_rows, first_norm, NORM)
     scatters[0].finish()
 
     gathers[1].start()
@@ -729,13 +820,13 @@
             def _():
                 gather.wait_across(half)
 
-            @pl.when(side == 1)
-            def _():
-                gather.wait_far(half)
-
             body(half, side)
 
     def up_other(half, side):
+        @pl.when(side == 1)
+        def _():
+            gathers[1].wait_far(half)
+
         up_part(tensor ^ (ACROSS + side), half)
 
         @pl.when(side == 1)
@@ -743,16 +834,14 @@
             down_line.step(2 + half)
 
     other_chip(gathers[1], up_other)
-
-    def down_part(rank, lanes):
-        return dot(r.hidden[block(rank), :], r.down[:, lanes])
 
     down_line.local().wait()
 
     @pl.loop(0, LINES)
     def _(at):
         down_line.arrive(at)
-        scatter_columns(scatters[1], at, down_part)
+        r.columns[...] = dot(r.hidden[...], r.down[:, column_block(at)])
+        scatter_columns(scatters[1], at)
 
     def add_to(row, value):
         r.sums[row : row + 1, :] += jnp.sum(value, axis=0, keepdims=True)
@@ -769,14 +858,14 @@
         r.grad_rows[here, :] = grad
         low = grad.astype(bf16)
         add_to(2, low.astype(f32))
-        r.second_all[pl.ds(pl.multiple_of(tensor * rows + here.start, CHUNK), CHUNK), :] = low
+        r.second_all[pl.ds(pl.multiple_of(tensor * rows + here.start, NORM), NORM), :] = low
 
     @pl.loop(0, LINES)
     def _(at):
         lanes = column_block(at)
         r.kept[:, lanes] = scatters[1].take(at, r.kept[:, lanes])
 
-    chunks(rows, 0, second_norm)
+    chunks(rows, 0, second_norm, NORM)
     saves = []
 
     def save(source, target):
@@ -805,28 +894,44 @@
             for half in range(HALVES):
                 scatters[2].give_near(half, r.partial[part_of(half), :])
 
-    def back_other(half, side):
-        back_part(tensor ^ (ACROSS + side), half)
-
-        @pl.when(side == 0)
-        def _():
-            r.held[...] = r.partial[:half_rows, :]
-
-        @pl.when(side == 1)
-        def _():
-            scatters[2].give_far(half, r.partial[:half_rows, :])
-            scatters[2].give_across(half, r.held[...])
-
-    other_chip(gathers[2], back_other)
-
-    def weight_grad(left, right, result):
+    def weight_grad(left, right, result, chip=None, add=False):
+        depth = slice(None) if chip is None else block(chip, 2 * rows)
+
         @pl.loop(0, left.shape[1] // rows)
         def _(index):
             lanes = block(index)
-            result[lanes, :] = dot_tn(left[:, lanes], right[...]).astype(bf16)
-
-    weight_grad(r.hidden, r.second_all, r.grad_down)
-    down_sum.start()
+            product = dot_tn(left[depth, lanes], right[depth, :])
+            if add:
+                product += result[lanes, :].astype(f32)
+            result[lanes, :] = product.astype(bf16)
+
+    weight_grad(r.hidden, r.second_all, r.grad_down, tensor // 2)
+
+    def back_other(half, side):
+        @pl.when((side == 1) & (half < HALVES - 1))
+        def _():
+            gathers[2].wait_far(half)
+
+        @pl.when((side == 0) & (half == HALVES - 1))
+        def _():
+            gathers[2].wait_far(half)
+            weight_grad(r.hidden, r.second_all, r.grad_down, 1 - tensor // 2, True)
+            rest_sum.start()
+            down_sum.start()
+
+        back_part(tensor ^ (ACROSS + side), half)
+
+        @pl.when(side == 0)
+        def _():
+            r.held[...] = r.partial[:half_rows, :]
+
+        @pl.when(side == 1)
+        def _():
+            scatters[2].give_far(half, r.partial[:half_rows, :])
+            scatters[2].give_across(half, r.held[...])
+
+    other_chip(gathers[2], back_other)
+
     weight_grad(r.first_all, r.upper_low, r.grad_up)
     up_sum.start()
 
@@ -839,12 +944,15 @@
         r.grad_rows[here, :] = grad
         low = grad.astype(bf16)
         add_to(0, low.astype(f32))
-        r.branch_all[pl.ds(pl.multiple_of(tensor * rows + here.start, CHUNK), CHUNK), :] = low
+        r.branch_all[pl.ds(pl.multiple_of(tensor * rows + here.start, NORM), NORM), :] = low
 
     for half in range(HALVES):
         part = part_of(half)
         r.kept[part, :] = scatters[2].take(half, r.kept[part, :])
-        chunks(half_rows, half * half_rows, first_back)
+        chunks(half_rows, half * half_rows, first_back, NORM)
+        if half == 0:
+            rest_sum.relay()
+            down_sum.relay(3)
     scatters[2].finish()
 
     gathers[3].start()
@@ -899,11 +1007,17 @@
 
         attend_back(tensor ^ turn)
 
-        @pl.when(turn < 3)
-        def _():
-            down_sum.relay(3 - turn)
-
-    up_sum.relay(3)
+        @pl.when(turn == 1)
+        def _():
+            down_sum.relay(1)
+            up_sum.relay(3)
+            down_sum.relay(2)
+
+        @pl.when(turn == 2)
+        def _():
+            rest_sum.turn(down_rest)
+
+    up_sum.relay(1)
     r.grad_output[...] = dot_tn(r.mixed[...], r.branch_all[...]).astype(bf16)
     r.projected_low[:, local : 2 * local] = grad_keys[...].astype(bf16)
     r.projected_low[:, 2 * local :] = grad_values[...].astype(bf16)
@@ -914,48 +1028,50 @@
         low = r.projected_low[:, at * local : (at + 1) * local].astype(f32)
         r.held_totals[0, row : row + 1, columns] = jnp.sum(low, axis=0, keepdims=True)
     total.start()
-    output_sum.start()
     for at in range(3):
         lanes = slice(at * local, (at + 1) * local)
         weight_grad(r.gathered, r.projected_low.at[:, lanes], r.grad_project.at[at])
     project_sum.start()
+    output_sum.start()
     up_sum.relay(2)
-
-    def token_part(rank, lanes):
-        product = 0
-        for at in range(3):
-            left = r.projected_low[block(rank), at * local : (at + 1) * local]
-            product += dot_nt(left, r.triple[at, lanes, :])
-        return product
-
-    @pl.loop(0, LINES)
-    def _(at):
-        scatter_columns(scatters[3], at, token_part)
-
-    up_sum.relay(1)
-    down_sum.finish(r.down_sum)
-    save(r.down_sum, r.down_out)
 
     @pl.loop(0, LINES)
     def _(at):
         lanes = column_block(at)
+        product = 0
+        for part in range(3):
+            left = r.projected_low[:, part * local : (part + 1) * local]
+            product += dot_nt(left, r.triple[part, lanes, :])
+        r.columns[...] = product
+        scatter_columns(scatters[3], at)
+
+    total.step(0)
+    project_sum.relay(3)
+    down_sum.finish(down_top)
+    rest_sum.finish(down_rest)
+    save(r.down_sum, r.down_out)
+
+    def take_tokens(at):
+        lanes = column_block(at)
         r.grad_rows[:, lanes] += scatters[3].take(at, r.kept[:, lanes])
 
+    take_tokens(0)
+    take_tokens(1)
+    take_tokens(2)
+    project_sum.relay(2)
+    take_tokens(3)
     save(r.grad_rows, r.grad_tokens)
-    total.step(0)
+    project_sum.relay(1)
     total.step(1)
+    up_sum.finish(r.up_sum)
+    save(r.up_sum, r.up_out)
     output_sum.relay(3)
     total.step(2)
     output_sum.relay(2)
     output_sum.relay(1)
-    up_sum.finish(r.up_sum)
-    save(r.up_sum, r.up_out)
-    project_sum.relay(3)
     total.step(3)
-    project_sum.relay(2)
-    output_sum.finish(r.output_sum)
-    save(r.output_sum, r.output_out)
-    project_sum.relay(1)
+    project_sum.finish(r.project_sum)
+    save(r.project_sum, r.project_out)
     total.step(4)
     r.bias_sum[...] = r.held_totals[5, 0:6, :]
     r.gains_sum[...] = r.held_totals[5, 6:8, :]
@@ -964,9 +1080,9 @@
     save(r.bias_sum, r.bias_out)
     save(r.gains_sum, r.gains_out)
     save(r.hidden_sum, r.hidden_out)
-    project_sum.finish(r.project_sum)
-    save(r.project_sum, r.project_out)
     scatters[3].finish()
+    output_sum.finish(r.output_sum)
+    save(r.output_sum, r.output_out)
     for each in gathers + lines + [total]:
         each.finish()
     for each in saves:
@@ -1064,6 +1180,7 @@
         second_all=((length, width), bf16),
         upper_low=((length, local_hidden), bf16),
         upper=((rows, local_hidden), f32),
+        columns=((length, 2 * piece), f32),
         kept=((rows, width), f32),
         held=((rows // HALVES, width), f32),
         grad_rows=((rows, width), f32),
@@ -1080,8 +1197,14 @@
     )
     for name, shape in shapes.items():
         scratch[name + "_sum"] = (shape, f32)
-        scratch[name + "_side"] = ((LINES,) + shape, bf16)
-        scratch[name + "_line"] = ((LINES - 1,) + shape, bf16)
+        moved = (local_hidden // 2, piece) if name == "down" else shape
+        scratch[name + "_side"] = ((LINES,) + moved, bf16)
+        scratch[name + "_line"] = ((LINES - 1,) + moved, bf16)
+    scratch |= dict(
+        rest_line=((LINES - 1, local_hidden // 2, 2 * piece), bf16),
+        rest_out=((local_hidden // 2, piece), bf16),
+        rest_in=((local_hidden // 2, piece), bf16),
+    )
     for name in ("near_out_", "near_in_"):
         scratch[name + "a"] = ((2 * HALVES, rows // HALVES, width), bf16)
         scratch[name + "b"] = ((2 * LINES, rows, 2 * piece), bf16)
@@ -1089,11 +1212,11 @@
         scratch[name + "a"] = ((rows, width), bf16)
         scratch[name + "b"] = ((LINES, rows, 2 * piece), bf16)
     semaphores = dict(
-        line_send=(4, 3 * LINES),
-        line_recv=(4, 2 * LINES),
-        line_local=(4,),
-        part_send=(4, 2 * LINES),
-        part_recv=(4, 2 * LINES),
+        line_send=(5, 3 * LINES),
+        line_recv=(5, 2 * LINES),
+        line_local=(5,),
+        part_send=(5, 2 * LINES),
+        part_recv=(5, 2 * LINES),
         row_send=(4, 1 + 2 * HALVES),
         row_recv=(4, 1 + 2 * HALVES),
         sum_send=(4, 3 * LINES),

time: 200 us -> 187 us (0.935)
  Pallas kernels: 199 us -> 186 us
    pallas_call x1, Pallas kernels: 196 us -> 182 us  [per_device_kernel(): pl.pallas_call(functools.partial(layer_kernel, names, rows), out_shape=[j...]
where the time goes in v5:
time: 187 us; the launch traced here: 186 us
  Pallas kernels  186 us (99%)
    pallas_call x1, Pallas kernels, per_device_kernel(): pl.pallas_call(functools.partial(layer_kernel, names, rows), out_shape=[j...  182 us

profile of v5, /device:TPU:0, one launch (start us, length us, event | category | flops | bytes accessed | tf_op | source)
XLA Modules:
  0.0 186.3 jit_solution(12842210241466220658)
XLA Ops:
  0.6 182.5 %layer.1 = (bf16[256,1024]{1,0:T(8,128)(2,1)}, f32[256,1024]{1,0:T(8,128)}, f32[3,128,256]{2,1,0:T(8,128)}, f32[256,128]{1,0:T(8,128)}, f32[128,1024]{1,0:T(8,12...) custom-call(bf16[256,1024]{1,0:T(8,128)(2,1)} %refs_0_.1, ...), custom_call_target="tpu_custom_call" | custom-call | tf_op jit(solution)/shard_map/layer/pallas_call | solution.py:1231
  183.1 3.0 %copy.20 = (bf16[256,1024]{1,0:T(8,128)(2,1)}, f32[256,1024]{1,0:T(8,128)}, f32[3,128,256]{2,1,0:T(8,128)}, f32[256,128]{1,0:T(8,128)}, f32[128,1024]{1,0:T(8,12...) custom-call(bf16[256,1024]{1,0:T(8,128)(2,1)} %get-tuple-element.27.refs_0_, ...), custom_call_target="tpu_custom_call" | custom-call | tf_op jit(solution)/shard_map/copy/pallas_call | solution.py:1243

commit v6 on v5

--- a/solution.py
+++ b/solution.py
@@ -93,28 +93,38 @@
     def start_across(self):
         self.copy(self.dp, 2, self.own).start()
 
-    def step(self, distance):
+    def step_along(self, distance):
         @pl.when(self.line >= distance)
         def _():
-            index = self.dp - 2 * distance
-            self.copy(index, 0).wait_recv()
+            self.copy(self.dp - 2 * distance, 0).wait_recv()
 
             @pl.when(self.line < LINES - 1)
             def _():
-                self.copy(index, 0).start()
-
-            self.copy(index, 2).start()
+                self.copy(self.dp - 2 * distance, 0).start()
 
         @pl.when(self.line + distance < LINES)
         def _():
-            index = self.dp + 2 * distance
-            self.copy(index, 1).wait_recv()
+            self.copy(self.dp + 2 * distance, 1).wait_recv()
 
             @pl.when(self.line > 0)
             def _():
-                self.copy(index, 1).start()
-
-            self.copy(index, 2).start()
+                self.copy(self.dp + 2 * distance, 1).start()
+
+    def step_across(self, distance):
+        @pl.when(self.line >= distance)
+        def _():
+            self.copy(self.dp - 2 * distance, 2).start()
+
+        @pl.when(self.line + distance < LINES)
+        def _():
+            self.copy(self.dp + 2 * distance, 2).start()
+
+    def step(self, distance):
+        self.step_along(distance)
+        self.step_across(distance)
+
+    def arrive_block(self, at):
+        self.copy(self.dp ^ (2 * at) ^ 1, 2).wait_recv()
 
     def arrive(self):
         self.local().wait()
@@ -161,10 +171,16 @@
         target = (self.dp, self.tensor ^ CORE)
         return remote(view, view, self.send_sem.at[slot], self.recv_sem.at[slot], target)
 
+    def start_half(self, half):
+        self.across(self.tensor, half).start()
+
+    def start_near(self):
+        self.near(self.tensor).start()
+
     def start(self):
         for half in range(HALVES):
-            self.across(self.tensor, half).start()
-        self.near(self.tensor).start()
+            self.start_half(half)
+        self.start_near()
 
     def wait_near(self):
         self.near(self.tensor ^ CORE).wait_recv()
@@ -292,13 +308,13 @@
 
     def start(self):
         self.along(3).start()
-        self.along(1).start()
 
     def relay(self):
         self.along(3).wait_recv()
         total = self.view(2)[...].astype(jnp.float32) + self.line_in[1].astype(jnp.float32)
         self.view(2)[...] = total.astype(jnp.bfloat16)
         self.along(2).start()
+        self.along(1).start()
 
     def turn(self, result):
         total = self.view(0)[...].astype(jnp.float32)
@@ -450,8 +466,8 @@
             (self.dp ^ (2 if step != 2 else 4), self.tensor),
         )
 
-    def start(self):
-        for step in ORDER:
+    def start(self, order=ORDER):
+        for step in order:
             self.across(step).start()
 
     def total(self, step):
@@ -559,7 +575,7 @@
                 (LineGather, own_b, r.triple, view_b),
                 (DirectGather, r.output_own, r.output, of_columns),
                 (LineGather, r.up_own, r.up, of_rows),
-                (DirectGather, r.down_own, r.down, of_columns),
+                (LineGather, r.down_own, r.down, of_columns),
             )
         )
     ]
@@ -662,6 +678,7 @@
     output_line.start_across()
     up_line.start_along()
     up_line.start_across()
+    down_line.start_along()
     for half in range(HALVES):
         gathers[0].wait_far(half)
     for line in triple_lines:
@@ -739,7 +756,7 @@
         @after(4)
         def _():
             up_line.step(2)
-            down_line.start_along()
+            down_line.step_along(1)
 
         @after(5)
         def _():
@@ -749,6 +766,7 @@
         def _():
             up_line.step(3)
             down_line.start_across()
+            down_line.step_across(1)
 
     r.partial[...] = dot(r.mixed[block(tensor), :], r.output[...])
     for half in range(HALVES):
@@ -765,9 +783,10 @@
             r.first_all[into, :] = first.astype(bf16)
 
         chunks(half_rows, half * half_rows, first_norm, NORM)
+        gathers[1].start_half(half)
     scatters[0].finish()
 
-    gathers[1].start()
+    gathers[1].start_near()
     r.sums[...] = jnp.zeros_like(r.sums)
 
     def extent(rank, half):
@@ -800,14 +819,15 @@
         chunks(size, start, body)
         r.partial[:size, :] = dot_nt(r.upper_low[here, :], r.up[...])
 
+    down_line.step(2)
     up_line.arrive()
 
     @pl.loop(0, 2)
     def _(turn):
         @pl.when(turn == 1)
         def _():
-            down_line.step(1)
             gathers[1].wait_near()
+            down_line.step(3)
 
         up_part(tensor ^ turn)
 
@@ -829,17 +849,13 @@
 
         up_part(tensor ^ (ACROSS + side), half)
 
-        @pl.when(side == 1)
-        def _():
-            down_line.step(2 + half)
-
     other_chip(gathers[1], up_other)
 
     down_line.local().wait()
 
     @pl.loop(0, LINES)
     def _(at):
-        down_line.arrive(at)
+        down_line.arrive_block(at)
         r.columns[...] = dot(r.hidden[...], r.down[:, column_block(at)])
         scatter_columns(scatters[1], at)
 
@@ -865,7 +881,9 @@
         lanes = column_block(at)
         r.kept[:, lanes] = scatters[1].take(at, r.kept[:, lanes])
 
-    chunks(rows, 0, second_norm, NORM)
+    for half in range(HALVES):
+        chunks(half_rows, half * half_rows, second_norm, NORM)
+        gathers[2].start_half(half)
     saves = []
 
     def save(source, target):
@@ -875,7 +893,7 @@
     save(r.layer_low, r.layer_out)
     scatters[1].finish()
 
-    gathers[2].start()
+    gathers[2].start_near()
 
     @pl.loop(0, 2)
     def _(turn):
@@ -950,12 +968,13 @@
         part = part_of(half)
         r.kept[part, :] = scatters[2].take(half, r.kept[part, :])
         chunks(half_rows, half * half_rows, first_back, NORM)
+        gathers[3].start_half(half)
         if half == 0:
             rest_sum.relay()
             down_sum.relay(3)
     scatters[2].finish()
 
-    gathers[3].start()
+    gathers[3].start_near()
     grad_keys, grad_values = r.slope.at[:, :local], r.slope.at[:, local : 2 * local]
     r.slope[:, : 2 * local] = jnp.zeros((r.slope.shape[0], 2 * local), f32)
 
@@ -1004,21 +1023,26 @@
         def _():
             for half in range(HALVES):
                 gathers[3].wait_far(half)
+            r.grad_output[...] = dot_tn(r.mixed[...], r.branch_all[...]).astype(bf16)
+            output_sum.start()
 
         attend_back(tensor ^ turn)
 
+        @pl.when(turn == 0)
+        def _():
+            down_sum.relay(1)
+
         @pl.when(turn == 1)
         def _():
-            down_sum.relay(1)
             up_sum.relay(3)
+
+        @pl.when(turn == 2)
+        def _():
             down_sum.relay(2)
-
-        @pl.when(turn == 2)
-        def _():
             rest_sum.turn(down_rest)
 
+    up_sum.relay(2)
     up_sum.relay(1)
-    r.grad_output[...] = dot_tn(r.mixed[...], r.branch_all[...]).astype(bf16)
     r.projected_low[:, local : 2 * local] = grad_keys[...].astype(bf16)
     r.projected_low[:, 2 * local :] = grad_values[...].astype(bf16)
     r.held_totals[0] = jnp.zeros(r.held_totals.shape[1:], f32)
@@ -1031,9 +1055,7 @@
     for at in range(3):
         lanes = slice(at * local, (at + 1) * local)
         weight_grad(r.gathered, r.projected_low.at[:, lanes], r.grad_project.at[at])
-    project_sum.start()
-    output_sum.start()
-    up_sum.relay(2)
+    project_sum.start((3, 1, 2, 0))
 
     @pl.loop(0, LINES)
     def _(at):
@@ -1046,6 +1068,7 @@
         scatter_columns(scatters[3], at)
 
     total.step(0)
+    output_sum.relay(3)
     project_sum.relay(3)
     down_sum.finish(down_top)
     rest_sum.finish(down_rest)
@@ -1057,17 +1080,16 @@
 
     take_tokens(0)
     take_tokens(1)
+    output_sum.relay(2)
     take_tokens(2)
-    project_sum.relay(2)
+    project_sum.relay(1)
+    total.step(1)
     take_tokens(3)
     save(r.grad_rows, r.grad_tokens)
-    project_sum.relay(1)
-    total.step(1)
+    project_sum.relay(2)
     up_sum.finish(r.up_sum)
     save(r.up_sum, r.up_out)
-    output_sum.relay(3)
     total.step(2)
-    output_sum.relay(2)
     output_sum.relay(1)
     total.step(3)
     project_sum.finish(r.project_sum)

time: 187 us -> 178 us (0.952)
  Pallas kernels: 186 us -> 178 us
    pallas_call x1, Pallas kernels: 182 us -> 174 us  [per_device_kernel(): pl.pallas_call(functools.partial(layer_kernel, names, rows), out_shape=[j...]
where the time goes in v6:
time: 178 us
  Pallas kernels  178 us (100%)
    pallas_call x1, Pallas kernels, per_device_kernel(): pl.pallas_call(functools.partial(layer_kernel, names, rows), out_shape=[j...  174 us

profile of v6, /device:TPU:0, one launch (start us, length us, event | category | flops | bytes accessed | tf_op | source)
XLA Modules:
  0.0 178.3 jit_solution(12296976743391519550)
XLA Ops:
  0.6 174.5 %layer.1 = (bf16[256,1024]{1,0:T(8,128)(2,1)}, f32[256,1024]{1,0:T(8,128)}, f32[3,128,256]{2,1,0:T(8,128)}, f32[256,128]{1,0:T(8,128)}, f32[128,1024]{1,0:T(8,12...) custom-call(bf16[256,1024]{1,0:T(8,128)(2,1)} %refs_0_.1, ...), custom_call_target="tpu_custom_call" | custom-call | tf_op jit(solution)/shard_map/layer/pallas_call | solution.py:1253
  175.1 3.0 %copy.20 = (bf16[256,1024]{1,0:T(8,128)(2,1)}, f32[256,1024]{1,0:T(8,128)}, f32[3,128,256]{2,1,0:T(8,128)}, f32[256,128]{1,0:T(8,128)}, f32[128,1024]{1,0:T(8,12...) custom-call(bf16[256,1024]{1,0:T(8,128)(2,1)} %get-tuple-element.27.refs_0_, ...), custom_call_target="tpu_custom_call" | custom-call | tf_op jit(solution)/shard_map/copy/pallas_call | solution.py:1265

commit v7 on v6

--- a/solution.py
+++ b/solution.py
@@ -71,7 +71,7 @@
         return remote(
             view if src is None else src,
             view,
-            self.send_sem.at[way * LINES + index // 2],
+            self.send_sem.at[(LINES - 1) * way - way % 2 + index // 2],
             self.recv_sem.at[index],
             self.targets[way],
         )
@@ -278,6 +278,81 @@
     return inverse * (grad - average - normed * along)
 
 
+class PairGather:
+    def __init__(self, own, full, piece, pair, send_sem, recv_sem, local_sem):
+        self.own, self.full, self.piece, self.pair = own, full, piece, pair
+        self.send_sem, self.recv_sem, self.local_sem = send_sem, recv_sem, local_sem
+        self.dp, self.tensor = position()
+        self.line = self.dp // 2
+
+    def local(self):
+        return pltpu.make_async_copy(self.own, self.piece(self.full, self.dp), self.local_sem)
+
+    def across(self):
+        return remote(
+            self.own,
+            self.piece(self.full, self.dp),
+            self.send_sem.at[0],
+            self.recv_sem.at[LINES],
+            (self.dp ^ 1, self.tensor),
+        )
+
+    def along(self, line, way):
+        view = self.pair(self.full, line)
+        return remote(
+            view,
+            view,
+            self.send_sem.at[1 + way * 2 + line],
+            self.recv_sem.at[line],
+            (self.dp + 2 - 4 * way, self.tensor),
+        )
+
+    def start(self):
+        self.local().start()
+        self.across().start()
+
+    def begin(self):
+        self.local().wait()
+        self.across().wait_recv()
+
+        @pl.when(self.line < LINES - 1)
+        def _():
+            self.along(self.line, 0).start()
+
+        @pl.when(self.line > 0)
+        def _():
+            self.along(self.line, 1).start()
+
+    def step(self, distance):
+        @pl.when(self.line >= distance)
+        def _():
+            self.along(self.line - distance, 0).wait_recv()
+
+            @pl.when(self.line < LINES - 1)
+            def _():
+                self.along(self.line - distance, 0).start()
+
+        @pl.when(self.line + distance < LINES)
+        def _():
+            self.along(self.line + distance, 1).wait_recv()
+
+            @pl.when(self.line > 0)
+            def _():
+                self.along(self.line + distance, 1).start()
+
+    def finish(self):
+        self.across().wait_send()
+        for line in range(LINES):
+
+            @pl.when((self.line < LINES - 1) & (line <= self.line))
+            def _():
+                self.along(line, 0).wait_send()
+
+            @pl.when((self.line > 0) & (line >= self.line))
+            def _():
+                self.along(line, 1).wait_send()
+
+
 class LineFirstScatter:
     def __init__(self, partial, piece, line_in, across_out, across_in, send_sem, recv_sem):
         self.partial, self.piece, self.line_in = partial, piece, line_in
@@ -321,8 +396,7 @@
         for step, slot in ((1, 0), (2, 2)):
             self.along(step).wait_recv()
             total = total + self.line_in[slot].astype(jnp.float32)
-        width = result.shape[1]
-        first, second = total[:, :width], total[:, width:]
+        first, second = jnp.split(total, 2, 0 if result.shape[1] == total.shape[1] else 1)
         even = self.dp % 2 == 0
         result[...] = jnp.where(even, first, second)
         self.across_out[...] = jnp.where(even, second, first).astype(jnp.bfloat16)
@@ -537,7 +611,7 @@
     local = r.queries.shape[1]
     piece = r.triple_own.shape[1]
     pairs = local // (2 * HEAD)
-    hidden = r.hidden.shape[1]
+    length, hidden = r.hidden.shape
     near, across, far = tensor ^ CORE, tensor ^ ACROSS, tensor ^ FAR
 
     def of_rows(ref, index):
@@ -575,11 +649,24 @@
                 (LineGather, own_b, r.triple, view_b),
                 (DirectGather, r.output_own, r.output, of_columns),
                 (LineGather, r.up_own, r.up, of_rows),
-                (LineGather, r.down_own, r.down, of_columns),
+                (LineGather, r.down_own.at[: hidden // 2, :], r.down.at[: hidden // 2, :], of_columns),
             )
         )
     ]
     *triple_lines, output_line, up_line, down_line = lines
+
+    def of_both(ref, index):
+        return column_piece(ref, index, 2 * piece)
+
+    rest_line = PairGather(
+        r.down_own.at[hidden // 2 :, :],
+        r.down.at[hidden // 2 :, :],
+        of_columns,
+        of_both,
+        r.pair_send,
+        r.pair_recv,
+        r.pair_local,
+    )
     sums = [
         LineScatter(partial, view, side, along, r.part_send.at[at], r.part_recv.at[at])
         for at, (partial, view, side, along) in enumerate(
@@ -593,33 +680,26 @@
     ]
     project_sum, output_sum, up_sum, down_sum = sums
 
-    def of_both(ref, index):
-        return column_piece(ref, index, 2 * piece)
-
     rest_sum = LineFirstScatter(
         r.grad_down.at[hidden // 2 :, :],
         of_both,
         r.rest_line,
         r.rest_out,
         r.rest_in,
-        r.part_send.at[4],
-        r.part_recv.at[4],
+        r.rest_send.at[0],
+        r.rest_recv.at[0],
     )
     down_top, down_rest = r.down_sum.at[: hidden // 2, :], r.down_sum.at[hidden // 2 :, :]
     gathers = [
-        RowGather(full, rows, r.row_send.at[at], r.row_recv.at[at])
-        for at, full in enumerate((r.gathered, r.first_all, r.second_all, r.branch_all))
+        RowGather(full, rows, r.row_send, r.row_recv)
+        for full in (r.gathered, r.first_all, r.second_all, r.branch_all)
     ]
+    row_buffers = r.near_out_a, r.near_in_a, r.across_out_a, r.across_in_a
+    column_buffers = r.near_out_b, r.near_in_b, r.across_out_b, r.across_in_b
     scatters = [
-        kind(*buffers, r.sum_send.at[at], r.sum_recv.at[at])
-        for at, (kind, buffers) in enumerate(
-            (
-                (RowScatter, (r.near_out_a, r.near_in_a, r.across_out_a, r.across_in_a)),
-                (ColumnScatter, (r.near_out_b, r.near_in_b, r.across_out_b, r.across_in_b)),
-            )
-            * 2
-        )
-    ]
+        RowScatter(*row_buffers, r.row_sum_send, r.row_sum_recv),
+        ColumnScatter(*column_buffers, r.column_sum_send, r.column_sum_recv),
+    ] * 2
     total = Total(r.held_totals, r.arrived_totals, r.total_send, r.total_recv)
 
     def column_block(at):
@@ -676,8 +756,8 @@
         line.step(3)
     output_line.start_along()
     output_line.start_across()
+    rest_line.start()
     up_line.start_along()
-    up_line.start_across()
     down_line.start_along()
     for half in range(HALVES):
         gathers[0].wait_far(half)
@@ -704,6 +784,7 @@
 
     for step in range(1, LINES):
         output_line.step(step)
+    up_line.start_across()
 
     def head_rows(head):
         return pl.ds(pl.multiple_of(head * HEAD, HEAD), HEAD)
@@ -745,6 +826,10 @@
         def _():
             up_line.step(1)
 
+        @after(1)
+        def _():
+            rest_line.begin()
+
         @after(3)
         def _():
             output_line.local().wait()
@@ -764,11 +849,13 @@
 
         @after(7)
         def _():
+            rest_line.step(1)
             up_line.step(3)
             down_line.start_across()
             down_line.step_across(1)
 
     r.partial[...] = dot(r.mixed[block(tensor), :], r.output[...])
+    gathers[0].finish()
     for half in range(HALVES):
         part = part_of(half)
         r.kept[part, :] = scatters[0].take(half, r.partial[part, :])
@@ -828,6 +915,7 @@
         def _():
             gathers[1].wait_near()
             down_line.step(3)
+            rest_line.step(2)
 
         up_part(tensor ^ turn)
 
@@ -851,6 +939,7 @@
 
     other_chip(gathers[1], up_other)
 
+    rest_line.step(3)
     down_line.local().wait()
 
     @pl.loop(0, LINES)
@@ -881,6 +970,7 @@
         lanes = column_block(at)
         r.kept[:, lanes] = scatters[1].take(at, r.kept[:, lanes])
 
+    gathers[1].finish()
     for half in range(HALVES):
         chunks(half_rows, half * half_rows, second_norm, NORM)
         gathers[2].start_half(half)
@@ -964,6 +1054,7 @@
         add_to(0, low.astype(f32))
         r.branch_all[pl.ds(pl.multiple_of(tensor * rows + here.start, NORM), NORM), :] = low
 
+    gathers[2].finish()
     for half in range(HALVES):
         part = part_of(half)
         r.kept[part, :] = scatters[2].take(half, r.kept[part, :])
@@ -1048,14 +1139,19 @@
     r.held_totals[0] = jnp.zeros(r.held_totals.shape[1:], f32)
     r.held_totals[0, 2:8, :] = r.sums[0:6, :]
     r.held_totals[0, pl.ds(8 + tensor, 1), :] = r.sums[6:7, :]
+    shifts = dot(jnp.ones((CHUNK, length), bf16), r.projected_low[...])
     for row, at in ((0, 0), (1, 2)):
-        low = r.projected_low[:, at * local : (at + 1) * local].astype(f32)
-        r.held_totals[0, row : row + 1, columns] = jnp.sum(low, axis=0, keepdims=True)
+        r.held_totals[0, row : row + 1, columns] = shifts[:1, at * local : (at + 1) * local]
     total.start()
-    for at in range(3):
-        lanes = slice(at * local, (at + 1) * local)
-        weight_grad(r.gathered, r.projected_low.at[:, lanes], r.grad_project.at[at])
-    project_sum.start((3, 1, 2, 0))
+
+    @pl.loop(0, r.gathered.shape[1] // rows)
+    def _(index):
+        lanes = block(index)
+        product = dot_tn(r.gathered[:, lanes], r.projected_low[...]).astype(bf16)
+        for at in range(3):
+            r.grad_project[at, lanes, :] = product[:, at * local : (at + 1) * local]
+
+    project_sum.start()
 
     @pl.loop(0, LINES)
     def _(at):
@@ -1082,11 +1178,15 @@
     take_tokens(1)
     output_sum.relay(2)
     take_tokens(2)
-    project_sum.relay(1)
     total.step(1)
     take_tokens(3)
     save(r.grad_rows, r.grad_tokens)
+    gathers[3].finish()
+    for each in lines + [rest_line]:
+        each.finish()
     project_sum.relay(2)
+    project_sum.relay(1)
+    scatters[3].finish()
     up_sum.finish(r.up_sum)
     save(r.up_sum, r.up_out)
     total.step(2)
@@ -1102,11 +1202,9 @@
     save(r.bias_sum, r.bias_out)
     save(r.gains_sum, r.gains_out)
     save(r.hidden_sum, r.hidden_out)
-    scatters[3].finish()
     output_sum.finish(r.output_sum)
     save(r.output_sum, r.output_out)
-    for each in gathers + lines + [total]:
-        each.finish()
+    total.finish()
     for each in saves:
         each.wait()
 
@@ -1234,15 +1332,22 @@
         scratch[name + "a"] = ((rows, width), bf16)
         scratch[name + "b"] = ((LINES, rows, 2 * piece), bf16)
     semaphores = dict(
-        line_send=(5, 3 * LINES),
+        line_send=(5, 3 * LINES - 2),
         line_recv=(5, 2 * LINES),
         line_local=(5,),
-        part_send=(5, 2 * LINES),
-        part_recv=(5, 2 * LINES),
-        row_send=(4, 1 + 2 * HALVES),
-        row_recv=(4, 1 + 2 * HALVES),
-        sum_send=(4, 3 * LINES),
-        sum_recv=(4, 3 * LINES),
+        part_send=(4, 2 * LINES),
+        part_recv=(4, 2 * LINES),
+        pair_send=(2 * LINES - 1,),
+        pair_recv=(LINES + 1,),
+        pair_local=(),
+        rest_send=(1, LINES),
+        rest_recv=(1, LINES),
+        row_send=(1 + 2 * HALVES,),
+        row_recv=(1 + 2 * HALVES,),
+        row_sum_send=(3 * HALVES,),
+        row_sum_recv=(3 * HALVES,),
+        column_sum_send=(3 * LINES,),
+        column_sum_recv=(3 * LINES,),
         total_send=(5,),
         total_recv=(5,),
         load_sem=(6,),

time: 178 us -> 174 us (0.978)
  Pallas kernels: 178 us -> 173 us
    pallas_call x1, Pallas kernels: 174 us -> 170 us  [per_device_kernel(): pl.pallas_call(functools.partial(layer_kernel, names, rows), out_shape=[j...]
where the time goes in v7:
time: 174 us
  Pallas kernels  173 us (99%)
    pallas_call x1, Pallas kernels, per_device_kernel(): pl.pallas_call(functools.partial(layer_kernel, names, rows), out_shape=[j...  170 us

profile of v7, /device:TPU:0, one launch (start us, length us, event | category | flops | bytes accessed | tf_op | source)
XLA Modules:
  0.0 173.8 jit_solution(16111942829371512514)
XLA Ops:
  0.6 169.9 %layer.1 = (bf16[256,1024]{1,0:T(8,128)(2,1)}, f32[256,1024]{1,0:T(8,128)}, f32[3,128,256]{2,1,0:T(8,128)}, f32[256,128]{1,0:T(8,128)}, f32[128,1024]{1,0:T(8,12...) custom-call(bf16[256,1024]{1,0:T(8,128)(2,1)} %refs_0_.1, ...), custom_call_target="tpu_custom_call" | custom-call | tf_op jit(solution)/shard_map/layer/pallas_call | solution.py:1358
  170.6 3.0 %copy.20 = (bf16[256,1024]{1,0:T(8,128)(2,1)}, f32[256,1024]{1,0:T(8,128)}, f32[3,128,256]{2,1,0:T(8,128)}, f32[256,128]{1,0:T(8,128)}, f32[128,1024]{1,0:T(8,12...) custom-call(bf16[256,1024]{1,0:T(8,128)(2,1)} %get-tuple-element.27.refs_0_, ...), custom_call_target="tpu_custom_call" | custom-call | tf_op jit(solution)/shard_map/copy/pallas_call | solution.py:1370

commit v8 on v7

--- a/solution.py
+++ b/solution.py
@@ -702,14 +702,20 @@
     ] * 2
     total = Total(r.held_totals, r.arrived_totals, r.total_send, r.total_recv)
 
-    def column_block(at):
-        return block((dp // 2) ^ at, 2 * piece)
-
-    def scatter_columns(scatter, at):
-        scatter.give_far(at, r.columns[block(far), :])
-        scatter.give_near(at, r.columns[block(near), :])
-        scatter.give_across(at, r.columns[block(across), :])
-        r.kept[:, column_block(at)] = r.columns[block(tensor), :]
+    def column_pair(at):
+        return block((dp // 4) ^ at, 4 * piece)
+
+    def give_halves(method, at, partial):
+        for half in range(HALVES):
+            method(at * HALVES + half, partial[part_of(half)])
+
+    def keep_near(scatter, at, product):
+        give_halves(scatter.give_near, at, product(near, column_pair(at)))
+        r.kept[:, column_pair(at)] = product(tensor, column_pair(at))
+
+    def take_columns(scatter, result, at):
+        part, lanes = block(at % HALVES, half_rows), column_pair(at // HALVES)
+        result[part, lanes] = scatter.take(at, r.kept[part, lanes])
 
     def chunks(size, start, body, step=CHUNK):
         @pl.loop(0, size // step)
@@ -937,16 +943,36 @@
 
         up_part(tensor ^ (ACROSS + side), half)
 
-    other_chip(gathers[1], up_other)
-
+    def down_part(rank, lanes):
+        return dot(r.hidden[block(rank), :], r.down[:, lanes])
+
+    def send_unit(at, half):
+        def product(rank):
+            return dot(r.hidden[extent(rank, half)[2], :], r.down[:, column_pair(at)])
+
+        scatters[1].give_far(at * HALVES + half, product(far))
+        scatters[1].give_across(at * HALVES + half, product(across))
+
+    def up_and_send(half, side):
+        up_other(half, side)
+
+        @pl.when((side == 1) & (half == 0))
+        def _():
+            down_line.local().wait()
+            down_line.arrive_block(0)
+            down_line.arrive_block(1)
+            send_unit(0, 0)
+
+    other_chip(gathers[1], up_and_send)
+
+    send_unit(0, 1)
+    keep_near(scatters[1], 0, down_part)
     rest_line.step(3)
-    down_line.local().wait()
-
-    @pl.loop(0, LINES)
-    def _(at):
-        down_line.arrive_block(at)
-        r.columns[...] = dot(r.hidden[...], r.down[:, column_block(at)])
-        scatter_columns(scatters[1], at)
+    down_line.arrive_block(2)
+    down_line.arrive_block(3)
+    send_unit(1, 0)
+    send_unit(1, 1)
+    keep_near(scatters[1], 1, down_part)
 
     def add_to(row, value):
         r.sums[row : row + 1, :] += jnp.sum(value, axis=0, keepdims=True)
@@ -965,13 +991,10 @@
         add_to(2, low.astype(f32))
         r.second_all[pl.ds(pl.multiple_of(tensor * rows + here.start, NORM), NORM), :] = low
 
-    @pl.loop(0, LINES)
-    def _(at):
-        lanes = column_block(at)
-        r.kept[:, lanes] = scatters[1].take(at, r.kept[:, lanes])
-
     gathers[1].finish()
     for half in range(HALVES):
+        for at in range(2):
+            take_columns(scatters[1], r.kept, at * HALVES + half)
         chunks(half_rows, half * half_rows, second_norm, NORM)
         gathers[2].start_half(half)
     saves = []
@@ -1153,15 +1176,18 @@
 
     project_sum.start()
 
-    @pl.loop(0, LINES)
-    def _(at):
-        lanes = column_block(at)
+    def token_part(rank, lanes):
         product = 0
         for part in range(3):
-            left = r.projected_low[:, part * local : (part + 1) * local]
+            left = r.projected_low[block(rank), part * local : (part + 1) * local]
             product += dot_nt(left, r.triple[part, lanes, :])
-        r.columns[...] = product
-        scatter_columns(scatters[3], at)
+        return product
+
+    @pl.loop(0, 2)
+    def _(at):
+        give_halves(scatters[3].give_far, at, token_part(far, column_pair(at)))
+        give_halves(scatters[3].give_across, at, token_part(across, column_pair(at)))
+        keep_near(scatters[3], at, token_part)
 
     total.step(0)
     output_sum.relay(3)
@@ -1171,8 +1197,8 @@
     save(r.down_sum, r.down_out)
 
     def take_tokens(at):
-        lanes = column_block(at)
-        r.grad_rows[:, lanes] += scatters[3].take(at, r.kept[:, lanes])
+        part, lanes = part_of(at % HALVES), column_pair(at // HALVES)
+        r.grad_rows[part, lanes] += scatters[3].take(at, r.kept[part, lanes])
 
     take_tokens(0)
     take_tokens(1)
@@ -1300,7 +1326,6 @@
         second_all=((length, width), bf16),
         upper_low=((length, local_hidden), bf16),
         upper=((rows, local_hidden), f32),
-        columns=((length, 2 * piece), f32),
         kept=((rows, width), f32),
         held=((rows // HALVES, width), f32),
         grad_rows=((rows, width), f32),
@@ -1327,10 +1352,10 @@
     )
     for name in ("near_out_", "near_in_"):
         scratch[name + "a"] = ((2 * HALVES, rows // HALVES, width), bf16)
-        scratch[name + "b"] = ((2 * LINES, rows, 2 * piece), bf16)
+        scratch[name + "b"] = ((2 * LINES, rows // HALVES, 4 * piece), bf16)
     for name in ("across_out_", "across_in_"):
         scratch[name + "a"] = ((rows, width), bf16)
-        scratch[name + "b"] = ((LINES, rows, 2 * piece), bf16)
+        scratch[name + "b"] = ((LINES, rows // HALVES, 4 * piece), bf16)
     semaphores = dict(
         line_send=(5, 3 * LINES - 2),
         line_recv=(5, 2 * LINES),

time: 174 us -> 171 us (0.983)
  Pallas kernels: 173 us -> 170 us
    pallas_call x1, Pallas kernels: 170 us -> 167 us  [per_device_kernel(): pl.pallas_call(functools.partial(layer_kernel, names, rows), out_shape=[j...]
where the time goes in v8:
time: 171 us
  Pallas kernels  170 us (99%)
    pallas_call x1, Pallas kernels, per_device_kernel(): pl.pallas_call(functools.partial(layer_kernel, names, rows), out_shape=[j...  167 us

profile of v8, /device:TPU:0, one launch (start us, length us, event | category | flops | bytes accessed | tf_op | source)
XLA Modules:
  0.0 171.3 jit_solution(131034040123368668)
XLA Ops:
  0.6 167.4 %layer.1 = (bf16[256,1024]{1,0:T(8,128)(2,1)}, f32[256,1024]{1,0:T(8,128)}, f32[3,128,256]{2,1,0:T(8,128)}, f32[256,128]{1,0:T(8,128)}, f32[128,1024]{1,0:T(8,12...) custom-call(bf16[256,1024]{1,0:T(8,128)(2,1)} %refs_0_.1, ...), custom_call_target="tpu_custom_call" | custom-call | tf_op jit(solution)/shard_map/layer/pallas_call | solution.py:1383
  168.1 3.0 %copy.20 = (bf16[256,1024]{1,0:T(8,128)(2,1)}, f32[256,1024]{1,0:T(8,128)}, f32[3,128,256]{2,1,0:T(8,128)}, f32[256,128]{1,0:T(8,128)}, f32[128,1024]{1,0:T(8,12...) custom-call(bf16[256,1024]{1,0:T(8,128)(2,1)} %get-tuple-element.27.refs_0_, ...), custom_call_target="tpu_custom_call" | custom-call | tf_op jit(solution)/shard_map/copy/pallas_call | solution.py:1395

commit v9 on v8

--- a/solution.py
+++ b/solution.py
@@ -60,9 +60,11 @@
         self.send_sem, self.recv_sem, self.local_sem = send_sem, recv_sem, local_sem
         self.dp, self.tensor = position()
         self.line, self.side = self.dp // 2, self.dp % 2
+        up = self.dp + jnp.where(self.line < LINES - 1, 2, -2)
+        down = self.dp + jnp.where(self.line > 0, -2, 2)
         self.targets = (
-            (self.dp + 2, self.tensor),
-            (self.dp - 2, self.tensor),
+            (up, self.tensor),
+            (down, self.tensor),
             (self.dp ^ 1, self.tensor),
         )
 
@@ -284,6 +286,8 @@
         self.send_sem, self.recv_sem, self.local_sem = send_sem, recv_sem, local_sem
         self.dp, self.tensor = position()
         self.line = self.dp // 2
+        self.up = jnp.where(self.line < LINES - 1, 2, -2)
+        self.down = jnp.where(self.line > 0, -2, 2)
 
     def local(self):
         return pltpu.make_async_copy(self.own, self.piece(self.full, self.dp), self.local_sem)
@@ -304,7 +308,7 @@
             view,
             self.send_sem.at[1 + way * 2 + line],
             self.recv_sem.at[line],
-            (self.dp + 2 - 4 * way, self.tensor),
+            (self.dp + (self.up if way == 0 else self.down), self.tensor),
         )
 
     def start(self):
@@ -930,9 +934,9 @@
         def _(turn):
             half, side = turn // 2, turn % 2
 
-            @pl.when(side == 0)
+            @pl.when(turn == 0)
             def _():
-                gather.wait_across(half)
+                gather.wait_across(0)
 
             body(half, side)
 
@@ -958,6 +962,7 @@
 
         @pl.when((side == 1) & (half == 0))
         def _():
+            gathers[1].wait_across(1)
             down_line.local().wait()
             down_line.arrive_block(0)
             down_line.arrive_block(1)
@@ -1059,6 +1064,11 @@
         @pl.when(side == 1)
         def _():
             scatters[2].give_far(half, r.partial[:half_rows, :])
+
+            @pl.when(half == 0)
+            def _():
+                gathers[2].wait_across(1)
+
             scatters[2].give_across(half, r.held[...])
 
     other_chip(gathers[2], back_other)

time: 171 us -> 170 us (level)
  no operation moved by 1% of the time
where the time goes in v9:
time: 170 us
  Pallas kernels  169 us (99%)
    pallas_call x1, Pallas kernels, per_device_kernel(): pl.pallas_call(functools.partial(layer_kernel, names, rows), out_shape=[j...  166 us

profile of v9, /device:TPU:0, one launch (start us, length us, event | category | flops | bytes accessed | tf_op | source)
XLA Modules:
  0.0 170.0 jit_solution(1042706007356682213)
XLA Ops:
  0.6 166.2 %layer.1 = (bf16[256,1024]{1,0:T(8,128)(2,1)}, f32[256,1024]{1,0:T(8,128)}, f32[3,128,256]{2,1,0:T(8,128)}, f32[256,128]{1,0:T(8,128)}, f32[128,1024]{1,0:T(8,12...) custom-call(bf16[256,1024]{1,0:T(8,128)(2,1)} %refs_0_.1, ...), custom_call_target="tpu_custom_call" | custom-call | tf_op jit(solution)/shard_map/layer/pallas_call | solution.py:1393
  166.8 3.0 %copy.20 = (bf16[256,1024]{1,0:T(8,128)(2,1)}, f32[256,1024]{1,0:T(8,128)}, f32[3,128,256]{2,1,0:T(8,128)}, f32[256,128]{1,0:T(8,128)}, f32[128,1024]{1,0:T(8,12...) custom-call(bf16[256,1024]{1,0:T(8,128)(2,1)} %get-tuple-element.27.refs_0_, ...), custom_call_target="tpu_custom_call" | custom-call | tf_op jit(solution)/shard_map/copy/pallas_call | solution.py:1405

commit v10 on v9

--- a/solution.py
+++ b/solution.py
@@ -586,8 +586,8 @@
 
     def copy(self, step):
         return remote(
-            self.held.at[step],
-            self.arrived.at[step],
+            self.part(self.held, step),
+            self.part(self.arrived, step),
             self.send_sem.at[step],
             self.recv_sem.at[step],
             self.targets[step],
@@ -596,9 +596,16 @@
     def start(self):
         self.copy(0).start()
 
-    def step(self, step):
+    def part(self, ref, step):
+        return ref.at[step, :8] if step < 3 else ref.at[step]
+
+    def step(self, step, spread=None):
         self.copy(step).wait_recv()
-        self.held[step + 1] = self.held[step] + self.arrived[step]
+        total = self.part(self.held, step)[...] + self.part(self.arrived, step)[...]
+        if spread is None:
+            self.held[step + 1, : total.shape[0]] = total
+        else:
+            spread(total)
         if step + 1 < len(self.targets):
             self.copy(step + 1).start()
 
@@ -1169,12 +1176,20 @@
     up_sum.relay(1)
     r.projected_low[:, local : 2 * local] = grad_keys[...].astype(bf16)
     r.projected_low[:, 2 * local :] = grad_values[...].astype(bf16)
-    r.held_totals[0] = jnp.zeros(r.held_totals.shape[1:], f32)
+    r.held_totals[0, :8] = jnp.zeros((8,) + r.held_totals.shape[2:], f32)
+    r.held_totals[0, 1:2, :] = r.sums[6:7, :]
     r.held_totals[0, 2:8, :] = r.sums[0:6, :]
-    r.held_totals[0, pl.ds(8 + tensor, 1), :] = r.sums[6:7, :]
     shifts = dot(jnp.ones((CHUNK, length), bf16), r.projected_low[...])
     for row, at in ((0, 0), (1, 2)):
-        r.held_totals[0, row : row + 1, columns] = shifts[:1, at * local : (at + 1) * local]
+        r.held_totals[0, 0:1, row * local : (row + 1) * local] = shifts[:1, at * local : (at + 1) * local]
+
+    def spread(sums):
+        r.held_totals[3] = jnp.zeros(r.held_totals.shape[1:], f32)
+        r.held_totals[3, 2:8, :] = sums[2:8]
+        r.held_totals[3, pl.ds(8 + tensor, 1), :] = sums[1:2]
+        for row in range(2):
+            r.held_totals[3, row : row + 1, columns] = sums[:1, row * local : (row + 1) * local]
+
     total.start()
 
     @pl.loop(0, r.gathered.shape[1] // rows)
@@ -1225,7 +1240,7 @@
     scatters[3].finish()
     up_sum.finish(r.up_sum)
     save(r.up_sum, r.up_out)
-    total.step(2)
+    total.step(2, spread)
     output_sum.relay(1)
     total.step(3)
     project_sum.finish(r.project_sum)

time: 170 us -> 169 us (level)
  no operation moved by 1% of the time
where the time goes in v10:
time: 169 us
  Pallas kernels  168 us (99%)
    pallas_call x1, Pallas kernels, per_device_kernel(): pl.pallas_call(functools.partial(layer_kernel, names, rows), out_shape=[j...  165 us

profile of v10, /device:TPU:0, one launch (start us, length us, event | category | flops | bytes accessed | tf_op | source)
XLA Modules:
  0.0 169.0 jit_solution(10792794361165845508)
XLA Ops:
  0.6 165.1 %layer.1 = (bf16[256,1024]{1,0:T(8,128)(2,1)}, f32[256,1024]{1,0:T(8,128)}, f32[3,128,256]{2,1,0:T(8,128)}, f32[256,128]{1,0:T(8,128)}, f32[128,1024]{1,0:T(8,12...) custom-call(bf16[256,1024]{1,0:T(8,128)(2,1)} %refs_0_.1, ...), custom_call_target="tpu_custom_call" | custom-call | tf_op jit(solution)/shard_map/layer/pallas_call | solution.py:1408
  165.8 3.0 %copy.20 = (bf16[256,1024]{1,0:T(8,128)(2,1)}, f32[256,1024]{1,0:T(8,128)}, f32[3,128,256]{2,1,0:T(8,128)}, f32[256,128]{1,0:T(8,128)}, f32[128,1024]{1,0:T(8,12...) custom-call(bf16[256,1024]{1,0:T(8,128)(2,1)} %get-tuple-element.27.refs_0_, ...), custom_call_target="tpu_custom_call" | custom-call | tf_op jit(solution)/shard_map/copy/pallas_call | solution.py:1420
